TPU v7x, 128 devices: a whole 4x4x4 slice. The times are simulated.
128 devices in a mesh: bx: 16 (over x, y), by: 8 (over z, core).
Axes of the slice: x: 4, y: 4, z: 4, core: 2. Of those that a mesh axis runs over, the one named last changes fastest.
Arguments:
- tendency: bfloat16 [1536, 40, 64, 128], P(('bx', 'by')), may hold values from -6 to 6
- thickness: float32 [40], replicated, may hold values from 0.04 to 0.25
- depth: float32 [2048, 8192], P('by', 'bx'), may hold values from 0.25 to 1
- block_owner: int32 [1536], replicated, may hold values from 0 to 2047, as said below
- block_mask: int32 [32, 64], P('by', 'bx'), may hold values from 0 to 1, as said below
- ocean_counts: int32 [32, 64], P('by', 'bx'), may hold values from 0 to 8192, as said below
Outputs:
- heights: float32 [1536, 64, 128], P(('bx', 'by'))
Inputs may be any that keep to these rules, and one draw needn't show every extreme that they name: `block_owner`: distinct grid blocks. Device t (index over bx+by with bx slowest; index i along bx, j along by) owns the region of block rows j * 4 to j * 4 + 3 and block columns i * 4 to i * 4 + 3; its slots t * 12 to t * 12 + 11 name blocks of its own region except 1 to 2 of its last 2 slots, which name blocks of the region of device (t + k) modulo 128 for one k of 1 to 2. Some device has 2 such slots with k = 2. `block_mask`: 1 exactly on the blocks that block_owner names. `ocean_counts`: 0 on land blocks; on ocean blocks from 2048 to 8192, and every region has a block with 8192.
All inputs are finite; a program needn't handle non-finite values.
Results may differ from a plain program's by a relative error of at most 0.0003.
Values sent between devices are 32-bit elements; how exact they have to be, the bound alone decides.
No kernel may reach another device: no remote copies, remote signals or barrier semaphores. Data moves between devices by JAX's collectives and lax.ppermute only.
A program may use at most 64 MiB of HBM per device.

v0:
```python
import jax
import jax.numpy as jnp
from jax import lax
from jax.sharding import PartitionSpec as P

MOVE = 2
REACH = 2
ITERS = 10


surface_term = 0.1
lower_bound = 0.05
upper_bound = 2.0


def shifted(value, axis, steps):
    count = lax.axis_size(axis)
    pairs = [(source, (source + steps) % count) for source in range(count)]
    return lax.ppermute(value, axis, pairs)


def with_halo(cells, sides, width):
    for axis, dim in sides:
        count = lax.axis_size(axis)
        head = lax.slice_in_dim(cells, 0, width, axis=dim)
        tail = lax.slice_in_dim(cells, cells.shape[dim] - width, cells.shape[dim], axis=dim)
        cells = jnp.concatenate(
            [
                lax.ppermute(tail, axis, [(i, (i + 1) % count) for i in range(count)]),
                cells,
                lax.ppermute(head, axis, [((i + 1) % count, i) for i in range(count)]),
            ],
            axis=dim,
        )
    return cells


def chebyshev_plan():
    centre_value = (upper_bound + lower_bound) / 2.0
    half_width = (upper_bound - lower_bound) / 2.0
    ratio_value = centre_value / half_width
    weight = 1.0 / ratio_value
    scales = []
    for sweep in range(ITERS):
        renewed = 1.0 / (2.0 * ratio_value - weight)
        scales.append((renewed * weight, 2.0 * renewed / half_width))
        weight = renewed
    return (1.0 / centre_value, scales)


def corners(padded):
    return jnp.minimum(
        jnp.minimum(padded[:-1, :-1], padded[:-1, 1:]), jnp.minimum(padded[1:, :-1], padded[1:, 1:])
    )


def beside_all(values):
    return values[:-1, :-1] + values[:-1, 1:] + values[1:, :-1] + values[1:, 1:]


def operate(padded, corner_depth):
    corner_mean = 0.25 * beside_all(padded)
    centre = padded[1:-1, 1:-1]
    return (
        surface_term * centre
        + beside_all(corner_depth) * centre
        - beside_all(corner_depth * corner_mean)
    )


def clear_poles(padded, margin_cells, row_index, rows_axis):
    row_ids = jnp.arange(padded.shape[0], dtype=jnp.int32)[:, None]
    cut_rows = (row_ids < margin_cells) & (row_index == 0) | (
        row_ids >= padded.shape[0] - margin_cells
    ) & (row_index == rows_axis - 1)
    return jnp.where(cut_rows, 0.0, padded)


def locate(block_ids, region_rows, region_cols, rows_axis, grid_cols):
    grid_row = block_ids // grid_cols
    grid_col = block_ids % grid_cols
    holder = grid_col // region_cols * rows_axis + grid_row // region_rows
    local_block = grid_row % region_rows * region_cols + grid_col % region_cols
    return (holder, local_block)


def selector(holder, local_block, myself, region_blocks):
    targets = jnp.arange(region_blocks, dtype=jnp.int32)
    chosen = holder == myself
    return ((local_block[:, None] == targets[None, :]) & chosen[:, None]).astype(jnp.float32)


def on_device(tendency, thickness, depth, block_owner, block_mask, ocean_counts):
    held_slots = tendency.shape[0]
    block_height = tendency.shape[2]
    block_width = tendency.shape[3]
    region_rows, region_cols = block_mask.shape
    region_blocks = region_rows * region_cols
    rows_axis = lax.axis_size("by")
    devices = lax.axis_size("bx") * rows_axis
    grid_cols = region_cols * lax.axis_size("bx")
    row_index = lax.axis_index("by")
    myself = lax.axis_index("bx") * rows_axis + row_index

    def to_field(blocks):
        shaped = blocks.reshape(region_rows, region_cols, block_height, block_width).transpose(
            0, 2, 1, 3
        )
        return shaped.reshape(region_rows * block_height, region_cols * block_width)

    forcing = jnp.sum(tendency.astype(jnp.float32) * thickness[None, :, None, None], axis=1)
    own_ids = lax.dynamic_slice_in_dim(block_owner, myself * held_slots, held_slots)
    trailing_forcing = forcing[held_slots - MOVE :]
    tail_table = block_owner.reshape(devices, held_slots)[:, held_slots - MOVE :]
    pieces = []
    id_pieces = []
    for offset in range(1, REACH + 1):
        pieces.append(shifted(trailing_forcing, ("bx", "by"), offset))
        sender = (myself - offset) % devices
        id_pieces.append(lax.dynamic_index_in_dim(tail_table, sender, 0, keepdims=False))
    arrived = jnp.concatenate(pieces, axis=0)
    arrived_ids = jnp.concatenate(id_pieces, axis=0)
    all_ids = jnp.concatenate([own_ids, arrived_ids])
    holder, local_block = locate(all_ids, region_rows, region_cols, rows_axis, grid_cols)
    matches = selector(holder, local_block, myself, region_blocks)
    placed = jnp.einsum(
        "nl,nyx->lyx",
        matches,
        jnp.concatenate([forcing, arrived], axis=0),
        precision=lax.Precision.HIGHEST,
    )
    forcing_field = to_field(placed)
    position = (
        jnp.arange(block_height, dtype=jnp.int32)[:, None] * block_width
        + jnp.arange(block_width, dtype=jnp.int32)[None, :]
    )
    wetness = (position[None, None] < ocean_counts[:, :, None, None]) & (
        block_mask[:, :, None, None] == 1
    )
    oceanic = to_field(wetness.astype(jnp.float32))
    masked_depth = depth * oceanic
    source = forcing_field * oceanic
    padded_depth = with_halo(masked_depth, (("bx", 1), ("by", 0)), 2)
    padded_depth = clear_poles(padded_depth, 2, row_index, rows_axis)
    outer_corner = corners(padded_depth)
    inner_corner = outer_corner[1:-1, 1:-1]
    outer_inverse = 1.0 / (surface_term + 0.75 * beside_all(outer_corner))
    inverse = outer_inverse[1:-1, 1:-1]
    opening, scales = chebyshev_plan()
    solution = jnp.zeros_like(source)
    residual = source
    direction = opening * (inverse * residual)
    for sweep in range(ITERS):
        carry_scale, forward_scale = scales[sweep]
        padded = with_halo(direction, (("bx", 1), ("by", 0)), 1)
        applied = operate(padded, inner_corner)
        solution = solution + direction
        residual = residual - applied
        if sweep + 1 < ITERS:
            direction = carry_scale * direction + forward_scale * (inverse * residual)
    shaped = solution.reshape(region_rows, block_height, region_cols, block_width).transpose(
        0, 2, 1, 3
    )
    solution_blocks = shaped.reshape(region_blocks, block_height, block_width)
    own_heights = jnp.einsum(
        "nl,lyx->nyx", matches[:held_slots], solution_blocks, precision=lax.Precision.HIGHEST
    )
    remote = jnp.zeros((MOVE, block_height, block_width), jnp.float32)
    for offset in range(1, REACH + 1):
        rows_used = matches[held_slots + (offset - 1) * MOVE : held_slots + offset * MOVE]
        answers = jnp.einsum(
            "nl,lyx->nyx", rows_used, solution_blocks, precision=lax.Precision.HIGHEST
        )
        remote = remote + shifted(answers, ("bx", "by"), -offset)
    padding = jnp.zeros((held_slots - MOVE, block_height, block_width), jnp.float32)
    return own_heights + jnp.concatenate([padding, remote], axis=0)


def solution(mesh):
    placed = (
        P(("bx", "by"), None, None, None),
        P(),
        P("by", "bx"),
        P(),
        P("by", "bx"),
        P("by", "bx"),
    )
    return jax.shard_map(
        on_device,
        mesh=mesh,
        in_specs=placed,
        out_specs=P(("bx", "by"), None, None),
        check_vma=False,
    )
```

profile of v0, /device:TPU:1, one launch (start us, length us, event | category | flops | bytes accessed | tf_op | source)
XLA Modules:
  0.0 173.5 jit_solution(10954130403463500537)
XLA Ops:
  0.0 5.4 %multiply_reduce_fusion = f32[12,64,128]{2,1,0:T(8,128)S(1)} fusion(bf16[12,40,64,128]{3,2,1,0:T(8,128)(2,1)} %param.6, f32[40]{0:T(128)} %param.7), kind=kLoop, calls=%fused_computation | loop fusion | flops 11698176 | bytes 8257696 | tf_op jit(solution)/shard_map/reduce_sum | solution.py:111
  5.7 3.1 %collective-permute-start.4 = (f32[2,64,128]{2,0,1:T(2,128)S(1)}, f32[2,64,128]{2,0,1:T(2,128)S(1)}, u32[]{:S(2)}, u32[]{:S(2)}) collective-permute-start(f32[2,64,128]{2,0,1:T(2,128)S(1)} %slice.612), channel_id=1, source_target_pairs={{0,1},{1,2},{2,3},{3,4},{4,5},{5,6},{6,7},{7,8},{8,9},{9,10},{10,1... | collective-permute-start | bytes 196616 | tf_op jit(solution)/shard_map/ppermute | solution.py:19
  8.8 1.6 collective-permute-start.5
  11.0 1.4 collective-permute-start
  12.4 3.7 %collective-permute-start.1 = (f32[256,2]{1,0:T(8,128)S(1)}, f32[256,2]{1,0:T(8,128)S(1)}, u32[]{:S(2)}, u32[]{:S(2)}) collective-permute-start(f32[256,2]{1,0:T(8,128)S(1)} %get-tuple-element.88), channel_id=1, source_target_pairs={{8,0},{16,8},{24,16},{32,24},{40,32},{48,40},{56,48},{64,56},{72,6... | collective-permute-start | bytes 6152 | tf_op jit(solution)/shard_map/ppermute | solution.py:31
  16.5 2.4 %collective-permute-done = f32[256,2]{1,0:T(8,128)S(1)} collective-permute-done((f32[256,2]{1,0:T(8,128)S(1)}, f32[256,2]{1,0:T(8,128)S(1)}, u32[]{:S(2)}, u32[]{:S(2)}) %collective-permute-start) | collective-permute-done | bytes 2080 | tf_op jit(solution)/shard_map/ppermute | solution.py:29
  19.0 1.7 collective-permute-start.2
  20.7 0.8 collective-permute-done.2
  21.5 2.3 %collective-permute-done.3 = f32[2,516]{1,0:T(2,128)S(1)} collective-permute-done((f32[2,516]{1,0:T(2,128)S(1)}, f32[2,516]{1,0:T(2,128)S(1)}, u32[]{:S(2)}, u32[]{:S(2)}) %collective-permute-start.3) | collective-permute-done | bytes 4160 | tf_op jit(solution)/shard_map/ppermute | solution.py:31
  25.6 0.8 broadcast_multiply_fusion
  26.6 5.4 %collective-permute-start.7 = (f32[256,1]{1,0:T(8,128)S(1)}, f32[256,1]{1,0:T(8,128)S(1)}, u32[]{:S(2)}, u32[]{:S(2)}) collective-permute-start(f32[256,1]{1,0:T(8,128)S(1)} %get-tuple-element.86), channel_id=1, source_target_pairs={{8,0},{16,8},{24,16},{32,24},{40,32},{48,40},{56,48},{64,56},{72,6... | collective-permute-start | bytes 3080 | tf_op jit(solution)/shard_map/ppermute | solution.py:31
  31.9 3.2 %collective-permute-done.6 = f32[256,1]{1,0:T(8,128)S(1)} collective-permute-done((f32[256,1]{1,0:T(8,128)S(1)}, f32[256,1]{1,0:T(8,128)S(1)}, u32[]{:S(2)}, u32[]{:S(2)}) %collective-permute-start.6) | collective-permute-done | bytes 1056 | tf_op jit(solution)/shard_map/ppermute | solution.py:29
  35.2 1.1 collective-permute-start.8
  36.3 0.7 collective-permute-done.8
  37.1 2.4 %collective-permute-done.9 = f32[1,514]{1,0:T(1,128)S(1)} collective-permute-done((f32[1,514]{1,0:T(1,128)S(1)}, f32[1,514]{1,0:T(1,128)S(1)}, u32[]{:S(2)}, u32[]{:S(2)}) %collective-permute-start.9) | collective-permute-done | bytes 2088 | tf_op jit(solution)/shard_map/ppermute | solution.py:31
  40.5 0.9 multiply_add_fusion.7
  41.6 5.6 %collective-permute-start.11 = (f32[256,1]{1,0:T(8,128)S(1)}, f32[256,1]{1,0:T(8,128)S(1)}, u32[]{:S(2)}, u32[]{:S(2)}) collective-permute-start(f32[256,1]{1,0:T(8,128)S(1)} %get-tuple-element.84), channel_id=1, source_target_pairs={{8,0},{16,8},{24,16},{32,24},{40,32},{48,40},{56,48},{64,56},{72,6... | collective-permute-start | bytes 3080 | tf_op jit(solution)/shard_map/ppermute | solution.py:31
  47.2 3.2 %collective-permute-done.10 = f32[256,1]{1,0:T(8,128)S(1)} collective-permute-done((f32[256,1]{1,0:T(8,128)S(1)}, f32[256,1]{1,0:T(8,128)S(1)}, u32[]{:S(2)}, u32[]{:S(2)}) %collective-permute-start.10) | collective-permute-done | bytes 1056 | tf_op jit(solution)/shard_map/ppermute | solution.py:29
  50.5 1.0 collective-permute-start.12
  51.5 0.7 collective-permute-done.12
  52.3 2.6 %collective-permute-done.13 = f32[1,514]{1,0:T(1,128)S(1)} collective-permute-done((f32[1,514]{1,0:T(1,128)S(1)}, f32[1,514]{1,0:T(1,128)S(1)}, u32[]{:S(2)}, u32[]{:S(2)}) %collective-permute-start.13) | collective-permute-done | bytes 2088 | tf_op jit(solution)/shard_map/ppermute | solution.py:31
  56.6 5.6 %collective-permute-start.15 = (f32[256,1]{1,0:T(8,128)S(1)}, f32[256,1]{1,0:T(8,128)S(1)}, u32[]{:S(2)}, u32[]{:S(2)}) collective-permute-start(f32[256,1]{1,0:T(8,128)S(1)} %get-tuple-element.82), channel_id=1, source_target_pairs={{8,0},{16,8},{24,16},{32,24},{40,32},{48,40},{56,48},{64,56},{72,6... | collective-permute-start | bytes 3080 | tf_op jit(solution)/shard_map/ppermute | solution.py:31
  62.2 3.3 %collective-permute-done.14 = f32[256,1]{1,0:T(8,128)S(1)} collective-permute-done((f32[256,1]{1,0:T(8,128)S(1)}, f32[256,1]{1,0:T(8,128)S(1)}, u32[]{:S(2)}, u32[]{:S(2)}) %collective-permute-start.14) | collective-permute-done | bytes 1056 | tf_op jit(solution)/shard_map/ppermute | solution.py:29
  65.9 0.7 collective-permute-start.17
  66.6 0.6 collective-permute-done.16
  67.3 1.7 collective-permute-done.17
  69.4 0.6 fusion.13
  70.7 4.9 %collective-permute-start.19 = (f32[256,1]{1,0:T(8,128)S(1)}, f32[256,1]{1,0:T(8,128)S(1)}, u32[]{:S(2)}, u32[]{:S(2)}) collective-permute-start(f32[256,1]{1,0:T(8,128)S(1)} %get-tuple-element.80), channel_id=1, source_target_pairs={{8,0},{16,8},{24,16},{32,24},{40,32},{48,40},{56,48},{64,56},{72,6... | collective-permute-start | bytes 3080 | tf_op jit(solution)/shard_map/ppermute | solution.py:31
  75.7 2.3 %collective-permute-done.18 = f32[256,1]{1,0:T(8,128)S(1)} collective-permute-done((f32[256,1]{1,0:T(8,128)S(1)}, f32[256,1]{1,0:T(8,128)S(1)}, u32[]{:S(2)}, u32[]{:S(2)}) %collective-permute-start.18) | collective-permute-done | bytes 1056 | tf_op jit(solution)/shard_map/ppermute | solution.py:29
  78.0 2.2 %collective-permute-start.20 = (f32[1,514]{1,0:T(1,128)S(1)}, f32[1,514]{1,0:T(1,128)S(1)}, u32[]{:S(2)}, u32[]{:S(2)}) collective-permute-start(f32[1,514]{1,0:T(1,128)S(1)} %get-tuple-element.49), channel_id=1, source_target_pairs={{0,1},{1,2},{2,3},{3,4},{4,5},{5,6},{6,7},{7,0},{8,9},{9,10},{10,1... | collective-permute-start | bytes 6176 | tf_op jit(solution)/shard_map/ppermute | solution.py:29
  80.2 0.9 collective-permute-start.21
  81.1 0.6 collective-permute-done.20
  81.7 1.5 collective-permute-done.21
  85.0 4.9 %collective-permute-start.23 = (f32[256,1]{1,0:T(8,128)S(1)}, f32[256,1]{1,0:T(8,128)S(1)}, u32[]{:S(2)}, u32[]{:S(2)}) collective-permute-start(f32[256,1]{1,0:T(8,128)S(1)} %get-tuple-element.78), channel_id=1, source_target_pairs={{8,0},{16,8},{24,16},{32,24},{40,32},{48,40},{56,48},{64,56},{72,6... | collective-permute-start | bytes 3080 | tf_op jit(solution)/shard_map/ppermute | solution.py:31
  89.9 2.3 %collective-permute-done.22 = f32[256,1]{1,0:T(8,128)S(1)} collective-permute-done((f32[256,1]{1,0:T(8,128)S(1)}, f32[256,1]{1,0:T(8,128)S(1)}, u32[]{:S(2)}, u32[]{:S(2)}) %collective-permute-start.22) | collective-permute-done | bytes 1056 | tf_op jit(solution)/shard_map/ppermute | solution.py:29
  92.3 2.5 %collective-permute-start.24 = (f32[1,514]{1,0:T(1,128)S(1)}, f32[1,514]{1,0:T(1,128)S(1)}, u32[]{:S(2)}, u32[]{:S(2)}) collective-permute-start(f32[1,514]{1,0:T(1,128)S(1)} %get-tuple-element.45), channel_id=1, source_target_pairs={{0,1},{1,2},{2,3},{3,4},{4,5},{5,6},{6,7},{7,0},{8,9},{9,10},{10,1... | collective-permute-start | bytes 6176 | tf_op jit(solution)/shard_map/ppermute | solution.py:29
  94.8 0.7 collective-permute-start.25
  96.1 1.7 collective-permute-done.25
  99.6 5.0 %collective-permute-start.27 = (f32[256,1]{1,0:T(8,128)S(1)}, f32[256,1]{1,0:T(8,128)S(1)}, u32[]{:S(2)}, u32[]{:S(2)}) collective-permute-start(f32[256,1]{1,0:T(8,128)S(1)} %get-tuple-element.76), channel_id=1, source_target_pairs={{8,0},{16,8},{24,16},{32,24},{40,32},{48,40},{56,48},{64,56},{72,6... | collective-permute-start | bytes 3080 | tf_op jit(solution)/shard_map/ppermute | solution.py:31
  104.5 2.3 %collective-permute-done.26 = f32[256,1]{1,0:T(8,128)S(1)} collective-permute-done((f32[256,1]{1,0:T(8,128)S(1)}, f32[256,1]{1,0:T(8,128)S(1)}, u32[]{:S(2)}, u32[]{:S(2)}) %collective-permute-start.26) | collective-permute-done | bytes 1056 | tf_op jit(solution)/shard_map/ppermute | solution.py:29
  106.9 2.0 %collective-permute-start.28 = (f32[1,514]{1,0:T(1,128)S(1)}, f32[1,514]{1,0:T(1,128)S(1)}, u32[]{:S(2)}, u32[]{:S(2)}) collective-permute-start(f32[1,514]{1,0:T(1,128)S(1)} %get-tuple-element.41), channel_id=1, source_target_pairs={{0,1},{1,2},{2,3},{3,4},{4,5},{5,6},{6,7},{7,0},{8,9},{9,10},{10,1... | collective-permute-start | bytes 6176 | tf_op jit(solution)/shard_map/ppermute | solution.py:29
  108.9 1.0 collective-permute-start.29
  110.0 0.6 collective-permute-done.28
  110.6 1.4 collective-permute-done.29
  113.7 5.1 %collective-permute-start.31 = (f32[256,1]{1,0:T(8,128)S(1)}, f32[256,1]{1,0:T(8,128)S(1)}, u32[]{:S(2)}, u32[]{:S(2)}) collective-permute-start(f32[256,1]{1,0:T(8,128)S(1)} %get-tuple-element.74), channel_id=1, source_target_pairs={{8,0},{16,8},{24,16},{32,24},{40,32},{48,40},{56,48},{64,56},{72,6... | collective-permute-start | bytes 3080 | tf_op jit(solution)/shard_map/ppermute | solution.py:31
  118.9 2.1 %collective-permute-done.30 = f32[256,1]{1,0:T(8,128)S(1)} collective-permute-done((f32[256,1]{1,0:T(8,128)S(1)}, f32[256,1]{1,0:T(8,128)S(1)}, u32[]{:S(2)}, u32[]{:S(2)}) %collective-permute-start.30) | collective-permute-done | bytes 1056 | tf_op jit(solution)/shard_map/ppermute | solution.py:29
  121.0 1.7 collective-permute-start.32
  122.7 1.7 collective-permute-start.33
  125.1 0.7 collective-permute-done.33
  127.5 5.1 %collective-permute-start.35 = (f32[256,1]{1,0:T(8,128)S(1)}, f32[256,1]{1,0:T(8,128)S(1)}, u32[]{:S(2)}, u32[]{:S(2)}) collective-permute-start(f32[256,1]{1,0:T(8,128)S(1)} %get-tuple-element.72), channel_id=1, source_target_pairs={{8,0},{16,8},{24,16},{32,24},{40,32},{48,40},{56,48},{64,56},{72,6... | collective-permute-start | bytes 3080 | tf_op jit(solution)/shard_map/ppermute | solution.py:31
  132.6 2.3 %collective-permute-done.34 = f32[256,1]{1,0:T(8,128)S(1)} collective-permute-done((f32[256,1]{1,0:T(8,128)S(1)}, f32[256,1]{1,0:T(8,128)S(1)}, u32[]{:S(2)}, u32[]{:S(2)}) %collective-permute-start.34) | collective-permute-done | bytes 1056 | tf_op jit(solution)/shard_map/ppermute | solution.py:29
  135.0 1.1 collective-permute-start.36
  136.1 3.0 %collective-permute-start.37 = (f32[1,514]{1,0:T(1,128)S(1)}, f32[1,514]{1,0:T(1,128)S(1)}, u32[]{:S(2)}, u32[]{:S(2)}) collective-permute-start(f32[1,514]{1,0:T(1,128)S(1)} %get-tuple-element.34), channel_id=1, source_target_pairs={{1,0},{2,1},{3,2},{4,3},{5,4},{6,5},{7,6},{0,7},{9,8},{10,9},{11,1... | collective-permute-start | bytes 6176 | tf_op jit(solution)/shard_map/ppermute | solution.py:31
  139.1 0.6 collective-permute-done.36
  141.8 5.2 %collective-permute-start.39 = (f32[256,1]{1,0:T(8,128)S(1)}, f32[256,1]{1,0:T(8,128)S(1)}, u32[]{:S(2)}, u32[]{:S(2)}) collective-permute-start(f32[256,1]{1,0:T(8,128)S(1)} %get-tuple-element.70), channel_id=1, source_target_pairs={{8,0},{16,8},{24,16},{32,24},{40,32},{48,40},{56,48},{64,56},{72,6... | collective-permute-start | bytes 3080 | tf_op jit(solution)/shard_map/ppermute | solution.py:31
  147.0 2.3 %collective-permute-done.38 = f32[256,1]{1,0:T(8,128)S(1)} collective-permute-done((f32[256,1]{1,0:T(8,128)S(1)}, f32[256,1]{1,0:T(8,128)S(1)}, u32[]{:S(2)}, u32[]{:S(2)}) %collective-permute-start.38) | collective-permute-done | bytes 1056 | tf_op jit(solution)/shard_map/ppermute | solution.py:29
  149.4 1.3 collective-permute-start.40
  150.7 3.0 %collective-permute-start.41 = (f32[1,514]{1,0:T(1,128)S(1)}, f32[1,514]{1,0:T(1,128)S(1)}, u32[]{:S(2)}, u32[]{:S(2)}) collective-permute-start(f32[1,514]{1,0:T(1,128)S(1)} %get-tuple-element.30), channel_id=1, source_target_pairs={{1,0},{2,1},{3,2},{4,3},{5,4},{6,5},{7,6},{0,7},{9,8},{10,9},{11,1... | collective-permute-start | bytes 6176 | tf_op jit(solution)/shard_map/ppermute | solution.py:31
  155.0 0.6 fusion.1
  155.6 1.1 fusion.24
  157.6 10.9 %collective-permute-start.43 = (f32[2,64,128]{2,0,1:T(2,128)S(1)}, f32[2,64,128]{2,0,1:T(2,128)S(1)}, u32[]{:S(2)}, u32[]{:S(2)}) collective-permute-start(f32[2,64,128]{2,0,1:T(2,128)S(1)} %fusion.57), channel_id=1, source_target_pairs={{0,126},{1,127},{2,0},{3,1},{4,2},{5,3},{6,4},{7,5},{8,6},{9,7},{1... | collective-permute-start | bytes 196616 | tf_op jit(solution)/shard_map/ppermute | solution.py:19
  168.5 1.3 collective-permute-done.43
  169.8 2.4 %collective-permute-done.42 = f32[2,64,128]{2,0,1:T(2,128)S(1)} collective-permute-done((f32[2,64,128]{2,0,1:T(2,128)S(1)}, f32[2,64,128]{2,0,1:T(2,128)S(1)}, u32[]{:S(2)}, u32[]{:S(2)}) %collective-permute-start.42) | collective-permute-done | bytes 65568 | tf_op jit(solution)/shard_map/ppermute | solution.py:19
  172.6 0.9 copy.20
  (109 shorter events, 21.3 us)
Async XLA Ops:
  0.0 10.5 %copy-start.2 = (s32[4,4]{1,0:T(4,128)S(1)}, s32[4,4]{1,0:T(4,128)}, u32[]{:S(2)}) copy-start(s32[4,4]{1,0:T(4,128)} %param.10) | copy-start | bytes 196
  0.0 10.5 %copy-start.3 = (s32[4,4]{1,0:T(4,128)S(1)}, s32[4,4]{1,0:T(4,128)}, u32[]{:S(2)}) copy-start(s32[4,4]{1,0:T(4,128)} %param.11) | copy-start | bytes 196
  0.0 10.8 %copy-start = (f32[256,512]{1,0:T(8,128)S(1)}, f32[256,512]{1,0:T(8,128)}, u32[]{:S(2)}) copy-start(f32[256,512]{1,0:T(8,128)} %param.8) | copy-start | bytes 1572868
  0.0 16.1 %copy-start.1 = (s32[1536]{0:T(1024)S(1)}, s32[1536]{0:T(1024)}, u32[]{:S(2)}) copy-start(s32[1536]{0:T(1024)} %param.9) | copy-start | bytes 18436
  5.7 19.3 %collective-permute-start.4 = (f32[2,64,128]{2,0,1:T(2,128)S(1)}, f32[2,64,128]{2,0,1:T(2,128)S(1)}, u32[]{:S(2)}, u32[]{:S(2)}) collective-permute-start(f32[2,64,128]{2,0,1:T(2,128)S(1)} %slice.612), channel_id=1, source_target_pairs={{0,1},{1,2},{2,3},{3,4},{4,5},{5,6},{6,7},{7,8},{8,9},{9,10},{10,1... | collective-permute-start | bytes 196616 | tf_op jit(solution)/shard_map/ppermute | solution.py:19
  8.8 16.2 %collective-permute-start.5 = (f32[2,64,128]{2,0,1:T(2,128)S(1)}, f32[2,64,128]{2,0,1:T(2,128)S(1)}, u32[]{:S(2)}, u32[]{:S(2)}) collective-permute-start(f32[2,64,128]{2,0,1:T(2,128)S(1)} %slice.612), channel_id=1, source_target_pairs={{0,2},{1,3},{2,4},{3,5},{4,6},{5,7},{6,8},{7,9},{8,10},{9,11},{10,... | collective-permute-start | bytes 196616 | tf_op jit(solution)/shard_map/ppermute | solution.py:19
  11.0 7.9 %collective-permute-start = (f32[256,2]{1,0:T(8,128)S(1)}, f32[256,2]{1,0:T(8,128)S(1)}, u32[]{:S(2)}, u32[]{:S(2)}) collective-permute-start(f32[256,2]{1,0:T(8,128)S(1)} %get-tuple-element.87), channel_id=1, source_target_pairs={{0,8},{8,16},{16,24},{24,32},{32,40},{40,48},{48,56},{56,64},{64,7... | collective-permute-start | bytes 6152 | tf_op jit(solution)/shard_map/ppermute | solution.py:29
  12.4 6.5 %collective-permute-start.1 = (f32[256,2]{1,0:T(8,128)S(1)}, f32[256,2]{1,0:T(8,128)S(1)}, u32[]{:S(2)}, u32[]{:S(2)}) collective-permute-start(f32[256,2]{1,0:T(8,128)S(1)} %get-tuple-element.88), channel_id=1, source_target_pairs={{8,0},{16,8},{24,16},{32,24},{40,32},{48,40},{56,48},{64,56},{72,6... | collective-permute-start | bytes 6152 | tf_op jit(solution)/shard_map/ppermute | solution.py:31
  19.0 2.5 %collective-permute-start.2 = (f32[2,516]{1,0:T(2,128)S(1)}, f32[2,516]{1,0:T(2,128)S(1)}, u32[]{:S(2)}, u32[]{:S(2)}) collective-permute-start(f32[2,516]{1,0:T(2,128)S(1)} %get-tuple-element.63), channel_id=1, source_target_pairs={{0,1},{1,2},{2,3},{3,4},{4,5},{5,6},{6,7},{7,0},{8,9},{9,10},{10,1... | collective-permute-start | bytes 12392 | tf_op jit(solution)/shard_map/ppermute | solution.py:29
  20.7 3.0 %collective-permute-start.3 = (f32[2,516]{1,0:T(2,128)S(1)}, f32[2,516]{1,0:T(2,128)S(1)}, u32[]{:S(2)}, u32[]{:S(2)}) collective-permute-start(f32[2,516]{1,0:T(2,128)S(1)} %get-tuple-element.64), channel_id=1, source_target_pairs={{1,0},{2,1},{3,2},{4,3},{5,4},{6,5},{7,6},{0,7},{9,8},{10,9},{11,1... | collective-permute-start | bytes 12392 | tf_op jit(solution)/shard_map/ppermute | solution.py:31
  26.5 8.7 %collective-permute-start.6 = (f32[256,1]{1,0:T(8,128)S(1)}, f32[256,1]{1,0:T(8,128)S(1)}, u32[]{:S(2)}, u32[]{:S(2)}) collective-permute-start(f32[256,1]{1,0:T(8,128)S(1)} %get-tuple-element.85), channel_id=1, source_target_pairs={{0,8},{8,16},{16,24},{24,32},{32,40},{40,48},{48,56},{56,64},{64,7... | collective-permute-start | bytes 3080 | tf_op jit(solution)/shard_map/ppermute | solution.py:29
  26.6 8.6 %collective-permute-start.7 = (f32[256,1]{1,0:T(8,128)S(1)}, f32[256,1]{1,0:T(8,128)S(1)}, u32[]{:S(2)}, u32[]{:S(2)}) collective-permute-start(f32[256,1]{1,0:T(8,128)S(1)} %get-tuple-element.86), channel_id=1, source_target_pairs={{8,0},{16,8},{24,16},{32,24},{40,32},{48,40},{56,48},{64,56},{72,6... | collective-permute-start | bytes 3080 | tf_op jit(solution)/shard_map/ppermute | solution.py:31
  35.2 1.8 %collective-permute-start.8 = (f32[1,514]{1,0:T(1,128)S(1)}, f32[1,514]{1,0:T(1,128)S(1)}, u32[]{:S(2)}, u32[]{:S(2)}) collective-permute-start(f32[1,514]{1,0:T(1,128)S(1)} %get-tuple-element.61), channel_id=1, source_target_pairs={{0,1},{1,2},{2,3},{3,4},{4,5},{5,6},{6,7},{7,0},{8,9},{9,10},{10,1... | collective-permute-start | bytes 6176 | tf_op jit(solution)/shard_map/ppermute | solution.py:29
  36.3 3.1 %collective-permute-start.9 = (f32[1,514]{1,0:T(1,128)S(1)}, f32[1,514]{1,0:T(1,128)S(1)}, u32[]{:S(2)}, u32[]{:S(2)}) collective-permute-start(f32[1,514]{1,0:T(1,128)S(1)} %get-tuple-element.62), channel_id=1, source_target_pairs={{1,0},{2,1},{3,2},{4,3},{5,4},{6,5},{7,6},{0,7},{9,8},{10,9},{11,1... | collective-permute-start | bytes 6176 | tf_op jit(solution)/shard_map/ppermute | solution.py:31
  41.6 8.9 %collective-permute-start.10 = (f32[256,1]{1,0:T(8,128)S(1)}, f32[256,1]{1,0:T(8,128)S(1)}, u32[]{:S(2)}, u32[]{:S(2)}) collective-permute-start(f32[256,1]{1,0:T(8,128)S(1)} %get-tuple-element.83), channel_id=1, source_target_pairs={{0,8},{8,16},{16,24},{24,32},{32,40},{40,48},{48,56},{56,64},{64,7... | collective-permute-start | bytes 3080 | tf_op jit(solution)/shard_map/ppermute | solution.py:29
  41.6 8.8 %collective-permute-start.11 = (f32[256,1]{1,0:T(8,128)S(1)}, f32[256,1]{1,0:T(8,128)S(1)}, u32[]{:S(2)}, u32[]{:S(2)}) collective-permute-start(f32[256,1]{1,0:T(8,128)S(1)} %get-tuple-element.84), channel_id=1, source_target_pairs={{8,0},{16,8},{24,16},{32,24},{40,32},{48,40},{56,48},{64,56},{72,6... | collective-permute-start | bytes 3080 | tf_op jit(solution)/shard_map/ppermute | solution.py:31
  50.5 1.7 collective-permute-start.12
  51.5 3.3 %collective-permute-start.13 = (f32[1,514]{1,0:T(1,128)S(1)}, f32[1,514]{1,0:T(1,128)S(1)}, u32[]{:S(2)}, u32[]{:S(2)}) collective-permute-start(f32[1,514]{1,0:T(1,128)S(1)} %get-tuple-element.58), channel_id=1, source_target_pairs={{1,0},{2,1},{3,2},{4,3},{5,4},{6,5},{7,6},{0,7},{9,8},{10,9},{11,1... | collective-permute-start | bytes 6176 | tf_op jit(solution)/shard_map/ppermute | solution.py:31
  56.5 9.0 %collective-permute-start.14 = (f32[256,1]{1,0:T(8,128)S(1)}, f32[256,1]{1,0:T(8,128)S(1)}, u32[]{:S(2)}, u32[]{:S(2)}) collective-permute-start(f32[256,1]{1,0:T(8,128)S(1)} %get-tuple-element.81), channel_id=1, source_target_pairs={{0,8},{8,16},{16,24},{24,32},{32,40},{40,48},{48,56},{56,64},{64,7... | collective-permute-start | bytes 3080 | tf_op jit(solution)/shard_map/ppermute | solution.py:29
  56.6 8.9 %collective-permute-start.15 = (f32[256,1]{1,0:T(8,128)S(1)}, f32[256,1]{1,0:T(8,128)S(1)}, u32[]{:S(2)}, u32[]{:S(2)}) collective-permute-start(f32[256,1]{1,0:T(8,128)S(1)} %get-tuple-element.82), channel_id=1, source_target_pairs={{8,0},{16,8},{24,16},{32,24},{40,32},{48,40},{56,48},{64,56},{72,6... | collective-permute-start | bytes 3080 | tf_op jit(solution)/shard_map/ppermute | solution.py:31
  65.5 1.7 collective-permute-start.16
  65.9 3.0 %collective-permute-start.17 = (f32[1,514]{1,0:T(1,128)S(1)}, f32[1,514]{1,0:T(1,128)S(1)}, u32[]{:S(2)}, u32[]{:S(2)}) collective-permute-start(f32[1,514]{1,0:T(1,128)S(1)} %get-tuple-element.54), channel_id=1, source_target_pairs={{1,0},{2,1},{3,2},{4,3},{5,4},{6,5},{7,6},{0,7},{9,8},{10,9},{11,1... | collective-permute-start | bytes 6176 | tf_op jit(solution)/shard_map/ppermute | solution.py:31
  70.7 7.3 %collective-permute-start.18 = (f32[256,1]{1,0:T(8,128)S(1)}, f32[256,1]{1,0:T(8,128)S(1)}, u32[]{:S(2)}, u32[]{:S(2)}) collective-permute-start(f32[256,1]{1,0:T(8,128)S(1)} %get-tuple-element.79), channel_id=1, source_target_pairs={{0,8},{8,16},{16,24},{24,32},{32,40},{40,48},{48,56},{56,64},{64,7... | collective-permute-start | bytes 3080 | tf_op jit(solution)/shard_map/ppermute | solution.py:29
  70.7 7.2 %collective-permute-start.19 = (f32[256,1]{1,0:T(8,128)S(1)}, f32[256,1]{1,0:T(8,128)S(1)}, u32[]{:S(2)}, u32[]{:S(2)}) collective-permute-start(f32[256,1]{1,0:T(8,128)S(1)} %get-tuple-element.80), channel_id=1, source_target_pairs={{8,0},{16,8},{24,16},{32,24},{40,32},{48,40},{56,48},{64,56},{72,6... | collective-permute-start | bytes 3080 | tf_op jit(solution)/shard_map/ppermute | solution.py:31
  78.0 3.7 %collective-permute-start.20 = (f32[1,514]{1,0:T(1,128)S(1)}, f32[1,514]{1,0:T(1,128)S(1)}, u32[]{:S(2)}, u32[]{:S(2)}) collective-permute-start(f32[1,514]{1,0:T(1,128)S(1)} %get-tuple-element.49), channel_id=1, source_target_pairs={{0,1},{1,2},{2,3},{3,4},{4,5},{5,6},{6,7},{7,0},{8,9},{9,10},{10,1... | collective-permute-start | bytes 6176 | tf_op jit(solution)/shard_map/ppermute | solution.py:29
  80.2 3.0 %collective-permute-start.21 = (f32[1,514]{1,0:T(1,128)S(1)}, f32[1,514]{1,0:T(1,128)S(1)}, u32[]{:S(2)}, u32[]{:S(2)}) collective-permute-start(f32[1,514]{1,0:T(1,128)S(1)} %get-tuple-element.50), channel_id=1, source_target_pairs={{1,0},{2,1},{3,2},{4,3},{5,4},{6,5},{7,6},{0,7},{9,8},{10,9},{11,1... | collective-permute-start | bytes 6176 | tf_op jit(solution)/shard_map/ppermute | solution.py:31
  84.9 7.3 %collective-permute-start.22 = (f32[256,1]{1,0:T(8,128)S(1)}, f32[256,1]{1,0:T(8,128)S(1)}, u32[]{:S(2)}, u32[]{:S(2)}) collective-permute-start(f32[256,1]{1,0:T(8,128)S(1)} %get-tuple-element.77), channel_id=1, source_target_pairs={{0,8},{8,16},{16,24},{24,32},{32,40},{40,48},{48,56},{56,64},{64,7... | collective-permute-start | bytes 3080 | tf_op jit(solution)/shard_map/ppermute | solution.py:29
  85.0 7.2 %collective-permute-start.23 = (f32[256,1]{1,0:T(8,128)S(1)}, f32[256,1]{1,0:T(8,128)S(1)}, u32[]{:S(2)}, u32[]{:S(2)}) collective-permute-start(f32[256,1]{1,0:T(8,128)S(1)} %get-tuple-element.78), channel_id=1, source_target_pairs={{8,0},{16,8},{24,16},{32,24},{40,32},{48,40},{56,48},{64,56},{72,6... | collective-permute-start | bytes 3080 | tf_op jit(solution)/shard_map/ppermute | solution.py:31
  92.3 3.8 %collective-permute-start.24 = (f32[1,514]{1,0:T(1,128)S(1)}, f32[1,514]{1,0:T(1,128)S(1)}, u32[]{:S(2)}, u32[]{:S(2)}) collective-permute-start(f32[1,514]{1,0:T(1,128)S(1)} %get-tuple-element.45), channel_id=1, source_target_pairs={{0,1},{1,2},{2,3},{3,4},{4,5},{5,6},{6,7},{7,0},{8,9},{9,10},{10,1... | collective-permute-start | bytes 6176 | tf_op jit(solution)/shard_map/ppermute | solution.py:29
  94.8 3.0 %collective-permute-start.25 = (f32[1,514]{1,0:T(1,128)S(1)}, f32[1,514]{1,0:T(1,128)S(1)}, u32[]{:S(2)}, u32[]{:S(2)}) collective-permute-start(f32[1,514]{1,0:T(1,128)S(1)} %get-tuple-element.46), channel_id=1, source_target_pairs={{1,0},{2,1},{3,2},{4,3},{5,4},{6,5},{7,6},{0,7},{9,8},{10,9},{11,1... | collective-permute-start | bytes 6176 | tf_op jit(solution)/shard_map/ppermute | solution.py:31
  99.5 7.3 %collective-permute-start.26 = (f32[256,1]{1,0:T(8,128)S(1)}, f32[256,1]{1,0:T(8,128)S(1)}, u32[]{:S(2)}, u32[]{:S(2)}) collective-permute-start(f32[256,1]{1,0:T(8,128)S(1)} %get-tuple-element.75), channel_id=1, source_target_pairs={{0,8},{8,16},{16,24},{24,32},{32,40},{40,48},{48,56},{56,64},{64,7... | collective-permute-start | bytes 3080 | tf_op jit(solution)/shard_map/ppermute | solution.py:29
  99.6 7.2 %collective-permute-start.27 = (f32[256,1]{1,0:T(8,128)S(1)}, f32[256,1]{1,0:T(8,128)S(1)}, u32[]{:S(2)}, u32[]{:S(2)}) collective-permute-start(f32[256,1]{1,0:T(8,128)S(1)} %get-tuple-element.76), channel_id=1, source_target_pairs={{8,0},{16,8},{24,16},{32,24},{40,32},{48,40},{56,48},{64,56},{72,6... | collective-permute-start | bytes 3080 | tf_op jit(solution)/shard_map/ppermute | solution.py:31
  106.9 3.7 %collective-permute-start.28 = (f32[1,514]{1,0:T(1,128)S(1)}, f32[1,514]{1,0:T(1,128)S(1)}, u32[]{:S(2)}, u32[]{:S(2)}) collective-permute-start(f32[1,514]{1,0:T(1,128)S(1)} %get-tuple-element.41), channel_id=1, source_target_pairs={{0,1},{1,2},{2,3},{3,4},{4,5},{5,6},{6,7},{7,0},{8,9},{9,10},{10,1... | collective-permute-start | bytes 6176 | tf_op jit(solution)/shard_map/ppermute | solution.py:29
  108.9 3.0 %collective-permute-start.29 = (f32[1,514]{1,0:T(1,128)S(1)}, f32[1,514]{1,0:T(1,128)S(1)}, u32[]{:S(2)}, u32[]{:S(2)}) collective-permute-start(f32[1,514]{1,0:T(1,128)S(1)} %get-tuple-element.42), channel_id=1, source_target_pairs={{1,0},{2,1},{3,2},{4,3},{5,4},{6,5},{7,6},{0,7},{9,8},{10,9},{11,1... | collective-permute-start | bytes 6176 | tf_op jit(solution)/shard_map/ppermute | solution.py:31
  113.6 7.3 %collective-permute-start.30 = (f32[256,1]{1,0:T(8,128)S(1)}, f32[256,1]{1,0:T(8,128)S(1)}, u32[]{:S(2)}, u32[]{:S(2)}) collective-permute-start(f32[256,1]{1,0:T(8,128)S(1)} %get-tuple-element.73), channel_id=1, source_target_pairs={{0,8},{8,16},{16,24},{24,32},{32,40},{40,48},{48,56},{56,64},{64,7... | collective-permute-start | bytes 3080 | tf_op jit(solution)/shard_map/ppermute | solution.py:29
  113.7 7.2 %collective-permute-start.31 = (f32[256,1]{1,0:T(8,128)S(1)}, f32[256,1]{1,0:T(8,128)S(1)}, u32[]{:S(2)}, u32[]{:S(2)}) collective-permute-start(f32[256,1]{1,0:T(8,128)S(1)} %get-tuple-element.74), channel_id=1, source_target_pairs={{8,0},{16,8},{24,16},{32,24},{40,32},{48,40},{56,48},{64,56},{72,6... | collective-permute-start | bytes 3080 | tf_op jit(solution)/shard_map/ppermute | solution.py:31
  121.0 4.1 %collective-permute-start.32 = (f32[1,514]{1,0:T(1,128)S(1)}, f32[1,514]{1,0:T(1,128)S(1)}, u32[]{:S(2)}, u32[]{:S(2)}) collective-permute-start(f32[1,514]{1,0:T(1,128)S(1)} %get-tuple-element.37), channel_id=1, source_target_pairs={{0,1},{1,2},{2,3},{3,4},{4,5},{5,6},{6,7},{7,0},{8,9},{9,10},{10,1... | collective-permute-start | bytes 6176 | tf_op jit(solution)/shard_map/ppermute | solution.py:29
  122.7 3.0 %collective-permute-start.33 = (f32[1,514]{1,0:T(1,128)S(1)}, f32[1,514]{1,0:T(1,128)S(1)}, u32[]{:S(2)}, u32[]{:S(2)}) collective-permute-start(f32[1,514]{1,0:T(1,128)S(1)} %get-tuple-element.38), channel_id=1, source_target_pairs={{1,0},{2,1},{3,2},{4,3},{5,4},{6,5},{7,6},{0,7},{9,8},{10,9},{11,1... | collective-permute-start | bytes 6176 | tf_op jit(solution)/shard_map/ppermute | solution.py:31
  127.4 7.5 %collective-permute-start.34 = (f32[256,1]{1,0:T(8,128)S(1)}, f32[256,1]{1,0:T(8,128)S(1)}, u32[]{:S(2)}, u32[]{:S(2)}) collective-permute-start(f32[256,1]{1,0:T(8,128)S(1)} %get-tuple-element.71), channel_id=1, source_target_pairs={{0,8},{8,16},{16,24},{24,32},{32,40},{40,48},{48,56},{56,64},{64,7... | collective-permute-start | bytes 3080 | tf_op jit(solution)/shard_map/ppermute | solution.py:29
  127.5 7.4 %collective-permute-start.35 = (f32[256,1]{1,0:T(8,128)S(1)}, f32[256,1]{1,0:T(8,128)S(1)}, u32[]{:S(2)}, u32[]{:S(2)}) collective-permute-start(f32[256,1]{1,0:T(8,128)S(1)} %get-tuple-element.72), channel_id=1, source_target_pairs={{8,0},{16,8},{24,16},{32,24},{40,32},{48,40},{56,48},{64,56},{72,6... | collective-permute-start | bytes 3080 | tf_op jit(solution)/shard_map/ppermute | solution.py:31
  135.0 4.8 %collective-permute-start.36 = (f32[1,514]{1,0:T(1,128)S(1)}, f32[1,514]{1,0:T(1,128)S(1)}, u32[]{:S(2)}, u32[]{:S(2)}) collective-permute-start(f32[1,514]{1,0:T(1,128)S(1)} %get-tuple-element.33), channel_id=1, source_target_pairs={{0,1},{1,2},{2,3},{3,4},{4,5},{5,6},{6,7},{7,0},{8,9},{9,10},{10,1... | collective-permute-start | bytes 6176 | tf_op jit(solution)/shard_map/ppermute | solution.py:29
  136.1 3.9 %collective-permute-start.37 = (f32[1,514]{1,0:T(1,128)S(1)}, f32[1,514]{1,0:T(1,128)S(1)}, u32[]{:S(2)}, u32[]{:S(2)}) collective-permute-start(f32[1,514]{1,0:T(1,128)S(1)} %get-tuple-element.34), channel_id=1, source_target_pairs={{1,0},{2,1},{3,2},{4,3},{5,4},{6,5},{7,6},{0,7},{9,8},{10,9},{11,1... | collective-permute-start | bytes 6176 | tf_op jit(solution)/shard_map/ppermute | solution.py:31
  141.7 7.6 %collective-permute-start.38 = (f32[256,1]{1,0:T(8,128)S(1)}, f32[256,1]{1,0:T(8,128)S(1)}, u32[]{:S(2)}, u32[]{:S(2)}) collective-permute-start(f32[256,1]{1,0:T(8,128)S(1)} %get-tuple-element.69), channel_id=1, source_target_pairs={{0,8},{8,16},{16,24},{24,32},{32,40},{40,48},{48,56},{56,64},{64,7... | collective-permute-start | bytes 3080 | tf_op jit(solution)/shard_map/ppermute | solution.py:29
  141.8 7.5 %collective-permute-start.39 = (f32[256,1]{1,0:T(8,128)S(1)}, f32[256,1]{1,0:T(8,128)S(1)}, u32[]{:S(2)}, u32[]{:S(2)}) collective-permute-start(f32[256,1]{1,0:T(8,128)S(1)} %get-tuple-element.70), channel_id=1, source_target_pairs={{8,0},{16,8},{24,16},{32,24},{40,32},{48,40},{56,48},{64,56},{72,6... | collective-permute-start | bytes 3080 | tf_op jit(solution)/shard_map/ppermute | solution.py:31
  149.4 5.0 %collective-permute-start.40 = (f32[1,514]{1,0:T(1,128)S(1)}, f32[1,514]{1,0:T(1,128)S(1)}, u32[]{:S(2)}, u32[]{:S(2)}) collective-permute-start(f32[1,514]{1,0:T(1,128)S(1)} %get-tuple-element.29), channel_id=1, source_target_pairs={{0,1},{1,2},{2,3},{3,4},{4,5},{5,6},{6,7},{7,0},{8,9},{9,10},{10,1... | collective-permute-start | bytes 6176 | tf_op jit(solution)/shard_map/ppermute | solution.py:29
  150.7 3.9 %collective-permute-start.41 = (f32[1,514]{1,0:T(1,128)S(1)}, f32[1,514]{1,0:T(1,128)S(1)}, u32[]{:S(2)}, u32[]{:S(2)}) collective-permute-start(f32[1,514]{1,0:T(1,128)S(1)} %get-tuple-element.30), channel_id=1, source_target_pairs={{1,0},{2,1},{3,2},{4,3},{5,4},{6,5},{7,6},{0,7},{9,8},{10,9},{11,1... | collective-permute-start | bytes 6176 | tf_op jit(solution)/shard_map/ppermute | solution.py:31
  157.6 12.2 %collective-permute-start.43 = (f32[2,64,128]{2,0,1:T(2,128)S(1)}, f32[2,64,128]{2,0,1:T(2,128)S(1)}, u32[]{:S(2)}, u32[]{:S(2)}) collective-permute-start(f32[2,64,128]{2,0,1:T(2,128)S(1)} %fusion.57), channel_id=1, source_target_pairs={{0,126},{1,127},{2,0},{3,1},{4,2},{5,3},{6,4},{7,5},{8,6},{9,7},{1... | collective-permute-start | bytes 196616 | tf_op jit(solution)/shard_map/ppermute | solution.py:19
  168.5 3.7 %collective-permute-start.42 = (f32[2,64,128]{2,0,1:T(2,128)S(1)}, f32[2,64,128]{2,0,1:T(2,128)S(1)}, u32[]{:S(2)}, u32[]{:S(2)}) collective-permute-start(f32[2,64,128]{2,0,1:T(2,128)S(1)} %fusion.58), channel_id=1, source_target_pairs={{0,127},{1,0},{2,1},{3,2},{4,3},{5,4},{6,5},{7,6},{8,7},{9,8},{10,... | collective-permute-start | bytes 196616 | tf_op jit(solution)/shard_map/ppermute | solution.py:19
where the time goes:
time: 174 us; the launch traced here: 173 us
  starting transfers between devices  94.3 us (54%)
  waiting for transfers between devices  50.4 us (29%)
  other arithmetic  23.6 us (14%)
  local copies, waits for them, and re-layouts  3.18 us (2%)
    ppermute x20, starting transfers between devices, with_halo(): lax.ppermute(head, axis, [((i + 1) % count, i) for i in range(count)])  61.6 us
    ppermute x20, waiting for transfers between devices, with_halo(): lax.ppermute(tail, axis, [(i, (i + 1) % count) for i in range(count)])  32.2 us
    ppermute x20, starting transfers between devices, with_halo(): lax.ppermute(tail, axis, [(i, (i + 1) % count) for i in range(count)])  17 us
    ppermute x4, starting transfers between devices, shifted(): return lax.ppermute(value, axis, pairs)  15.6 us
    ppermute x20, waiting for transfers between devices, with_halo(): lax.ppermute(head, axis, [((i + 1) % count, i) for i in range(count)])  14.5 us
    mul x9, other arithmetic, operate(): corner_depth * corner_mean  5.58 us
    reduce_sum x1, other arithmetic, on_device(): jnp.sum(tendency.astype(jnp.float32) * thickness[None, :, None, None], ax...  5.39 us
    add x8, other arithmetic, on_device(): direction = carry_scale * direction + forward_scale * (inverse * residual)  4.34 us
  transfers between devices with their start and end apart: 44, of which 32 were waited for; matrix products, arithmetic and copies ran while one was open for 1% of the time, Pallas kernels for 0%

commit v1 on v0

v1 whole, which is shorter than its diff:
```python
import functools

import jax
import jax.numpy as jnp
from jax import lax
from jax.experimental import pallas as pl
from jax.experimental.pallas import tpu as pltpu
from jax.sharding import PartitionSpec as P

MOVE = 2
ITERS = 10
ROWS, LANES = 64, 128
SLOTS = 12
KEPT = SLOTS - MOVE
LEVELS = 40
REGION = 4
OWN_ROWS = REGION * ROWS
CHUNK = 35
EXT_ROWS = 8 * CHUNK
FOLD = 72
PACK_ROWS = 4 * FOLD
COLS = REGION + 1

surface_term = 0.1
lower_bound = 0.05
upper_bound = 2.0

VMEM = pltpu.MemorySpace.VMEM
SMEM = pltpu.MemorySpace.SMEM


def chebyshev_plan():
    centre_value = (upper_bound + lower_bound) / 2.0
    half_width = (upper_bound - lower_bound) / 2.0
    ratio_value = centre_value / half_width
    weight = 1.0 / ratio_value
    scales = []
    for sweep in range(ITERS):
        renewed = 1.0 / (2.0 * ratio_value - weight)
        scales.append((renewed * weight, 2.0 * renewed / half_width))
        weight = renewed
    return (1.0 / centre_value, scales)


def place(block):
    row, col = block // 64, block % 64
    return (col // REGION) * 8 + row // REGION, row % REGION, col % REGION


def rolled(value, steps, axis):
    return pltpu.roll(value, steps % value.shape[axis], axis)


def column_sum(tend_ref, thick_ref):
    out = []
    for tile in range(ROWS // 16):
        total = jnp.zeros((16, LANES), jnp.float32)
        for level in range(LEVELS):
            part = tend_ref[0, level, tile * 16 : tile * 16 + 16, :].astype(jnp.float32)
            total = total + part * thick_ref[level]
        out.append(total)
    return out


def moved_kernel(thick_ref, tend_ref, moved_ref, bottom_ref):
    tiles = column_sum(tend_ref, thick_ref)
    for tile, value in enumerate(tiles):
        moved_ref[0, tile * 16 : tile * 16 + 16, :] = value
    bottom_ref[0] = tiles[-1]


def wetness(rows, first_row, count, mask):
    position = (lax.broadcasted_iota(jnp.int32, (rows, LANES), 0) + first_row) * LANES + (
        lax.broadcasted_iota(jnp.int32, (rows, LANES), 1)
    )
    return (position < count) & (mask == 1)


def kept_kernel(
    thick_ref, owner_ref, count_ref, mask_ref, tend_ref, moved_ref, head_ref, tail_ref,
    kept_ref, up_ref, down_ref,
):
    step = pl.program_id(0)
    myself = lax.axis_index("bx") * 8 + lax.axis_index("by")

    def edges(slot, top, bottom):
        region, row, col = place(owner_ref[myself * SLOTS + slot])
        lanes = pl.ds(pl.multiple_of(col * LANES, LANES), LANES)

        @pl.when((region == myself) & (row == 0))
        def _():
            up_ref[16:32, lanes] = top

        @pl.when((region == myself) & (row == REGION - 1))
        def _():
            down_ref[16:32, lanes] = bottom

    @pl.when(step == 0)
    def _():
        up_ref[16:32, :] = jnp.zeros((16, REGION * LANES), jnp.float32)
        down_ref[16:32, :] = jnp.zeros((16, REGION * LANES), jnp.float32)
        for col in range(REGION):
            lanes = slice(col * LANES, (col + 1) * LANES)
            wet = wetness(16, 0, count_ref[0, col], mask_ref[0, col])
            up_ref[0:16, lanes] = jnp.where(wet, head_ref[:, lanes], 0.0)
            wet = wetness(16, ROWS - 16, count_ref[REGION - 1, col], mask_ref[REGION - 1, col])
            down_ref[0:16, lanes] = jnp.where(wet, tail_ref[:, lanes], 0.0)
        for extra in range(MOVE):
            edges(KEPT + extra, moved_ref[extra, 0:16, :], moved_ref[extra, 48:64, :])

    tiles = column_sum(tend_ref, thick_ref)
    for tile, value in enumerate(tiles):
        kept_ref[0, tile * 16 : tile * 16 + 16, :] = value
    edges(step, tiles[0], tiles[-1])


def gather_kernel(
    owner_ref, count_ref, mask_ref, depth_ref, kept_ref, moved_ref, one_ref, two_ref, three_ref,
    north_ref, south_ref,
    source_ref, masked_ref, left_ref, right_ref,
):
    row_index = lax.axis_index("by")
    myself = lax.axis_index("bx") * 8 + row_index
    end = OWN_ROWS + 8
    lane = lax.broadcasted_iota(jnp.int32, (8, LANES), 1)
    upper = lax.broadcasted_iota(jnp.int32, (8, LANES), 0) < 4

    not_south = row_index == 7
    not_north = row_index == 0
    for col in range(REGION):
        lanes = slice(col * LANES, (col + 1) * LANES)
        for row in range(REGION):
            rows = slice(row * ROWS, (row + 1) * ROWS)
            wet = wetness(ROWS, 0, count_ref[row, col], mask_ref[row, col])
            masked_ref[col, rows, :] = jnp.where(wet, depth_ref[rows, lanes], 0.0)
        south = [jnp.where(not_south, 0.0, south_ref[8 * i : 8 * i + 8, lanes]) for i in range(2)]
        north = [jnp.where(not_north, 0.0, north_ref[8 * i : 8 * i + 8, lanes]) for i in range(2)]
        masked_ref[col, OWN_ROWS:end, :] = south[0]
        masked_ref[col, end : end + 8, :] = jnp.where(upper, south[1], north[0])
        masked_ref[col, end + 8 : end + 16, :] = north[1]
        masked_ref[col, EXT_ROWS:PACK_ROWS, :] = jnp.zeros((8, LANES), jnp.float32)
        source_ref[col, 0:OWN_ROWS, :] = jnp.zeros((OWN_ROWS, LANES), jnp.float32)
        source_ref[col, OWN_ROWS:end, :] = south_ref[16:24, lanes]
        source_ref[col, end : end + 8, :] = jnp.where(
            upper, south_ref[24:32, lanes], north_ref[16:24, lanes]
        )
        source_ref[col, end + 8 : end + 16, :] = north_ref[24:32, lanes]
        source_ref[col, EXT_ROWS:PACK_ROWS, :] = jnp.zeros((8, LANES), jnp.float32)

    def spread(sender, slot, block, bottom, inside=True, above=True, below=True):
        region, row, col = place(owner_ref[sender * SLOTS + slot])
        if inside:

            @pl.when(region == myself)
            def _():
                first = pl.multiple_of(row * ROWS, ROWS)
                source_ref[col, pl.ds(first, ROWS), :] = block[...]

        if below:

            @pl.when((region == myself + 1) & (row == 0))
            def _():
                source_ref[col, OWN_ROWS:end, :] = block[0:8, :]
                mixed = source_ref[col, end : end + 8, :]
                source_ref[col, end : end + 8, :] = jnp.where(upper, block[8:16, :], mixed)

        if above:

            @pl.when((region == myself - 1) & (row == REGION - 1))
            def _():
                mixed = source_ref[col, end : end + 8, :]
                source_ref[col, end : end + 8, :] = jnp.where(upper, mixed, bottom[0:8, :])
                source_ref[col, end + 8 : end + 16, :] = bottom[8:16, :]

    for slot in range(KEPT):
        spread(myself, slot, kept_ref.at[slot], None, above=False, below=False)
    for extra in range(MOVE):
        slot = KEPT + extra
        block = moved_ref.at[extra]
        spread(myself, slot, block, None, above=False)
        block = one_ref.at[extra]
        spread((myself + 127) % 128, slot, block, None, above=False)
        block = two_ref.at[extra]
        spread((myself + 126) % 128, slot, block, block.at[48:64, :], below=False)
        spread((myself + 125) % 128, slot, None, three_ref.at[extra], inside=False, below=False)

    for col in range(REGION):
        for row in range(PACK_ROWS // 8):
            rows = slice(row * 8, row * 8 + 8)
            value = source_ref[col, rows, :]
            source_ref[col, rows, :] = jnp.where(masked_ref[col, rows, :] > 0.0, value, 0.0)

    for row in range(FOLD // 8):
        left = jnp.zeros((8, LANES), jnp.float32)
        right = jnp.zeros((8, LANES), jnp.float32)
        for group in range(4):
            rows = slice(group * FOLD + row * 8, group * FOLD + row * 8 + 8)
            for field, ref in enumerate((masked_ref, source_ref)):
                to = 32 * group + 16 * field
                here = (lane >= to) & (lane < to + 16)
                left = jnp.where(here, rolled(ref[0, rows, :], to, 1), left)
                right = jnp.where(here, rolled(ref[REGION - 1, rows, :], to + 16, 1), right)
        left_ref[row * 8 : row * 8 + 8, :] = left
        right_ref[row * 8 : row * 8 + 8, :] = right


def solve_kernel(
    owner_ref, source_ref, masked_ref, west_ref, east_ref,
    out_ref, one_ref, two_ref,
    side, direction, residual, total, corner, inverse, diagonal, standard,
):
    myself = lax.axis_index("bx") * 8 + lax.axis_index("by")
    lane = lax.broadcasted_iota(jnp.int32, (8, LANES), 1)
    first_lane, last_lane = lane == 0, lane == LANES - 1
    opening, scales = chebyshev_plan()

    for group in range(4):
        for row in range(FOLD // 8):
            rows = slice(row * 8, row * 8 + 8)
            west, east = west_ref[rows, :], east_ref[rows, :]
            for field in range(2):
                start = 32 * group + 16 * field
                value = jnp.where(lane < 16, rolled(east, -start, 1), 0.0)
                value = jnp.where(lane >= 112, rolled(west, 112 - start, 1), value)
                first = group * FOLD + row * 8
                side[field, first : first + 8, :] = value

    def strided(ref, field, k):
        rows = pl.ds(k, 8, stride=CHUNK)
        return [ref[col, rows, :] for col in range(REGION)] + [side[field, rows, :]]

    def from_west(row):
        turned = [rolled(value, 1, 1) for value in row]
        return [jnp.where(first_lane, turned[c - 1], turned[c]) for c in range(COLS)]

    def from_east(row):
        turned = [rolled(value, -1, 1) for value in row]
        return [jnp.where(last_lane, turned[(c + 1) % COLS], turned[c]) for c in range(COLS)]

    def join(f, *rows):
        return [f(*values) for values in zip(*rows)]

    def down(row):
        return [rolled(value, 1, 0) for value in row]

    def up(row):
        return [rolled(value, -1, 0) for value in row]

    def load(ref, k):
        return [ref[k, col] for col in range(COLS)]

    def store(ref, k, row):
        for col in range(COLS):
            ref[k, col] = row[col]

    def corner_depth(above, here):
        both = join(jnp.minimum, above, here)
        return join(jnp.minimum, both, from_west(both))

    def gathered(row):
        return join(jnp.add, row, from_east(row))

    here = strided(masked_ref, 1 - 1, 0)
    first_corner = corner_depth(down(strided(masked_ref, 0, CHUNK - 1)), here)
    below_last = up(first_corner)

    def prepare(k, carry):
        here, above_corner = carry
        following = strided(masked_ref, 0, jnp.minimum(k + 1, CHUNK - 1))
        under = corner_depth(here, following)
        last = k == CHUNK - 1
        under = join(lambda a, b: jnp.where(last, b, a), under, below_last)
        around = gathered(join(jnp.add, above_corner, under))
        source = strided(source_ref, 1, k)
        for col in range(COLS):
            inv = 1.0 / (surface_term + 0.75 * around[col])
            start = inv * source[col]
            inverse[k, col] = inv
            diagonal[k, col] = inv * (surface_term + around[col])
            corner[k, col] = 0.25 * above_corner[col]
            residual[k, col] = start
            direction[k, col] = opening * start
            total[k, col] = jnp.zeros((8, LANES), jnp.float32)
        return tuple(following), tuple(under)

    lax.fori_loop(0, CHUNK, prepare, (tuple(here), tuple(first_corner)))

    def flux(above, here, k):
        both = join(jnp.add, above, here)
        spread = join(jnp.add, both, from_west(both))
        return join(jnp.multiply, spread, load(corner, k))

    for sweep in range(ITERS - 1):
        carry_scale, forward_scale = scales[sweep]
        final = sweep == ITERS - 2
        first_row = load(direction, 0)
        first_flux = flux(down(load(direction, CHUNK - 1)), first_row, 0)
        below_last = up(first_flux)

        def advance(k, here, flux_above, following, flux_below):
            back = gathered(join(jnp.add, flux_above, flux_below))
            for col in range(COLS):
                rest = residual[k, col] - diagonal[k, col] * here[col] + inverse[k, col] * back[col]
                turned = carry_scale * here[col] + forward_scale * rest
                summed = total[k, col] + here[col]
                if final:
                    if col < REGION:
                        standard[col, pl.ds(k, 8, stride=CHUNK), :] = summed + turned
                else:
                    residual[k, col] = rest
                    direction[k, col] = turned
                    total[k, col] = summed

        def body(k, carry):
            here, flux_above = carry
            following = load(direction, k + 1)
            flux_below = flux(here, following, k + 1)
            advance(k, here, flux_above, following, flux_below)
            return tuple(following), tuple(flux_below)

        here, flux_above = lax.fori_loop(
            0, CHUNK - 1, body, (tuple(first_row), tuple(first_flux)), unroll=2
        )
        advance(CHUNK - 1, here, flux_above, None, below_last)

    def answer(sender, slot, ref, index):
        region, row, col = place(owner_ref[sender * SLOTS + slot])
        mine = region == myself
        first = pl.multiple_of(row * ROWS, ROWS)
        value = standard[col, pl.ds(first, ROWS), :]
        ref[index] = jnp.where(mine, value, 0.0)

    for extra in range(MOVE):
        answer((myself + 127) % 128, KEPT + extra, one_ref, extra)
        answer((myself + 126) % 128, KEPT + extra, two_ref, extra)
    for slot in range(SLOTS):
        answer(myself, slot, out_ref, slot)


def whole(space=VMEM):
    return pl.BlockSpec(memory_space=space)


def ring(value, steps):
    count = lax.axis_size("bx") * lax.axis_size("by")
    return lax.ppermute(value, ("bx", "by"), [(i, (i + steps) % count) for i in range(count)])


def along(value, axis, steps):
    count = lax.axis_size(axis)
    return lax.ppermute(value, axis, [(i, (i + steps) % count) for i in range(count)])


def on_device(tendency, thickness, depth, block_owner, block_mask, ocean_counts):
    f32 = jnp.float32

    def shape(*dims):
        return jax.ShapeDtypeStruct(dims, f32)

    moved, bottom = pl.pallas_call(
        moved_kernel,
        grid=(MOVE,),
        in_specs=[
            whole(SMEM),
            pl.BlockSpec((1, LEVELS, ROWS, LANES), lambda i: (KEPT + i, 0, 0, 0)),
        ],
        out_specs=[
            pl.BlockSpec((1, ROWS, LANES), lambda i: (i, 0, 0)),
            pl.BlockSpec((1, 16, LANES), lambda i: (i, 0, 0)),
        ],
        out_shape=[shape(MOVE, ROWS, LANES), shape(MOVE, 16, LANES)],
        name="moved_forcing",
    )(thickness, tendency)
    one, two, three = ring(moved, 1), ring(moved, 2), ring(bottom, 3)

    edge = pl.BlockSpec((16, REGION * LANES), lambda i: (0, 0))
    kept, upper, lower = pl.pallas_call(
        kept_kernel,
        grid=(KEPT,),
        in_specs=[
            whole(SMEM), whole(SMEM), whole(SMEM), whole(SMEM),
            pl.BlockSpec((1, LEVELS, ROWS, LANES), lambda i: (i, 0, 0, 0)),
            pl.BlockSpec((MOVE, ROWS, LANES), lambda i: (0, 0, 0)),
            edge,
            pl.BlockSpec((16, REGION * LANES), lambda i: (OWN_ROWS // 16 - 1, 0)),
        ],
        out_specs=[
            pl.BlockSpec((1, ROWS, LANES), lambda i: (i, 0, 0)),
            pl.BlockSpec((32, REGION * LANES), lambda i: (0, 0)),
            pl.BlockSpec((32, REGION * LANES), lambda i: (0, 0)),
        ],
        out_shape=[
            shape(KEPT, ROWS, LANES),
            shape(32, REGION * LANES),
            shape(32, REGION * LANES),
        ],
        name="kept_forcing",
    )(thickness, block_owner, ocean_counts, block_mask, tendency, moved, depth, depth)
    north = along(lower, "by", 1)
    south = along(upper, "by", -1)

    source, masked, left, right = pl.pallas_call(
        gather_kernel,
        in_specs=[whole(SMEM)] * 3 + [whole()] * 8,
        out_specs=[whole()] * 4,
        out_shape=[
            shape(REGION, PACK_ROWS, LANES),
            shape(REGION, PACK_ROWS, LANES),
            shape(FOLD, LANES),
            shape(FOLD, LANES),
        ],
        name="assemble",
    )(block_owner, ocean_counts, block_mask, depth, kept, moved, one, two, three, north, south)
    west = along(right, "bx", 1)
    east = along(left, "bx", -1)

    field = pltpu.VMEM((CHUNK, COLS, 8, LANES), f32)
    heights, first, second = pl.pallas_call(
        solve_kernel,
        in_specs=[whole(SMEM)] + [whole()] * 4,
        out_specs=[whole()] * 3,
        out_shape=[shape(SLOTS, ROWS, LANES), shape(MOVE, ROWS, LANES), shape(MOVE, ROWS, LANES)],
        scratch_shapes=[pltpu.VMEM((2, PACK_ROWS, LANES), f32)]
        + [field] * 6
        + [pltpu.VMEM((REGION, EXT_ROWS, LANES), f32)],
        compiler_params=pltpu.CompilerParams(vmem_limit_bytes=32 << 20),
        name="solve",
    )(block_owner, source, masked, west, east)
    back = ring(first, -1) + ring(second, -2)
    return heights.at[KEPT:].add(back)


def solution(mesh):
    placed = (
        P(("bx", "by"), None, None, None),
        P(),
        P("by", "bx"),
        P(),
        P("by", "bx"),
        P("by", "bx"),
    )
    return jax.shard_map(
        on_device,
        mesh=mesh,
        in_specs=placed,
        out_specs=P(("bx", "by"), None, None),
        check_vma=False,
    )
```

time: 174 us -> 79 us (0.45)
  starting transfers between devices: 94.3 us -> 17.2 us
  Pallas kernels: 0 us -> 46.7 us
  waiting for transfers between devices: 50.4 us -> 10.3 us
  other arithmetic: 23.6 us -> 1.48 us
    ppermute x44 -> x9, starting transfers between devices: 94.3 us -> 17.2 us  [the longest x5 11.9 us: ring(): lax.ppermute(value, ('bx', 'by'), [(i, (i + steps) % count) for i in rang...]
    pallas_call x0 -> x4, Pallas kernels: none -> 46.7 us  [the longest x1 33.7 us: on_device(): pl.pallas_call(solve_kernel, in_specs=[whole(SMEM)] + [whole()] * 4, out_...]
    ppermute x44 -> x9, waiting for transfers between devices: 50.4 us -> 10.3 us  [the longest x5 8.74 us: ring(): lax.ppermute(value, ('bx', 'by'), [(i, (i + steps) % count) for i in rang...]
    mul x12 -> x0, other arithmetic: 6.44 us -> none  [the longest x9 5.58 us: operate(): corner_depth * corner_mean]
    add x12 -> x0, other arithmetic: 5.54 us -> none  [the longest x8 4.34 us: on_device(): direction = carry_scale * direction + forward_scale * (inverse * residual)]
    reduce_sum x1 -> x0, other arithmetic: 5.39 us -> none  [on_device(): jnp.sum(tendency.astype(jnp.float32) * thickness[None, :, None, None], ax...]
    concatenate x9 -> x0, other arithmetic: 4.32 us -> none  [with_halo(): jnp.concatenate([lax.ppermute(tail, axis, [(i, (i + 1) % count) for i in...]
    unnamed x8 -> x18, local copies, waits for them, and re-layouts: 0.02 us -> 2.8 us
  transfers between devices with their start and end apart: 44 -> 9, of which waited for: 32 -> 4; matrix products, arithmetic and copies ran while one was open for 1% -> 0% of each run, Pallas kernels for 0% -> 10%
where the time goes in v1:
time: 79 us; the launch traced here: 78.5 us
  Pallas kernels  46.7 us (59%)
  starting transfers between devices  17.2 us (22%)
  waiting for transfers between devices  10.3 us (13%)
  local copies, waits for them, and re-layouts  2.8 us (4%)
  other arithmetic  1.48 us (2%)
    pallas_call x1, Pallas kernels, on_device(): pl.pallas_call(solve_kernel, in_specs=[whole(SMEM)] + [whole()] * 4, out_...  33.7 us
    ppermute x5, starting transfers between devices, ring(): lax.ppermute(value, ('bx', 'by'), [(i, (i + steps) % count) for i in rang...  11.9 us
    ppermute x5, waiting for transfers between devices, ring(): lax.ppermute(value, ('bx', 'by'), [(i, (i + steps) % count) for i in rang...  8.74 us
    pallas_call x1, Pallas kernels, on_device(): pl.pallas_call(kept_kernel, grid=(KEPT,), in_specs=[whole(SMEM), whole(SM...  7.97 us
    ppermute x4, starting transfers between devices, along(): lax.ppermute(value, axis, [(i, (i + steps) % count) for i in range(count)])  5.3 us
    pallas_call x1, Pallas kernels, on_device(): pl.pallas_call(gather_kernel, in_specs=[whole(SMEM)] * 3 + [whole()] * 8,...  2.96 us
    unnamed x18, local copies, waits for them, and re-layouts  2.8 us
    pallas_call x1, Pallas kernels, on_device(): pl.pallas_call(moved_kernel, grid=(MOVE,), in_specs=[whole(SMEM), pl.Bloc...  2.08 us
  transfers between devices with their start and end apart: 9, of which 4 were waited for; matrix products, arithmetic and copies ran while one was open for 0% of the time, Pallas kernels for 10%

profile of v1, /device:TPU:1, one launch (start us, length us, event | category | flops | bytes accessed | tf_op | source)
XLA Modules:
  0.0 78.5 jit_solution(5914622853106696461)
XLA Ops:
  0.0 0.0 copy-start.2
  0.0 2.1 %moved_forcing.1 = (f32[2,64,128]{2,1,0:T(8,128)}, f32[2,16,128]{2,1,0:T(8,128)}) custom-call(f32[40]{0:T(128)} %thick_ref.3, bf16[12,40,64,128]{3,2,1,0:T(8,128)(2,1)} %tend_ref.3), custom_call_target="tpu_custom_call" | custom-call | tf_op jit(solution)/shard_map/moved_forcing/pallas_call | solution.py:360
  2.1 0.0 copy-start.8
  2.1 2.5 %collective-permute-start.1 = (f32[2,64,128]{2,1,0:T(8,128)}, f32[2,64,128]{2,1,0:T(8,128)S(1)}, u32[]{:S(2)}, u32[]{:S(2)}) collective-permute-start(f32[2,64,128]{2,1,0:T(8,128)} %get-tuple-element.29.moved_ref), channel_id=1, source_target_pairs={{0,2},{1,3},{2,4},{3,5},{4,6},{5,7},{6,8},{7,9},{8,10},{9,11},{10,... | collective-permute-start | bytes 196616 | tf_op jit(solution)/shard_map/ppermute | solution.py:346
  4.6 2.5 %collective-permute-start = (f32[2,64,128]{2,1,0:T(8,128)}, f32[2,64,128]{2,1,0:T(8,128)S(1)}, u32[]{:S(2)}, u32[]{:S(2)}) collective-permute-start(f32[2,64,128]{2,1,0:T(8,128)} %get-tuple-element.29.moved_ref), channel_id=1, source_target_pairs={{0,1},{1,2},{2,3},{3,4},{4,5},{5,6},{6,7},{7,8},{8,9},{9,10},{10,1... | collective-permute-start | bytes 196616 | tf_op jit(solution)/shard_map/ppermute | solution.py:346
  7.0 8.0 %kept_forcing.1 = (f32[10,64,128]{2,1,0:T(8,128)}, f32[32,512]{1,0:T(8,128)}, f32[32,512]{1,0:T(8,128)}) custom-call(f32[40]{0:T(128)} %thick_ref.3, s32[1536]{0:T(1024)} %owner_ref.5, s32[4,4]{1,0:T(4,128)} %count_ref.3, s32[4,4]{1,0:T(4,128)} %mask_ref.3, bf16[12,40,64,128]{3,2,1,0:T(8,128)(2,1)} %tend_ref.3, f32[2,64,128]{2,1,0:T(8,128)} %get-tuple-element.29.moved_ref, ...), custom_call_target="tpu_custom_call" | custom-call | tf_op jit(solution)/shard_map/kept_forcing/pallas_call | solution.py:377
  15.0 0.0 collective-permute-start.3
  15.0 0.5 collective-permute-start.4
  15.5 0.0 copy-done.8
  15.5 2.9 %collective-permute-start.2 = (f32[2,16,128]{2,1,0:T(8,128)S(1)}, f32[2,16,128]{2,1,0:T(8,128)S(1)}, u32[]{:S(2)}, u32[]{:S(2)}) collective-permute-start(f32[2,16,128]{2,1,0:T(8,128)S(1)} %copy-done.8), channel_id=1, source_target_pairs={{0,3},{1,4},{2,5},{3,6},{4,7},{5,8},{6,9},{7,10},{8,11},{9,12},{10... | collective-permute-start | bytes 49160 | tf_op jit(solution)/shard_map/ppermute | solution.py:346
  18.4 5.7 %collective-permute-done.2.three_ref = f32[2,16,128]{2,1,0:T(8,128)S(1)} collective-permute-done((f32[2,16,128]{2,1,0:T(8,128)S(1)}, f32[2,16,128]{2,1,0:T(8,128)S(1)}, u32[]{:S(2)}, u32[]{:S(2)}) %collective-permute-start.2) | collective-permute-done | bytes 16416 | tf_op jit(solution)/shard_map/ppermute | solution.py:346
  24.1 0.0 copy-start.7
  24.1 0.0 collective-permute-done.1.two_ref
  24.1 0.0 copy-start.3
  24.1 0.0 collective-permute-done.one_ref
  24.1 0.0 copy-start.4
  24.1 0.0 collective-permute-done.3.north_ref
  24.1 0.0 copy-start.5
  24.2 0.0 collective-permute-done.4.south_ref
  24.2 0.0 copy-start.6
  24.2 0.5 copy-done.7
  24.7 0.0 copy-done.3
  24.7 0.0 copy-done.4
  24.8 0.0 copy-done.5
  24.8 0.0 copy-done.6
  24.8 3.0 %assemble.1 = (f32[4,288,128]{2,1,0:T(8,128)}, f32[4,288,128]{2,1,0:T(8,128)}, f32[72,128]{1,0:T(8,128)}, f32[72,128]{1,0:T(8,128)}) custom-call(s32[1536]{0:T(1024)} %owner_ref.5, s32[4,4]{1,0:T(4,128)} %count_ref.3, s32[4,4]{1,0:T(4,128)} %mask_ref.3, f32[256,512]{1,0:T(8,128)} %depth_ref.1, f32[10,64,128]{2,1,0:T(8,128)} %get-tuple-element.30.kept_ref, ...), custom_call_target="tpu_custom_call" | custom-call | tf_op jit(solution)/shard_map/assemble/pallas_call | solution.py:402
  27.8 0.0 collective-permute-start.5
  27.8 4.8 %collective-permute-start.6 = (f32[72,128]{1,0:T(8,128)}, f32[72,128]{1,0:T(8,128)S(1)}, u32[]{:S(2)}, u32[]{:S(2)}) collective-permute-start(f32[72,128]{1,0:T(8,128)} %get-tuple-element.37), channel_id=1, source_target_pairs={{0,120},{8,0},{16,8},{24,16},{32,24},{40,32},{48,40},{56,48},{64,5... | collective-permute-start | bytes 110600 | tf_op jit(solution)/shard_map/ppermute | solution.py:351
  32.6 1.6 %collective-permute-done.5.west_ref = f32[72,128]{1,0:T(8,128)S(1)} collective-permute-done((f32[72,128]{1,0:T(8,128)}, f32[72,128]{1,0:T(8,128)S(1)}, u32[]{:S(2)}, u32[]{:S(2)}) %collective-permute-start.5) | collective-permute-done | bytes 36896 | tf_op jit(solution)/shard_map/ppermute | solution.py:351
  34.1 0.0 collective-permute-done.6.east_ref
  34.1 0.0 copy-done.2
  34.1 0.0 copy-start
  34.1 1.1 %copy-done = f32[4,288,128]{2,1,0:T(8,128)S(1)} copy-done((f32[4,288,128]{2,1,0:T(8,128)S(1)}, f32[4,288,128]{2,1,0:T(8,128)}, u32[]{:S(2)}) %copy-start) | copy-done | bytes 589848
  35.2 0.0 copy-start.1
  35.2 1.1 %copy-done.1 = f32[4,288,128]{2,1,0:T(8,128)S(1)} copy-done((f32[4,288,128]{2,1,0:T(8,128)S(1)}, f32[4,288,128]{2,1,0:T(8,128)}, u32[]{:S(2)}) %copy-start.1) | copy-done | bytes 589848
  36.3 33.7 %solve.1 = (f32[12,64,128]{2,1,0:T(8,128)}, f32[2,64,128]{2,1,0:T(8,128)S(1)}, f32[2,64,128]{2,1,0:T(8,128)S(1)}) custom-call(s32[1536]{0:T(1024)S(1)} %copy-done.2, f32[4,288,128]{2,1,0:T(8,128)S(1)} %copy-done, f32[4,288,128]{2,1,0:T(8,128)S(1)} %copy-done.1, f32[72,128]{1,0:T(8,128)S(1)} %collective-permute-done.5.west_ref, ...), custom_call_target="tpu_custom_call" | custom-call | tf_op jit(solution)/shard_map/solve/pallas_call | solution.py:418
  69.9 3.4 %collective-permute-start.7 = (f32[2,64,128]{2,1,0:T(8,128)S(1)}, f32[2,64,128]{2,1,0:T(8,128)S(1)}, u32[]{:S(2)}, u32[]{:S(2)}) collective-permute-start(f32[2,64,128]{2,1,0:T(8,128)S(1)} %get-tuple-element.39), channel_id=1, source_target_pairs={{0,127},{1,0},{2,1},{3,2},{4,3},{5,4},{6,5},{7,6},{8,7},{9,8},{10,... | collective-permute-start | bytes 196616 | tf_op jit(solution)/shard_map/ppermute | solution.py:346
  73.3 0.7 collective-permute-start.8
  74.0 0.6 collective-permute-done.7
  74.6 2.5 %collective-permute-done.8 = f32[2,64,128]{2,1,0:T(8,128)S(1)} collective-permute-done((f32[2,64,128]{2,1,0:T(8,128)S(1)}, f32[2,64,128]{2,1,0:T(8,128)S(1)}, u32[]{:S(2)}, u32[]{:S(2)}) %collective-permute-start.8) | collective-permute-done | bytes 65568 | tf_op jit(solution)/shard_map/ppermute | solution.py:346
  77.1 1.5 %add_dynamic-update-slice_fusion = f32[12,64,128]{2,1,0:T(8,128)} fusion(f32[12,64,128]{2,1,0:T(8,128)} %get-tuple-element.38, f32[2,64,128]{2,1,0:T(8,128)S(1)} %collective-permute-done.7, f32[2,64,128]{2,1,0:T(8,128)S(1)} %collective-permute-done.8), kind=kLoop, calls=%fused_computation | loop fusion | flops 32768 | bytes 262144 | tf_op jit(solution)/shard_map/scatter-add | solution.py:430
Async XLA Ops:
  0.0 34.1 %copy-start.2 = (s32[1536]{0:T(1024)S(1)}, s32[1536]{0:T(1024)}, u32[]{:S(2)}) copy-start(s32[1536]{0:T(1024)} %owner_ref.5) | copy-start | bytes 18436
  2.1 13.4 %copy-start.8 = (f32[2,16,128]{2,1,0:T(8,128)S(1)}, f32[2,16,128]{2,1,0:T(8,128)}, u32[]{:S(2)}) copy-start(f32[2,16,128]{2,1,0:T(8,128)} %get-tuple-element.31) | copy-start | bytes 49156
  2.1 22.0 %collective-permute-start.1 = (f32[2,64,128]{2,1,0:T(8,128)}, f32[2,64,128]{2,1,0:T(8,128)S(1)}, u32[]{:S(2)}, u32[]{:S(2)}) collective-permute-start(f32[2,64,128]{2,1,0:T(8,128)} %get-tuple-element.29.moved_ref), channel_id=1, source_target_pairs={{0,2},{1,3},{2,4},{3,5},{4,6},{5,7},{6,8},{7,9},{8,10},{9,11},{10,... | collective-permute-start | bytes 196616 | tf_op jit(solution)/shard_map/ppermute | solution.py:346
  4.6 19.6 %collective-permute-start = (f32[2,64,128]{2,1,0:T(8,128)}, f32[2,64,128]{2,1,0:T(8,128)S(1)}, u32[]{:S(2)}, u32[]{:S(2)}) collective-permute-start(f32[2,64,128]{2,1,0:T(8,128)} %get-tuple-element.29.moved_ref), channel_id=1, source_target_pairs={{0,1},{1,2},{2,3},{3,4},{4,5},{5,6},{6,7},{7,8},{8,9},{9,10},{10,1... | collective-permute-start | bytes 196616 | tf_op jit(solution)/shard_map/ppermute | solution.py:346
  15.0 9.1 %collective-permute-start.3 = (f32[32,512]{1,0:T(8,128)}, f32[32,512]{1,0:T(8,128)S(1)}, u32[]{:S(2)}, u32[]{:S(2)}) collective-permute-start(f32[32,512]{1,0:T(8,128)} %get-tuple-element.32), channel_id=1, source_target_pairs={{0,1},{1,2},{2,3},{3,4},{4,5},{5,6},{6,7},{7,0},{8,9},{9,10},{10,1... | collective-permute-start | bytes 196616 | tf_op jit(solution)/shard_map/ppermute | solution.py:351
  15.0 9.1 %collective-permute-start.4 = (f32[32,512]{1,0:T(8,128)}, f32[32,512]{1,0:T(8,128)S(1)}, u32[]{:S(2)}, u32[]{:S(2)}) collective-permute-start(f32[32,512]{1,0:T(8,128)} %get-tuple-element.33), channel_id=1, source_target_pairs={{0,7},{1,0},{2,1},{3,2},{4,3},{5,4},{6,5},{7,6},{8,15},{9,8},{10,9... | collective-permute-start | bytes 196616 | tf_op jit(solution)/shard_map/ppermute | solution.py:351
  15.5 8.6 %collective-permute-start.2 = (f32[2,16,128]{2,1,0:T(8,128)S(1)}, f32[2,16,128]{2,1,0:T(8,128)S(1)}, u32[]{:S(2)}, u32[]{:S(2)}) collective-permute-start(f32[2,16,128]{2,1,0:T(8,128)S(1)} %copy-done.8), channel_id=1, source_target_pairs={{0,3},{1,4},{2,5},{3,6},{4,7},{5,8},{6,9},{7,10},{8,11},{9,12},{10... | collective-permute-start | bytes 49160 | tf_op jit(solution)/shard_map/ppermute | solution.py:346
  24.1 0.6 copy-start.7
  24.1 0.6 copy-start.3
  24.1 0.6 copy-start.4
  24.1 0.6 copy-start.5
  24.2 0.7 copy-start.6
  27.8 6.3 %collective-permute-start.5 = (f32[72,128]{1,0:T(8,128)}, f32[72,128]{1,0:T(8,128)S(1)}, u32[]{:S(2)}, u32[]{:S(2)}) collective-permute-start(f32[72,128]{1,0:T(8,128)} %get-tuple-element.36), channel_id=1, source_target_pairs={{0,8},{8,16},{16,24},{24,32},{32,40},{40,48},{48,56},{56,64},{64,7... | collective-permute-start | bytes 110600 | tf_op jit(solution)/shard_map/ppermute | solution.py:351
  27.8 6.3 %collective-permute-start.6 = (f32[72,128]{1,0:T(8,128)}, f32[72,128]{1,0:T(8,128)S(1)}, u32[]{:S(2)}, u32[]{:S(2)}) collective-permute-start(f32[72,128]{1,0:T(8,128)} %get-tuple-element.37), channel_id=1, source_target_pairs={{0,120},{8,0},{16,8},{24,16},{32,24},{40,32},{48,40},{56,48},{64,5... | collective-permute-start | bytes 110600 | tf_op jit(solution)/shard_map/ppermute | solution.py:351
  34.1 1.1 %copy-start = (f32[4,288,128]{2,1,0:T(8,128)S(1)}, f32[4,288,128]{2,1,0:T(8,128)}, u32[]{:S(2)}) copy-start(f32[4,288,128]{2,1,0:T(8,128)} %get-tuple-element.34.source_ref) | copy-start | bytes 1769476
  35.2 1.1 %copy-start.1 = (f32[4,288,128]{2,1,0:T(8,128)S(1)}, f32[4,288,128]{2,1,0:T(8,128)}, u32[]{:S(2)}) copy-start(f32[4,288,128]{2,1,0:T(8,128)} %get-tuple-element.35.masked_ref) | copy-start | bytes 1769476
  69.9 4.7 %collective-permute-start.7 = (f32[2,64,128]{2,1,0:T(8,128)S(1)}, f32[2,64,128]{2,1,0:T(8,128)S(1)}, u32[]{:S(2)}, u32[]{:S(2)}) collective-permute-start(f32[2,64,128]{2,1,0:T(8,128)S(1)} %get-tuple-element.39), channel_id=1, source_target_pairs={{0,127},{1,0},{2,1},{3,2},{4,3},{5,4},{6,5},{7,6},{8,7},{9,8},{10,... | collective-permute-start | bytes 196616 | tf_op jit(solution)/shard_map/ppermute | solution.py:346
  73.3 3.7 %collective-permute-start.8 = (f32[2,64,128]{2,1,0:T(8,128)S(1)}, f32[2,64,128]{2,1,0:T(8,128)S(1)}, u32[]{:S(2)}, u32[]{:S(2)}) collective-permute-start(f32[2,64,128]{2,1,0:T(8,128)S(1)} %get-tuple-element.40), channel_id=1, source_target_pairs={{0,126},{1,127},{2,0},{3,1},{4,2},{5,3},{6,4},{7,5},{8,6},{9,7},{1... | collective-permute-start | bytes 196616 | tf_op jit(solution)/shard_map/ppermute | solution.py:346

commit v2 on v1

v2 whole, which is shorter than its diff:
```python
import jax
import jax.numpy as jnp
from jax import lax
from jax.experimental import pallas as pl
from jax.experimental.pallas import tpu as pltpu
from jax.sharding import PartitionSpec as P

MOVE = 2
ITERS = 10
ROWS, LANES = 64, 128
SLOTS = 12
KEPT = SLOTS - MOVE
LEVELS = 40
REGION = 4
OWN_ROWS = REGION * ROWS
CHUNK = 35
EXT_ROWS = 8 * CHUNK
FOLD = 72
PACK_ROWS = 4 * FOLD
COLS = REGION + 1

surface_term = 0.1
lower_bound = 0.05
upper_bound = 2.0

VMEM = pltpu.MemorySpace.VMEM
SMEM = pltpu.MemorySpace.SMEM
HBM = pltpu.MemorySpace.HBM


def chebyshev_plan():
    centre_value = (upper_bound + lower_bound) / 2.0
    half_width = (upper_bound - lower_bound) / 2.0
    ratio_value = centre_value / half_width
    weight = 1.0 / ratio_value
    scales = []
    for sweep in range(ITERS):
        renewed = 1.0 / (2.0 * ratio_value - weight)
        scales.append((renewed * weight, 2.0 * renewed / half_width))
        weight = renewed
    return (1.0 / centre_value, scales)


def place(block):
    row, col = block // 64, block % 64
    return (col // REGION) * 8 + row // REGION, row % REGION, col % REGION


def rolled(value, steps, axis):
    return pltpu.roll(value, steps % value.shape[axis], axis)


def wetness(rows, count, mask):
    position = lax.broadcasted_iota(jnp.int32, (rows, LANES), 0) * LANES + (
        lax.broadcasted_iota(jnp.int32, (rows, LANES), 1)
    )
    return (position < count) & (mask == 1)


def forcing_kernel(
    thick_in, owner_in, count_in, mask_in, tend_ref, depth_ref,
    moved_ref, bottom_ref, up_ref, down_ref, source_ref, masked_ref,
    thick_ref, owner_ref, count_ref, mask_ref, levels, sea, table_sem, level_sem, sea_sem,
):
    myself = lax.axis_index("bx") * 8 + lax.axis_index("by")
    tables = []
    for index, (table_in, table_ref) in enumerate(
        ((count_in, count_ref), (mask_in, mask_ref), (thick_in, thick_ref), (owner_in, owner_ref))
    ):
        copy = pltpu.make_async_copy(table_in, table_ref, table_sem.at[index])
        copy.start()
        tables.append(copy)
    sea_copy = pltpu.make_async_copy(depth_ref, sea, sea_sem)
    sea_copy.start()
    copies = []
    for slot in range(SLOTS):
        copy = pltpu.make_async_copy(tend_ref.at[slot], levels.at[slot], level_sem.at[slot])
        copy.start()
        copies.append(copy)

    width = REGION * LANES
    up_ref[16:32, :] = jnp.zeros((16, width), jnp.float32)
    down_ref[16:32, :] = jnp.zeros((16, width), jnp.float32)
    source_ref[...] = jnp.zeros(source_ref.shape, jnp.float32)
    for copy in tables:
        copy.wait()
    sea_copy.wait()
    for col in range(REGION):
        lanes = slice(col * LANES, (col + 1) * LANES)
        for row in range(REGION):
            rows = slice(row * ROWS, (row + 1) * ROWS)
            wet = wetness(ROWS, count_ref[row, col], mask_ref[row, col])
            value = jnp.where(wet, sea[rows, lanes], 0.0)
            masked_ref[col, rows, :] = value
            if row == 0:
                up_ref[0:16, lanes] = value[0:16, :]
            if row == REGION - 1:
                down_ref[0:16, lanes] = value[48:64, :]
        masked_ref[col, OWN_ROWS:PACK_ROWS, :] = jnp.zeros((PACK_ROWS - OWN_ROWS, LANES), jnp.float32)

    for slot in range(SLOTS):
        copies[slot].wait()
        totals = [jnp.zeros((16, LANES), jnp.float32) for _ in range(ROWS // 16)]
        for level in range(LEVELS):
            weight = thick_ref[level]
            for tile in range(ROWS // 16):
                part = levels[slot, level, tile * 16 : tile * 16 + 16, :].astype(jnp.float32)
                totals[tile] = totals[tile] + part * weight
        if slot >= KEPT:
            for tile, value in enumerate(totals):
                moved_ref[slot - KEPT, tile * 16 : tile * 16 + 16, :] = value
            bottom_ref[slot - KEPT] = totals[-1]
        region, row, col = place(owner_ref[myself * SLOTS + slot])
        lanes = pl.ds(pl.multiple_of(col * LANES, LANES), LANES)

        @pl.when(region == myself)
        def _():
            for tile, value in enumerate(totals):
                first = pl.multiple_of(row * ROWS + tile * 16, 16)
                source_ref[col, pl.ds(first, 16), :] = value

        @pl.when((region == myself) & (row == 0))
        def _():
            up_ref[16:32, lanes] = totals[0]

        @pl.when((region == myself) & (row == REGION - 1))
        def _():
            down_ref[16:32, lanes] = totals[-1]


def gather_kernel(
    owner_ref, source_in, masked_in, moved_ref, one_ref, two_ref, three_ref, north_ref, south_ref,
    source_ref, masked_ref, left_ref, right_ref,
):
    del source_in, masked_in
    row_index = lax.axis_index("by")
    myself = lax.axis_index("bx") * 8 + row_index
    end = OWN_ROWS + 8
    lane = lax.broadcasted_iota(jnp.int32, (8, LANES), 1)
    upper = lax.broadcasted_iota(jnp.int32, (8, LANES), 0) < 4

    not_south = row_index == 7
    not_north = row_index == 0
    for col in range(REGION):
        lanes = slice(col * LANES, (col + 1) * LANES)
        south = [jnp.where(not_south, 0.0, south_ref[8 * i : 8 * i + 8, lanes]) for i in range(2)]
        north = [jnp.where(not_north, 0.0, north_ref[8 * i : 8 * i + 8, lanes]) for i in range(2)]
        masked_ref[col, OWN_ROWS:end, :] = south[0]
        masked_ref[col, end : end + 8, :] = jnp.where(upper, south[1], north[0])
        masked_ref[col, end + 8 : end + 16, :] = north[1]
        source_ref[col, OWN_ROWS:end, :] = south_ref[16:24, lanes]
        source_ref[col, end : end + 8, :] = jnp.where(
            upper, south_ref[24:32, lanes], north_ref[16:24, lanes]
        )
        source_ref[col, end + 8 : end + 16, :] = north_ref[24:32, lanes]

    def spread(sender, slot, block, bottom, inside=True, above=True, below=True):
        region, row, col = place(owner_ref[sender * SLOTS + slot])
        if inside:

            @pl.when(region == myself)
            def _():
                first = pl.multiple_of(row * ROWS, ROWS)
                source_ref[col, pl.ds(first, ROWS), :] = block[...]

        if below:

            @pl.when((region == myself + 1) & (row == 0))
            def _():
                source_ref[col, OWN_ROWS:end, :] = block[0:8, :]
                mixed = source_ref[col, end : end + 8, :]
                source_ref[col, end : end + 8, :] = jnp.where(upper, block[8:16, :], mixed)

        if above:

            @pl.when((region == myself - 1) & (row == REGION - 1))
            def _():
                mixed = source_ref[col, end : end + 8, :]
                source_ref[col, end : end + 8, :] = jnp.where(upper, mixed, bottom[0:8, :])
                source_ref[col, end + 8 : end + 16, :] = bottom[8:16, :]

    for extra in range(MOVE):
        slot = KEPT + extra
        block = moved_ref.at[extra]
        spread(myself, slot, block, None, inside=False, above=False)
        block = one_ref.at[extra]
        spread((myself + 127) % 128, slot, block, None, above=False)
        block = two_ref.at[extra]
        spread((myself + 126) % 128, slot, block, block.at[48:64, :], below=False)
        spread((myself + 125) % 128, slot, None, three_ref.at[extra], inside=False, below=False)

    for row in range(FOLD // 8):
        left = jnp.zeros((8, LANES), jnp.float32)
        right = jnp.zeros((8, LANES), jnp.float32)
        for group in range(4):
            rows = slice(group * FOLD + row * 8, group * FOLD + row * 8 + 8)
            for field, ref in enumerate((masked_ref, source_ref)):
                to = 32 * group + 16 * field
                here = (lane >= to) & (lane < to + 16)
                left = jnp.where(here, rolled(ref[0, rows, :], to, 1), left)
                right = jnp.where(here, rolled(ref[REGION - 1, rows, :], to + 16, 1), right)
        left_ref[row * 8 : row * 8 + 8, :] = left
        right_ref[row * 8 : row * 8 + 8, :] = right


def solve_kernel(
    owner_ref, scale_ref, source_ref, masked_ref, west_ref, east_ref,
    standard, one_ref, two_ref,
    side, direction, residual, total, corner, inverse, diagonal, flow,
):
    myself = lax.axis_index("bx") * 8 + lax.axis_index("by")
    lane = lax.broadcasted_iota(jnp.int32, (8, LANES), 1)
    first_lane, last_lane = lane == 0, lane == LANES - 1
    opening, _ = chebyshev_plan()

    for group in range(4):
        for row in range(FOLD // 8):
            rows = slice(row * 8, row * 8 + 8)
            west, east = west_ref[rows, :], east_ref[rows, :]
            for field in range(2):
                start = 32 * group + 16 * field
                value = jnp.where(lane < 16, rolled(east, -start, 1), 0.0)
                value = jnp.where(lane >= 112, rolled(west, 112 - start, 1), value)
                first = group * FOLD + row * 8
                side[field, first : first + 8, :] = value

    def strided(ref, field, k):
        rows = pl.ds(k, 8, stride=CHUNK)
        return [ref[col, rows, :] for col in range(REGION)] + [side[field, rows, :]]

    def from_west(row):
        turned = [rolled(value, 1, 1) for value in row]
        return [jnp.where(first_lane, turned[c - 1], turned[c]) for c in range(COLS)]

    def from_east(row):
        turned = [rolled(value, -1, 1) for value in row]
        return [jnp.where(last_lane, turned[(c + 1) % COLS], turned[c]) for c in range(COLS)]

    def join(f, *rows):
        return [f(*values) for values in zip(*rows)]

    def down(row):
        return [rolled(value, 1, 0) for value in row]

    def up(row):
        return [rolled(value, -1, 0) for value in row]

    def load(ref, k):
        return [ref[k, col] for col in range(COLS)]

    def store(ref, k, row):
        for col in range(COLS):
            ref[k, col] = row[col]

    def corner_depth(above, here):
        both = join(jnp.minimum, above, here)
        return join(jnp.minimum, both, from_west(both))

    def gathered(row):
        return join(jnp.add, row, from_east(row))

    above = down(strided(masked_ref, 0, CHUNK - 1))
    for k in range(CHUNK):
        here = strided(masked_ref, 0, k)
        store(corner, k, corner_depth(above, here))
        above = here
    for k in range(CHUNK):
        under = load(corner, k + 1) if k + 1 < CHUNK else up(load(corner, 0))
        around = gathered(join(jnp.add, load(corner, k), under))
        source, masked = strided(source_ref, 1, k), strided(masked_ref, 0, k)
        for col in range(COLS):
            inv = 1.0 / (surface_term + 0.75 * around[col])
            start = inv * jnp.where(masked[col] > 0.0, source[col], 0.0)
            inverse[k, col] = 0.25 * inv
            diagonal[k, col] = inv * (surface_term + around[col])
            residual[k, col] = start
            direction[k, col] = opening * start
            total[k, col] = opening * start

    def sweep(index, final):
        carry_scale, forward_scale = scale_ref[index, 0], scale_ref[index, 1]
        above = down(load(direction, CHUNK - 1))
        for k in range(CHUNK):
            here = load(direction, k)
            both = join(jnp.add, above, here)
            spread = join(jnp.add, both, from_west(both))
            store(flow, k, join(jnp.multiply, spread, load(corner, k)))
            above = here
        for k in range(CHUNK):
            under = load(flow, k + 1) if k + 1 < CHUNK else up(load(flow, 0))
            back = gathered(join(jnp.add, load(flow, k), under))
            for col in range(REGION if final else COLS):
                here = direction[k, col]
                rest = residual[k, col] - diagonal[k, col] * here + inverse[k, col] * back[col]
                turned = carry_scale * here + forward_scale * rest
                summed = total[k, col] + turned
                if final:
                    standard[col, pl.ds(k, 8, stride=CHUNK), :] = summed
                else:
                    residual[k, col] = rest
                    direction[k, col] = turned
                    total[k, col] = summed

    lax.fori_loop(0, ITERS - 2, lambda index, _: sweep(index, False), None)
    sweep(ITERS - 2, True)

    for extra in range(MOVE):
        block_of(myself, (myself + 127) % 128, KEPT + extra, owner_ref, standard, one_ref, extra)
        block_of(myself, (myself + 126) % 128, KEPT + extra, owner_ref, standard, two_ref, extra)


def block_of(myself, sender, slot, owner_ref, standard, ref, index):
    region, row, col = place(owner_ref[sender * SLOTS + slot])
    first = pl.multiple_of(row * ROWS, ROWS)
    value = standard[col, pl.ds(first, ROWS), :]
    ref[index] = jnp.where(region == myself, value, 0.0)


def write_kernel(owner_ref, standard, out_ref, tail_ref):
    myself = lax.axis_index("bx") * 8 + lax.axis_index("by")
    for slot in range(SLOTS):
        block_of(myself, myself, slot, owner_ref, standard, out_ref, slot)
    for extra in range(MOVE):
        tail_ref[extra] = out_ref[KEPT + extra]


def tail_kernel(heights_ref, tail_ref, one_ref, two_ref, out_ref, joined, sem):
    del heights_ref
    joined[...] = tail_ref[...] + (one_ref[...] + two_ref[...])
    copy = pltpu.make_async_copy(joined, out_ref.at[pl.ds(KEPT, MOVE)], sem)
    copy.start()
    copy.wait()


def whole(space=VMEM):
    return pl.BlockSpec(memory_space=space)


def ring(value, steps):
    count = lax.axis_size("bx") * lax.axis_size("by")
    return lax.ppermute(value, ("bx", "by"), [(i, (i + steps) % count) for i in range(count)])


def along(value, axis, steps):
    count = lax.axis_size(axis)
    return lax.ppermute(value, axis, [(i, (i + steps) % count) for i in range(count)])


def near(value):
    return pltpu.with_memory_space_constraint(value, VMEM)


def distant(value):
    return pltpu.with_memory_space_constraint(value, HBM)


def on_device(tendency, thickness, depth, block_owner, block_mask, ocean_counts):
    f32 = jnp.float32
    params = pltpu.CompilerParams(vmem_limit_bytes=32 << 20)
    far = pl.BlockSpec(memory_space=HBM)

    def here(*dims):
        return pltpu.VMEM(dims, f32)

    field = (REGION, PACK_ROWS, LANES)
    moved, bottom, upper, lower, source, masked = pl.pallas_call(
        forcing_kernel,
        in_specs=[far] * 6,
        out_specs=[whole()] * 6,
        out_shape=[
            here(MOVE, ROWS, LANES),
            here(MOVE, 16, LANES),
            here(32, REGION * LANES),
            here(32, REGION * LANES),
            here(*field),
            here(*field),
        ],
        scratch_shapes=[
            pltpu.SMEM(thickness.shape, f32),
            pltpu.SMEM(block_owner.shape, jnp.int32),
            pltpu.SMEM(ocean_counts.shape, jnp.int32),
            pltpu.SMEM(block_mask.shape, jnp.int32),
            pltpu.VMEM((SLOTS, LEVELS, ROWS, LANES), jnp.bfloat16),
            pltpu.VMEM((OWN_ROWS, REGION * LANES), f32),
            pltpu.SemaphoreType.DMA((4,)),
            pltpu.SemaphoreType.DMA((SLOTS,)),
            pltpu.SemaphoreType.DMA,
        ],
        compiler_params=params,
        name="forcing",
    )(*map(distant, (thickness, block_owner, ocean_counts, block_mask, tendency, depth)))
    one, two, three = ring(moved, 1), ring(moved, 2), ring(bottom, 3)
    north = along(lower, "by", 1)
    south = along(upper, "by", -1)

    inputs = [near(x) for x in (source, masked, moved, one, two, three, north, south)]
    source, masked, left, right = pl.pallas_call(
        gather_kernel,
        in_specs=[whole(SMEM)] + [whole()] * 8,
        out_specs=[whole()] * 4,
        out_shape=[here(*field), here(*field), here(FOLD, LANES), here(FOLD, LANES)],
        input_output_aliases={1: 0, 2: 1},
        compiler_params=params,
        name="assemble",
    )(block_owner, *inputs)
    west = along(right, "bx", 1)
    east = along(left, "bx", -1)

    scales = jnp.asarray(chebyshev_plan()[1], f32)
    inputs = [near(x) for x in (source, masked, west, east)]
    heights, first, second = pl.pallas_call(
        solve_kernel,
        in_specs=[whole(SMEM)] * 2 + [whole()] * 4,
        out_specs=[whole()] * 3,
        out_shape=[
            here(REGION, EXT_ROWS, LANES),
            here(MOVE, ROWS, LANES),
            here(MOVE, ROWS, LANES),
        ],
        scratch_shapes=[pltpu.VMEM((2, PACK_ROWS, LANES), f32)]
        + [pltpu.VMEM((CHUNK, COLS, 8, LANES), f32)] * 7,
        compiler_params=params,
        name="solve",
    )(block_owner, scales, *inputs)
    back = ring(first, -1), ring(second, -2)

    out, tail = pl.pallas_call(
        write_kernel,
        in_specs=[whole(SMEM), whole()],
        out_specs=[whole()] * 2,
        out_shape=[jax.ShapeDtypeStruct((SLOTS, ROWS, LANES), f32), here(MOVE, ROWS, LANES)],
        compiler_params=params,
        name="write",
    )(block_owner, near(heights))
    return pl.pallas_call(
        tail_kernel,
        in_specs=[far] + [whole()] * 3,
        out_specs=far,
        out_shape=jax.ShapeDtypeStruct((SLOTS, ROWS, LANES), f32),
        input_output_aliases={0: 0},
        scratch_shapes=[here(MOVE, ROWS, LANES), pltpu.SemaphoreType.DMA],
        compiler_params=params,
        name="tail",
    )(out, near(tail), near(back[0]), near(back[1]))


def solution(mesh):
    placed = (
        P(("bx", "by"), None, None, None),
        P(),
        P("by", "bx"),
        P(),
        P("by", "bx"),
        P("by", "bx"),
    )
    return jax.shard_map(
        on_device,
        mesh=mesh,
        in_specs=placed,
        out_specs=P(("bx", "by"), None, None),
        check_vma=False,
    )
```

time: 79 us -> 41 us (0.52)
  Pallas kernels: 46.7 us -> 15 us
  local copies, waits for them, and re-layouts: 2.8 us -> 0.01 us
  waiting for transfers between devices: 10.3 us -> 8.72 us
  other arithmetic: 1.48 us -> 0 us
    pallas_call x4 -> x5, Pallas kernels: 46.7 us -> 15 us  [the longest x1 6.46 us: on_device(): pl.pallas_call(solve_kernel, in_specs=[whole(SMEM)] * 2 + [whole()] * 4,...]
    unnamed x18 -> x4, local copies, waits for them, and re-layouts: 2.8 us -> 0.01 us
    ppermute x5, starting transfers between devices: 11.9 us -> 9.27 us  [ring(): lax.ppermute(value, ('bx', 'by'), [(i, (i + steps) % count) for i in rang...]
    ppermute x4, starting transfers between devices: 5.3 us -> 7.89 us  [along(): lax.ppermute(value, axis, [(i, (i + steps) % count) for i in range(count)])]
    ppermute x5, waiting for transfers between devices: 8.74 us -> 6.93 us  [ring(): lax.ppermute(value, ('bx', 'by'), [(i, (i + steps) % count) for i in rang...]
    scatter-add x1 -> x0, other arithmetic: 1.48 us -> none  [on_device(): return heights.at[KEPT:].add(back)]
  transfers between devices with their start and end apart: 9 -> 9, of which waited for: 4 -> 2; matrix products, arithmetic and copies ran while one was open for 0% -> 0% of each run, Pallas kernels for 10% -> 4%
where the time goes in v2:
time: 41 us; the launch traced here: 40.9 us
  starting transfers between devices  17.2 us (42%)
  Pallas kernels  15 us (37%)
  waiting for transfers between devices  8.72 us (21%)
    ppermute x5, starting transfers between devices, ring(): lax.ppermute(value, ('bx', 'by'), [(i, (i + steps) % count) for i in rang...  9.27 us
    ppermute x4, starting transfers between devices, along(): lax.ppermute(value, axis, [(i, (i + steps) % count) for i in range(count)])  7.89 us
    ppermute x5, waiting for transfers between devices, ring(): lax.ppermute(value, ('bx', 'by'), [(i, (i + steps) % count) for i in rang...  6.93 us
    pallas_call x1, Pallas kernels, on_device(): pl.pallas_call(solve_kernel, in_specs=[whole(SMEM)] * 2 + [whole()] * 4,...  6.46 us
    pallas_call x1, Pallas kernels, on_device(): pl.pallas_call(forcing_kernel, in_specs=[far] * 6, out_specs=[whole()] *...  5.17 us
    ppermute x4, waiting for transfers between devices, along(): lax.ppermute(value, axis, [(i, (i + steps) % count) for i in range(count)])  1.78 us
    pallas_call x1, Pallas kernels, on_device(): pl.pallas_call(write_kernel, in_specs=[whole(SMEM), whole()], out_specs=[...  1.61 us
    pallas_call x1, Pallas kernels, on_device(): pl.pallas_call(gather_kernel, in_specs=[whole(SMEM)] + [whole()] * 8, out...  1.09 us
  transfers between devices with their start and end apart: 9, of which 2 were waited for; matrix products, arithmetic and copies ran while one was open for 0% of the time, Pallas kernels for 4%

profile of v2, /device:TPU:1, one launch (start us, length us, event | category | flops | bytes accessed | tf_op | source)
XLA Modules:
  0.0 40.9 jit_solution(8425068559205331206)
XLA Ops:
  0.0 0.0 copy-start.1
  0.0 0.0 copy-start
  0.0 5.2 %forcing.1 = (f32[2,64,128]{2,1,0:T(8,128)S(1)}, f32[2,16,128]{2,1,0:T(8,128)S(1)}, f32[32,512]{1,0:T(8,128)S(1)}, f32[32,512]{1,0:T(8,128)S(1)}, f32[4,288,128]...) custom-call(f32[40]{0:T(128)} %thick_in.1, s32[1536]{0:T(1024)} %owner_ref.5, s32[4,4]{1,0:T(4,128)} %count_in.1, ...), custom_call_target="tpu_custom_call" | custom-call | tf_op jit(solution)/shard_map/forcing/pallas_call | solution.py:366
  5.2 3.0 %collective-permute-start.3 = (f32[32,512]{1,0:T(8,128)S(1)}, f32[32,512]{1,0:T(8,128)S(1)}, u32[]{:S(2)}, u32[]{:S(2)}) collective-permute-start(f32[32,512]{1,0:T(8,128)S(1)} %get-tuple-element.24), channel_id=1, source_target_pairs={{0,1},{1,2},{2,3},{3,4},{4,5},{5,6},{6,7},{7,0},{8,9},{9,10},{10,1... | collective-permute-start | bytes 196616 | tf_op jit(solution)/shard_map/ppermute | solution.py:346
  8.2 0.0 collective-permute-start.4
  8.2 1.6 %collective-permute-start.1 = (f32[2,64,128]{2,1,0:T(8,128)S(1)}, f32[2,64,128]{2,1,0:T(8,128)S(1)}, u32[]{:S(2)}, u32[]{:S(2)}) collective-permute-start(f32[2,64,128]{2,1,0:T(8,128)S(1)} %get-tuple-element.22.moved_ref), channel_id=1, source_target_pairs={{0,2},{1,3},{2,4},{3,5},{4,6},{5,7},{6,8},{7,9},{8,10},{9,11},{10,... | collective-permute-start | bytes 196616 | tf_op jit(solution)/shard_map/ppermute | solution.py:341
  9.9 2.0 %collective-permute-start = (f32[2,64,128]{2,1,0:T(8,128)S(1)}, f32[2,64,128]{2,1,0:T(8,128)S(1)}, u32[]{:S(2)}, u32[]{:S(2)}) collective-permute-start(f32[2,64,128]{2,1,0:T(8,128)S(1)} %get-tuple-element.22.moved_ref), channel_id=1, source_target_pairs={{0,1},{1,2},{2,3},{3,4},{4,5},{5,6},{6,7},{7,8},{8,9},{9,10},{10,1... | collective-permute-start | bytes 196616 | tf_op jit(solution)/shard_map/ppermute | solution.py:341
  11.9 1.7 %collective-permute-start.2 = (f32[2,16,128]{2,1,0:T(8,128)S(1)}, f32[2,16,128]{2,1,0:T(8,128)S(1)}, u32[]{:S(2)}, u32[]{:S(2)}) collective-permute-start(f32[2,16,128]{2,1,0:T(8,128)S(1)} %get-tuple-element.23), channel_id=1, source_target_pairs={{0,3},{1,4},{2,5},{3,6},{4,7},{5,8},{6,9},{7,10},{8,11},{9,12},{10... | collective-permute-start | bytes 49160 | tf_op jit(solution)/shard_map/ppermute | solution.py:341
  13.6 6.9 %collective-permute-done.2.three_ref = f32[2,16,128]{2,1,0:T(8,128)S(1)} collective-permute-done((f32[2,16,128]{2,1,0:T(8,128)S(1)}, f32[2,16,128]{2,1,0:T(8,128)S(1)}, u32[]{:S(2)}, u32[]{:S(2)}) %collective-permute-start.2) | collective-permute-done | bytes 16416 | tf_op jit(solution)/shard_map/ppermute | solution.py:341
  20.5 0.0 collective-permute-done.3.north_ref
  20.5 0.0 collective-permute-done.4.south_ref
  20.5 0.0 collective-permute-done.1.two_ref
  20.5 0.0 collective-permute-done.one_ref
  20.5 0.0 copy-done
  20.5 1.1 %assemble.1 = (f32[4,288,128]{2,1,0:T(8,128)S(1)}, f32[4,288,128]{2,1,0:T(8,128)S(1)}, f32[72,128]{1,0:T(8,128)S(1)}, f32[72,128]{1,0:T(8,128)S(1)}) custom-call(s32[1536]{0:T(1024)S(1)} %copy-done, f32[4,288,128]{2,1,0:T(8,128)S(1)} %get-tuple-element.20.source_in, ...), custom_call_target="tpu_custom_call", output_to_operand_aliasing={{0}: (1, {}), {1}: (2, {})} | custom-call | tf_op jit(solution)/shard_map/assemble/pallas_call | solution.py:397
  21.6 0.1 collective-permute-start.5
  21.7 4.8 %collective-permute-start.6 = (f32[72,128]{1,0:T(8,128)S(1)}, f32[72,128]{1,0:T(8,128)S(1)}, u32[]{:S(2)}, u32[]{:S(2)}) collective-permute-start(f32[72,128]{1,0:T(8,128)S(1)} %get-tuple-element.29), channel_id=1, source_target_pairs={{0,120},{8,0},{16,8},{24,16},{32,24},{40,32},{48,40},{56,48},{64,5... | collective-permute-start | bytes 110600 | tf_op jit(solution)/shard_map/ppermute | solution.py:346
  26.5 1.8 %collective-permute-done.5.west_ref = f32[72,128]{1,0:T(8,128)S(1)} collective-permute-done((f32[72,128]{1,0:T(8,128)S(1)}, f32[72,128]{1,0:T(8,128)S(1)}, u32[]{:S(2)}, u32[]{:S(2)}) %collective-permute-start.5) | collective-permute-done | bytes 36896 | tf_op jit(solution)/shard_map/ppermute | solution.py:346
  28.2 0.0 collective-permute-done.6.east_ref
  28.2 0.0 copy-done.1
  28.3 6.5 %solve.1 = (f32[4,280,128]{2,1,0:T(8,128)S(1)}, f32[2,64,128]{2,1,0:T(8,128)S(1)}, f32[2,64,128]{2,1,0:T(8,128)S(1)}) custom-call(s32[1536]{0:T(1024)S(1)} %copy-done, f32[10,2]{1,0:T(8,128)S(1)} %copy-done.1, f32[4,288,128]{2,1,0:T(8,128)S(1)} %get-tuple-element.26.source_ref, f32[4,288,128]{2,1,0:T(8,128)S(1)} %get-tuple-element.27.masked_ref, ...), custom_call_target="tpu_custom_call" | custom-call | tf_op jit(solution)/shard_map/solve/pallas_call | solution.py:411
  34.7 0.7 %collective-permute-start.7 = (f32[2,64,128]{2,1,0:T(8,128)S(1)}, f32[2,64,128]{2,1,0:T(8,128)S(1)}, u32[]{:S(2)}, u32[]{:S(2)}) collective-permute-start(f32[2,64,128]{2,1,0:T(8,128)S(1)} %get-tuple-element.33), channel_id=1, source_target_pairs={{0,127},{1,0},{2,1},{3,2},{4,3},{5,4},{6,5},{7,6},{8,7},{9,8},{10,... | collective-permute-start | bytes 196616 | tf_op jit(solution)/shard_map/ppermute | solution.py:341
  35.4 3.2 %collective-permute-start.8 = (f32[2,64,128]{2,1,0:T(8,128)S(1)}, f32[2,64,128]{2,1,0:T(8,128)S(1)}, u32[]{:S(2)}, u32[]{:S(2)}) collective-permute-start(f32[2,64,128]{2,1,0:T(8,128)S(1)} %get-tuple-element.34), channel_id=1, source_target_pairs={{0,126},{1,127},{2,0},{3,1},{4,2},{5,3},{6,4},{7,5},{8,6},{9,7},{1... | collective-permute-start | bytes 196616 | tf_op jit(solution)/shard_map/ppermute | solution.py:341
  38.7 1.6 %write.1 = (f32[12,64,128]{2,1,0:T(8,128)}, f32[2,64,128]{2,1,0:T(8,128)S(1)}) custom-call(s32[1536]{0:T(1024)S(1)} %copy-done, f32[4,280,128]{2,1,0:T(8,128)S(1)} %get-tuple-element.30.standard), custom_call_target="tpu_custom_call" | custom-call | tf_op jit(solution)/shard_map/write/pallas_call | solution.py:427
  40.3 0.0 collective-permute-done.7.one_ref
  40.3 0.0 collective-permute-done.8.two_ref
  40.3 0.7 %tail.1 = f32[12,64,128]{2,1,0:T(8,128)} custom-call(f32[12,64,128]{2,1,0:T(8,128)} %get-tuple-element.31.heights_ref, f32[2,64,128]{2,1,0:T(8,128)S(1)} %get-tuple-element.32.tail_ref, f32[2,64,128]{2,1,0:T(8,128)S(1)} %collective-permute-done.7.one_ref, f32[2,64,128]{2,1,0:T(8,128)S(1)} %collective-permute-done.8.two_ref), custom_call_target="tpu_custom_call", output_to_operand_aliasing={{}: (0, {})} | custom-call | tf_op jit(solution)/shard_map/tail/pallas_call | solution.py:435
Async XLA Ops:
  0.0 28.3 %copy-start.1 = (f32[10,2]{1,0:T(8,128)S(1)}, f32[10,2]{1,0:T(8,128)}, u32[]{:S(2)}) copy-start(f32[10,2]{1,0:T(8,128)} %constant.2.clone.scale_ref) | copy-start | bytes 244
  0.0 20.5 %copy-start = (s32[1536]{0:T(1024)S(1)}, s32[1536]{0:T(1024)}, u32[]{:S(2)}) copy-start(s32[1536]{0:T(1024)} %owner_ref.5) | copy-start | bytes 18436
  5.2 15.3 %collective-permute-start.3 = (f32[32,512]{1,0:T(8,128)S(1)}, f32[32,512]{1,0:T(8,128)S(1)}, u32[]{:S(2)}, u32[]{:S(2)}) collective-permute-start(f32[32,512]{1,0:T(8,128)S(1)} %get-tuple-element.24), channel_id=1, source_target_pairs={{0,1},{1,2},{2,3},{3,4},{4,5},{5,6},{6,7},{7,0},{8,9},{9,10},{10,1... | collective-permute-start | bytes 196616 | tf_op jit(solution)/shard_map/ppermute | solution.py:346
  8.2 12.3 %collective-permute-start.4 = (f32[32,512]{1,0:T(8,128)S(1)}, f32[32,512]{1,0:T(8,128)S(1)}, u32[]{:S(2)}, u32[]{:S(2)}) collective-permute-start(f32[32,512]{1,0:T(8,128)S(1)} %get-tuple-element.25), channel_id=1, source_target_pairs={{0,7},{1,0},{2,1},{3,2},{4,3},{5,4},{6,5},{7,6},{8,15},{9,8},{10,9... | collective-permute-start | bytes 196616 | tf_op jit(solution)/shard_map/ppermute | solution.py:346
  8.2 12.3 %collective-permute-start.1 = (f32[2,64,128]{2,1,0:T(8,128)S(1)}, f32[2,64,128]{2,1,0:T(8,128)S(1)}, u32[]{:S(2)}, u32[]{:S(2)}) collective-permute-start(f32[2,64,128]{2,1,0:T(8,128)S(1)} %get-tuple-element.22.moved_ref), channel_id=1, source_target_pairs={{0,2},{1,3},{2,4},{3,5},{4,6},{5,7},{6,8},{7,9},{8,10},{9,11},{10,... | collective-permute-start | bytes 196616 | tf_op jit(solution)/shard_map/ppermute | solution.py:341
  9.9 10.6 %collective-permute-start = (f32[2,64,128]{2,1,0:T(8,128)S(1)}, f32[2,64,128]{2,1,0:T(8,128)S(1)}, u32[]{:S(2)}, u32[]{:S(2)}) collective-permute-start(f32[2,64,128]{2,1,0:T(8,128)S(1)} %get-tuple-element.22.moved_ref), channel_id=1, source_target_pairs={{0,1},{1,2},{2,3},{3,4},{4,5},{5,6},{6,7},{7,8},{8,9},{9,10},{10,1... | collective-permute-start | bytes 196616 | tf_op jit(solution)/shard_map/ppermute | solution.py:341
  11.9 8.6 %collective-permute-start.2 = (f32[2,16,128]{2,1,0:T(8,128)S(1)}, f32[2,16,128]{2,1,0:T(8,128)S(1)}, u32[]{:S(2)}, u32[]{:S(2)}) collective-permute-start(f32[2,16,128]{2,1,0:T(8,128)S(1)} %get-tuple-element.23), channel_id=1, source_target_pairs={{0,3},{1,4},{2,5},{3,6},{4,7},{5,8},{6,9},{7,10},{8,11},{9,12},{10... | collective-permute-start | bytes 49160 | tf_op jit(solution)/shard_map/ppermute | solution.py:341
  21.6 6.6 %collective-permute-start.5 = (f32[72,128]{1,0:T(8,128)S(1)}, f32[72,128]{1,0:T(8,128)S(1)}, u32[]{:S(2)}, u32[]{:S(2)}) collective-permute-start(f32[72,128]{1,0:T(8,128)S(1)} %get-tuple-element.28), channel_id=1, source_target_pairs={{0,8},{8,16},{16,24},{24,32},{32,40},{40,48},{48,56},{56,64},{64,7... | collective-permute-start | bytes 110600 | tf_op jit(solution)/shard_map/ppermute | solution.py:346
  21.7 6.6 %collective-permute-start.6 = (f32[72,128]{1,0:T(8,128)S(1)}, f32[72,128]{1,0:T(8,128)S(1)}, u32[]{:S(2)}, u32[]{:S(2)}) collective-permute-start(f32[72,128]{1,0:T(8,128)S(1)} %get-tuple-element.29), channel_id=1, source_target_pairs={{0,120},{8,0},{16,8},{24,16},{32,24},{40,32},{48,40},{56,48},{64,5... | collective-permute-start | bytes 110600 | tf_op jit(solution)/shard_map/ppermute | solution.py:346
  34.7 5.6 %collective-permute-start.7 = (f32[2,64,128]{2,1,0:T(8,128)S(1)}, f32[2,64,128]{2,1,0:T(8,128)S(1)}, u32[]{:S(2)}, u32[]{:S(2)}) collective-permute-start(f32[2,64,128]{2,1,0:T(8,128)S(1)} %get-tuple-element.33), channel_id=1, source_target_pairs={{0,127},{1,0},{2,1},{3,2},{4,3},{5,4},{6,5},{7,6},{8,7},{9,8},{10,... | collective-permute-start | bytes 196616 | tf_op jit(solution)/shard_map/ppermute | solution.py:341
  35.4 4.8 %collective-permute-start.8 = (f32[2,64,128]{2,1,0:T(8,128)S(1)}, f32[2,64,128]{2,1,0:T(8,128)S(1)}, u32[]{:S(2)}, u32[]{:S(2)}) collective-permute-start(f32[2,64,128]{2,1,0:T(8,128)S(1)} %get-tuple-element.34), channel_id=1, source_target_pairs={{0,126},{1,127},{2,0},{3,1},{4,2},{5,3},{6,4},{7,5},{8,6},{9,7},{1... | collective-permute-start | bytes 196616 | tf_op jit(solution)/shard_map/ppermute | solution.py:341

commit v3 on v2

v3 whole, which is shorter than its diff:
```python
import jax
import jax.numpy as jnp
from jax import lax
from jax.experimental import pallas as pl
from jax.experimental.pallas import tpu as pltpu
from jax.sharding import PartitionSpec as P

MOVE = 2
ITERS = 10
ROWS, LANES = 64, 128
SLOTS = 12
KEPT = SLOTS - MOVE
LEVELS = 40
REGION = 4
OWN_ROWS = REGION * ROWS
CHUNK = 35
EXT_ROWS = 8 * CHUNK
FOLD = 72
PACK_ROWS = 4 * FOLD
COLS = REGION + 1

surface_term = 0.1
lower_bound = 0.05
upper_bound = 2.0

VMEM = pltpu.MemorySpace.VMEM
SMEM = pltpu.MemorySpace.SMEM
HBM = pltpu.MemorySpace.HBM


def chebyshev_plan():
    centre_value = (upper_bound + lower_bound) / 2.0
    half_width = (upper_bound - lower_bound) / 2.0
    ratio_value = centre_value / half_width
    weight = 1.0 / ratio_value
    scales = []
    for sweep in range(ITERS):
        renewed = 1.0 / (2.0 * ratio_value - weight)
        scales.append((renewed * weight, 2.0 * renewed / half_width))
        weight = renewed
    return (1.0 / centre_value, scales)


def place(block):
    row, col = block // 64, block % 64
    return (col // REGION) * 8 + row // REGION, row % REGION, col % REGION


def rolled(value, steps, axis):
    return pltpu.roll(value, steps % value.shape[axis], axis)


def wetness(rows, count, mask):
    position = lax.broadcasted_iota(jnp.int32, (rows, LANES), 0) * LANES + (
        lax.broadcasted_iota(jnp.int32, (rows, LANES), 1)
    )
    return (position < count) & (mask == 1)


def forcing_kernel(
    thick_in, owner_in, count_in, mask_in, tend_ref, depth_ref,
    inner_ref, outer_ref, moved_ref, bottom_ref, source_ref, masked_ref,
    thick_ref, owner_ref, count_ref, mask_ref, pair, levels, sea, table_sem, level_sem, sea_sem,
):
    myself = lax.axis_index("bx") * 8 + lax.axis_index("by")
    tables = []
    for index, (table_in, table_ref) in enumerate(
        ((count_in, count_ref), (mask_in, mask_ref), (thick_in, thick_ref), (owner_in, owner_ref))
    ):
        copy = pltpu.make_async_copy(table_in, table_ref, table_sem.at[index])
        copy.start()
        tables.append(copy)
    sea_copy = pltpu.make_async_copy(depth_ref, sea, sea_sem)
    sea_copy.start()
    copies = []
    for slot in range(SLOTS):
        copy = pltpu.make_async_copy(tend_ref.at[slot], levels.at[slot], level_sem.at[slot])
        copy.start()
        copies.append(copy)

    odd = lax.axis_index("by") % 2
    ahead_ref, back_ref = pair.at[odd], pair.at[1 - odd]
    ahead_ref[4:8, 16:32, :] = jnp.zeros((REGION, 16, LANES), jnp.float32)
    back_ref[...] = jnp.zeros((8, 32, LANES), jnp.float32)
    source_ref[...] = jnp.zeros(source_ref.shape, jnp.float32)
    for copy in tables:
        copy.wait()
    sea_copy.wait()
    for col in range(REGION):
        lanes = slice(col * LANES, (col + 1) * LANES)
        for row in range(REGION):
            rows = slice(row * ROWS, (row + 1) * ROWS)
            wet = wetness(ROWS, count_ref[row, col], mask_ref[row, col])
            value = jnp.where(wet, sea[rows, lanes], 0.0)
            masked_ref[col, rows, :] = value
            if row == 0:
                back_ref[4 + col, 0:16, :] = value[0:16, :]
            if row == REGION - 1:
                ahead_ref[4 + col, 0:16, :] = value[48:64, :]
        masked_ref[col, OWN_ROWS:PACK_ROWS, :] = jnp.zeros((PACK_ROWS - OWN_ROWS, LANES), jnp.float32)

    for slot in range(SLOTS):
        copies[slot].wait()
        totals = [jnp.zeros((16, LANES), jnp.float32) for _ in range(ROWS // 16)]
        for level in range(LEVELS):
            weight = thick_ref[level]
            for tile in range(ROWS // 16):
                part = levels[slot, level, tile * 16 : tile * 16 + 16, :].astype(jnp.float32)
                totals[tile] = totals[tile] + part * weight
        if slot >= KEPT:
            for tile, value in enumerate(totals):
                moved_ref[slot - KEPT, tile * 16 : tile * 16 + 16, :] = value
                half = slice(tile % 2 * 16, tile % 2 * 16 + 16)
                ahead_ref[(slot - KEPT) * 2 + tile // 2, half, :] = value
            bottom_ref[slot - KEPT] = totals[-1]
        region, row, col = place(owner_ref[myself * SLOTS + slot])

        @pl.when(region == myself)
        def _():
            for tile, value in enumerate(totals):
                first = pl.multiple_of(row * ROWS + tile * 16, 16)
                source_ref[col, pl.ds(first, 16), :] = value

        @pl.when((region == myself) & (row == 0))
        def _():
            back_ref[4 + col, 16:32, :] = totals[0]

        @pl.when((region == myself) & (row == REGION - 1))
        def _():
            ahead_ref[4 + col, 16:32, :] = totals[-1]

    inner_ref[...] = pair[0]
    outer_ref[...] = pair[1]


def gather_kernel(
    owner_ref, source_in, masked_in, moved_ref, inner_ref, outer_ref, two_ref, three_ref,
    source_ref, masked_ref, inner_side_ref, outer_side_ref,
    pair,
):
    del source_in, masked_in
    pair[0] = inner_ref[...]
    pair[1] = outer_ref[...]
    odd = lax.axis_index("by") % 2
    one_ref, under_ref = pair.at[1 - odd], pair.at[odd]
    row_index = lax.axis_index("by")
    myself = lax.axis_index("bx") * 8 + row_index
    end = OWN_ROWS + 8
    lane = lax.broadcasted_iota(jnp.int32, (8, LANES), 1)
    upper = lax.broadcasted_iota(jnp.int32, (8, LANES), 0) < 4

    not_south = row_index == 7
    not_north = row_index == 0
    for col in range(REGION):
        south_ref = under_ref.at[4 + col]
        south = [jnp.where(not_south, 0.0, south_ref[8 * i : 8 * i + 8, :]) for i in range(2)]
        north_ref = one_ref.at[4 + col]
        north = [jnp.where(not_north, 0.0, north_ref[8 * i : 8 * i + 8, :]) for i in range(2)]
        masked_ref[col, OWN_ROWS:end, :] = south[0]
        masked_ref[col, end : end + 8, :] = jnp.where(upper, south[1], north[0])
        masked_ref[col, end + 8 : end + 16, :] = north[1]
        source_ref[col, OWN_ROWS:end, :] = south_ref[16:24, :]
        source_ref[col, end : end + 8, :] = jnp.where(
            upper, south_ref[24:32, :], north_ref[16:24, :]
        )
        source_ref[col, end + 8 : end + 16, :] = north_ref[24:32, :]

    def spread(sender, slot, block, bottom, inside=True, above=True, below=True):
        region, row, col = place(owner_ref[sender * SLOTS + slot])
        if inside:

            @pl.when(region == myself)
            def _():
                first = pl.multiple_of(row * ROWS, ROWS)
                source_ref[col, pl.ds(first, ROWS), :] = block[...].reshape(ROWS, LANES)

        if below:

            @pl.when((region == myself + 1) & (row == 0))
            def _():
                source_ref[col, OWN_ROWS:end, :] = block[0, 0:8, :]
                mixed = source_ref[col, end : end + 8, :]
                source_ref[col, end : end + 8, :] = jnp.where(upper, block[0, 8:16, :], mixed)

        if above:

            @pl.when((region == myself - 1) & (row == REGION - 1))
            def _():
                mixed = source_ref[col, end : end + 8, :]
                source_ref[col, end : end + 8, :] = jnp.where(upper, mixed, bottom[0:8, :])
                source_ref[col, end + 8 : end + 16, :] = bottom[8:16, :]

    for extra in range(MOVE):
        slot = KEPT + extra
        block = moved_ref.at[extra : extra + 1]
        spread(myself, slot, block, None, inside=False, above=False)
        block = one_ref.at[2 * extra : 2 * extra + 2]
        spread((myself + 127) % 128, slot, block, None, above=False)
        block = two_ref.at[extra : extra + 1]
        spread((myself + 126) % 128, slot, block, block.at[0, 48:64, :], below=False)
        spread((myself + 125) % 128, slot, None, three_ref.at[extra], inside=False, below=False)

    even = lax.axis_index("bx") % 2 == 0
    for row in range(FOLD // 8):
        left = jnp.zeros((8, LANES), jnp.float32)
        right = jnp.zeros((8, LANES), jnp.float32)
        for group in range(4):
            rows = slice(group * FOLD + row * 8, group * FOLD + row * 8 + 8)
            for field, ref in enumerate((masked_ref, source_ref)):
                to = 32 * group + 16 * field
                here = (lane >= to) & (lane < to + 16)
                left = jnp.where(here, rolled(ref[0, rows, :], to, 1), left)
                right = jnp.where(here, rolled(ref[REGION - 1, rows, :], to + 16, 1), right)
        inner_side_ref[row * 8 : row * 8 + 8, :] = jnp.where(even, right, left)
        outer_side_ref[row * 8 : row * 8 + 8, :] = jnp.where(even, left, right)


class Sweeper:
    def __init__(self, cols, scale_ref, fields):
        self.cols, self.scale_ref = cols, scale_ref
        self.direction, self.residual, self.total = fields[:3]
        self.corner, self.inverse, self.diagonal, self.flow = fields[3:]
        lane = lax.broadcasted_iota(jnp.int32, (8, LANES), 1)
        self.first_lane, self.last_lane = lane == 0, lane == LANES - 1

    def from_west(self, row):
        turned = [rolled(value, 1, 1) for value in row]
        if self.cols == 1:
            return turned
        return [jnp.where(self.first_lane, turned[c - 1], turned[c]) for c in range(self.cols)]

    def gathered(self, row):
        turned = [rolled(value, -1, 1) for value in row]
        if self.cols > 1:
            following = turned[1:] + turned[:1]
            turned = join(lambda a, b: jnp.where(self.last_lane, a, b), following, turned)
        return join(jnp.add, row, turned)

    def load(self, ref, k):
        return [ref[k, col] for col in range(self.cols)]

    def store(self, ref, k, row):
        for col in range(self.cols):
            ref[k, col] = row[col]

    def prepare(self, masked_ref, source_ref):
        def strided(ref, k):
            return [ref[col, pl.ds(k, 8, stride=CHUNK), :] for col in range(self.cols)]

        opening, _ = chebyshev_plan()
        above = turn(strided(masked_ref, CHUNK - 1), 1)
        for k in range(CHUNK):
            here = strided(masked_ref, k)
            both = join(jnp.minimum, above, here)
            self.store(self.corner, k, join(jnp.minimum, both, self.from_west(both)))
            above = here
        for k in range(CHUNK):
            around = self.gathered(join(jnp.add, self.load(self.corner, k), self.below(self.corner, k)))
            source, masked = strided(source_ref, k), strided(masked_ref, k)
            for col in range(self.cols):
                inv = 1.0 / (surface_term + 0.75 * around[col])
                start = inv * jnp.where(masked[col] > 0.0, source[col], 0.0)
                self.inverse[k, col] = 0.25 * inv
                self.diagonal[k, col] = inv * (surface_term + around[col])
                self.residual[k, col] = start
                self.direction[k, col] = opening * start
                self.total[k, col] = opening * start

    def below(self, ref, k):
        return self.load(ref, k + 1) if k + 1 < CHUNK else turn(self.load(ref, 0), -1)

    def sweep(self, index, final=None):
        carry_scale, forward_scale = self.scale_ref[index, 0], self.scale_ref[index, 1]
        above = turn(self.load(self.direction, CHUNK - 1), 1)
        for k in range(CHUNK):
            here = self.load(self.direction, k)
            both = join(jnp.add, above, here)
            spread = join(jnp.add, both, self.from_west(both))
            self.store(self.flow, k, join(jnp.multiply, spread, self.load(self.corner, k)))
            above = here
        for k in range(CHUNK):
            back = self.gathered(join(jnp.add, self.load(self.flow, k), self.below(self.flow, k)))
            for col in range(self.cols):
                here = self.direction[k, col]
                rest = self.residual[k, col] - self.diagonal[k, col] * here
                rest = rest + self.inverse[k, col] * back[col]
                turned = carry_scale * here + forward_scale * rest
                summed = self.total[k, col] + turned
                if final is not None:
                    final(k, col, summed)
                else:
                    self.residual[k, col] = rest
                    self.direction[k, col] = turned
                    self.total[k, col] = summed

    def solve(self, final):
        lax.fori_loop(0, ITERS - 2, lambda index, _: self.sweep(index), None)
        self.sweep(ITERS - 2, final)


def join(f, *rows):
    return [f(*values) for values in zip(*rows)]


def turn(row, steps):
    return [rolled(value, steps, 0) for value in row]


def region_kernel(scale_ref, source_ref, masked_ref, standard, *fields):
    sweeper = Sweeper(REGION, scale_ref, fields)
    sweeper.prepare(masked_ref, source_ref)

    def final(k, col, value):
        standard[col, pl.ds(k, 8, stride=CHUNK), :] = value

    sweeper.solve(final)


def sides_kernel(
    owner_ref, scale_ref, standard_in, source_ref, masked_ref, inner_ref, outer_ref,
    standard, one_ref, two_ref,
    depth_side, source_side, *fields,
):
    del standard_in
    myself = lax.axis_index("bx") * 8 + lax.axis_index("by")
    lane = lax.broadcasted_iota(jnp.int32, (8, LANES), 1)
    even = lax.axis_index("bx") % 2 == 0
    outer_west, outer_east = lane < 16, (lane >= 96) & (lane < 112)
    own_west, own_east = (lane >= 16) & (lane < 48), (lane >= 64) & (lane < 96)
    for row in range(FOLD // 8):
        rows = slice(row * 8, row * 8 + 8)
        inner, outer = inner_ref[rows, :], outer_ref[rows, :]
        west, east = jnp.where(even, outer, inner), jnp.where(even, inner, outer)
        for group in range(4):
            first = group * FOLD + row * 8
            for field, (ref, side) in enumerate(((masked_ref, depth_side), (source_ref, source_side))):
                start = 32 * group + 16 * field
                inside = rolled(ref[0, first : first + 8, :], 16, 1)
                value = jnp.where(own_west, inside, 0.0)
                inside = rolled(ref[REGION - 1, first : first + 8, :], -32, 1)
                value = jnp.where(own_east, inside, value)
                value = jnp.where(outer_west, rolled(west, -start, 1), value)
                value = jnp.where(outer_east, rolled(east, 96 - start, 1), value)
                side[0, first : first + 8, :] = value

    sweeper = Sweeper(1, scale_ref, fields)
    sweeper.prepare(depth_side, source_side)
    first_columns, last_columns = lane < 16, lane >= 112

    def final(k, col, value):
        rows = pl.ds(k, 8, stride=CHUNK)
        standard[0, rows, :] = jnp.where(first_columns, rolled(value, -16, 1), standard[0, rows, :])
        last = REGION - 1
        standard[last, rows, :] = jnp.where(last_columns, rolled(value, 32, 1), standard[last, rows, :])

    sweeper.solve(final)
    for extra in range(MOVE):
        block_of(myself, (myself + 127) % 128, KEPT + extra, owner_ref, standard, one_ref, extra)
        block_of(myself, (myself + 126) % 128, KEPT + extra, owner_ref, standard, two_ref, extra)


def block_of(myself, sender, slot, owner_ref, standard, ref, index):
    region, row, col = place(owner_ref[sender * SLOTS + slot])
    first = pl.multiple_of(row * ROWS, ROWS)
    value = standard[col, pl.ds(first, ROWS), :]
    ref[index] = jnp.where(region == myself, value, 0.0)


def write_kernel(owner_ref, standard, out_ref, tail_ref):
    myself = lax.axis_index("bx") * 8 + lax.axis_index("by")
    for slot in range(SLOTS):
        block_of(myself, myself, slot, owner_ref, standard, out_ref, slot)
    for extra in range(MOVE):
        tail_ref[extra] = out_ref[KEPT + extra]


def tail_kernel(heights_ref, tail_ref, one_ref, two_ref, out_ref, joined, sem):
    del heights_ref
    joined[...] = tail_ref[...] + (one_ref[...] + two_ref[...])
    copy = pltpu.make_async_copy(joined, out_ref.at[pl.ds(KEPT, MOVE)], sem)
    copy.start()
    copy.wait()


def whole(space=VMEM):
    return pl.BlockSpec(memory_space=space)


def ring(value, steps, senders=range(8)):
    count = lax.axis_size("bx") * lax.axis_size("by")
    pairs = [(i, (i + steps) % count) for i in range(count) if i % 8 in senders]
    return lax.ppermute(value, ("bx", "by"), pairs)


def inner_swap(value, axis):
    return lax.ppermute(value, axis, [(i, i ^ 1) for i in range(lax.axis_size(axis))])


def outer_swap(value, axis):
    count = lax.axis_size(axis)
    pairs = [(i, (i + 1 if i % 2 else i - 1) % count) for i in range(count)]
    return lax.ppermute(value, axis, pairs)


def outer_ring_swap(value):
    count = lax.axis_size("bx") * lax.axis_size("by")
    pairs = [(i, (i + 1) % count) for i in range(1, count, 2)]
    pairs += [(i, i - 1) for i in range(0, count, 2) if i % 8]
    return lax.ppermute(value, ("bx", "by"), pairs)


def near(value):
    return pltpu.with_memory_space_constraint(value, VMEM)


def distant(value):
    return pltpu.with_memory_space_constraint(value, HBM)


def on_device(tendency, thickness, depth, block_owner, block_mask, ocean_counts):
    f32 = jnp.float32
    params = pltpu.CompilerParams(vmem_limit_bytes=32 << 20)
    far = pl.BlockSpec(memory_space=HBM)

    def here(*dims):
        return pltpu.VMEM(dims, f32)

    field = (REGION, PACK_ROWS, LANES)
    inner, outer, moved, bottom, source, masked = pl.pallas_call(
        forcing_kernel,
        in_specs=[far] * 6,
        out_specs=[whole()] * 6,
        out_shape=[
            here(8, 32, LANES),
            here(8, 32, LANES),
            here(MOVE, ROWS, LANES),
            here(MOVE, 16, LANES),
            here(*field),
            here(*field),
        ],
        scratch_shapes=[
            pltpu.SMEM(thickness.shape, f32),
            pltpu.SMEM(block_owner.shape, jnp.int32),
            pltpu.SMEM(ocean_counts.shape, jnp.int32),
            pltpu.SMEM(block_mask.shape, jnp.int32),
            here(2, 8, 32, LANES),
            pltpu.VMEM((SLOTS, LEVELS, ROWS, LANES), jnp.bfloat16),
            pltpu.VMEM((OWN_ROWS, REGION * LANES), f32),
            pltpu.SemaphoreType.DMA((4,)),
            pltpu.SemaphoreType.DMA((SLOTS,)),
            pltpu.SemaphoreType.DMA,
        ],
        compiler_params=params,
        name="forcing",
    )(*map(distant, (thickness, block_owner, ocean_counts, block_mask, tendency, depth)))
    outer = outer_ring_swap(outer)
    two = ring(moved, 2)
    three = ring(bottom, 3, (0, 1, 2, 3, 4, 6, 7))
    inner = inner_swap(inner, "by")

    inputs = [near(x) for x in (source, masked, moved, inner, outer, two, three)]
    source, masked, inner, outer = pl.pallas_call(
        gather_kernel,
        in_specs=[whole(SMEM)] + [whole()] * 7,
        out_specs=[whole()] * 4,
        out_shape=[here(*field), here(*field), here(FOLD, LANES), here(FOLD, LANES)],
        input_output_aliases={1: 0, 2: 1},
        scratch_shapes=[here(2, 8, 32, LANES)],
        compiler_params=params,
        name="assemble",
    )(block_owner, *inputs)
    inner, outer = inner_swap(inner, "bx"), outer_swap(outer, "bx")

    scales = jnp.asarray(chebyshev_plan()[1], f32)
    heights = pl.pallas_call(
        region_kernel,
        in_specs=[whole(SMEM)] + [whole()] * 2,
        out_specs=whole(),
        out_shape=here(REGION, EXT_ROWS, LANES),
        scratch_shapes=[here(CHUNK, REGION, 8, LANES)] * 7,
        compiler_params=params,
        name="region",
    )(scales, near(source), near(masked))

    inputs = [near(x) for x in (heights, source, masked, inner, outer)]
    heights, first, second = pl.pallas_call(
        sides_kernel,
        in_specs=[whole(SMEM)] * 2 + [whole()] * 5,
        out_specs=[whole()] * 3,
        out_shape=[
            here(REGION, EXT_ROWS, LANES),
            here(MOVE, ROWS, LANES),
            here(MOVE, ROWS, LANES),
        ],
        input_output_aliases={2: 0},
        scratch_shapes=[here(1, PACK_ROWS, LANES)] * 2 + [here(CHUNK, 1, 8, LANES)] * 7,
        compiler_params=params,
        name="sides",
    )(block_owner, scales, *inputs)
    back = ring(first, -1), ring(second, -2)

    out, tail = pl.pallas_call(
        write_kernel,
        in_specs=[whole(SMEM), whole()],
        out_specs=[whole()] * 2,
        out_shape=[jax.ShapeDtypeStruct((SLOTS, ROWS, LANES), f32), here(MOVE, ROWS, LANES)],
        compiler_params=params,
        name="write",
    )(block_owner, near(heights))
    return pl.pallas_call(
        tail_kernel,
        in_specs=[far] + [whole()] * 3,
        out_specs=far,
        out_shape=jax.ShapeDtypeStruct((SLOTS, ROWS, LANES), f32),
        input_output_aliases={0: 0},
        scratch_shapes=[here(MOVE, ROWS, LANES), pltpu.SemaphoreType.DMA],
        compiler_params=params,
        name="tail",
    )(out, near(tail), near(back[0]), near(back[1]))


def solution(mesh):
    placed = (
        P(("bx", "by"), None, None, None),
        P(),
        P("by", "bx"),
        P(),
        P("by", "bx"),
        P("by", "bx"),
    )
    return jax.shard_map(
        on_device,
        mesh=mesh,
        in_specs=placed,
        out_specs=P(("bx", "by"), None, None),
        check_vma=False,
    )
```

time: 41 us -> 39.1 us (0.954)
  waiting for transfers between devices: 8.72 us -> 6.15 us
  Pallas kernels: 15 us -> 16.9 us
  starting transfers between devices: 17.2 us -> 15.8 us
    ppermute x9 -> x8, waiting for transfers between devices: 8.72 us -> 6.15 us  [the longest x4 6.14 us: ring(): return lax.ppermute(value, ('bx', 'by'), pairs)]
    pallas_call x2 -> x3, Pallas kernels: 7.56 us -> 9.49 us  [the longest x1 5.25 us: on_device(): pl.pallas_call(region_kernel, in_specs=[whole(SMEM)] + [whole()] * 2, out...]
    ppermute x9 -> x8, starting transfers between devices: 17.2 us -> 15.8 us  [the longest x4 8.61 us: ring(): return lax.ppermute(value, ('bx', 'by'), pairs)]
  transfers between devices with their start and end apart: 9 -> 8, of which waited for: 2 -> 1; matrix products, arithmetic and copies ran while one was open for 0% -> 0% of each run, Pallas kernels for 4% -> 18%
where the time goes in v3:
time: 39.1 us; the launch traced here: 39 us
  Pallas kernels  16.9 us (43%)
  starting transfers between devices  15.8 us (40%)
  waiting for transfers between devices  6.15 us (16%)
    ppermute x4, starting transfers between devices, ring(): return lax.ppermute(value, ('bx', 'by'), pairs)  8.61 us
    ppermute x4, waiting for transfers between devices, ring(): return lax.ppermute(value, ('bx', 'by'), pairs)  6.14 us
    pallas_call x1, Pallas kernels, on_device(): pl.pallas_call(region_kernel, in_specs=[whole(SMEM)] + [whole()] * 2, out...  5.25 us
    pallas_call x1, Pallas kernels, on_device(): pl.pallas_call(forcing_kernel, in_specs=[far] * 6, out_specs=[whole()] *...  5.19 us
    ppermute x1, starting transfers between devices, outer_ring_swap(): return lax.ppermute(value, ('bx', 'by'), pairs)  3.53 us
    pallas_call x1, Pallas kernels, on_device(): pl.pallas_call(sides_kernel, in_specs=[whole(SMEM)] * 2 + [whole()] * 5,...  3.13 us
    ppermute x1, starting transfers between devices, outer_swap(): return lax.ppermute(value, axis, pairs)  2.06 us
    pallas_call x1, Pallas kernels, on_device(): pl.pallas_call(write_kernel, in_specs=[whole(SMEM), whole()], out_specs=[...  1.61 us
  transfers between devices with their start and end apart: 8, of which 1 were waited for; matrix products, arithmetic and copies ran while one was open for 0% of the time, Pallas kernels for 18%

profile of v3, /device:TPU:1, one launch (start us, length us, event | category | flops | bytes accessed | tf_op | source)
XLA Modules:
  0.0 39.0 jit_solution(11813153102347695174)
XLA Ops:
  0.0 0.0 copy-start.1
  0.0 0.0 copy-start
  0.0 5.2 %forcing.1 = (f32[8,32,128]{2,1,0:T(8,128)S(1)}, f32[8,32,128]{2,1,0:T(8,128)S(1)}, f32[2,64,128]{2,1,0:T(8,128)S(1)}, f32[2,16,128]{2,1,0:T(8,128)S(1)}, f32[4,...) custom-call(f32[40]{0:T(128)} %thick_in.1, s32[1536]{0:T(1024)} %owner_ref.5, s32[4,4]{1,0:T(4,128)} %count_in.1, ...), custom_call_target="tpu_custom_call" | custom-call | tf_op jit(solution)/shard_map/forcing/pallas_call | solution.py:429
  5.2 1.5 %collective-permute-start = (f32[8,32,128]{2,1,0:T(8,128)S(1)}, f32[8,32,128]{2,1,0:T(8,128)S(1)}, u32[]{:S(2)}, u32[]{:S(2)}) collective-permute-start(f32[8,32,128]{2,1,0:T(8,128)S(1)} %get-tuple-element.23), channel_id=1, source_target_pairs={{0,1},{1,0},{2,3},{3,2},{4,5},{5,4},{6,7},{7,6},{8,9},{9,8},{10,11... | collective-permute-start | bytes 393224 | tf_op jit(solution)/shard_map/ppermute | solution.py:396
  6.7 3.5 %collective-permute-start.1 = (f32[8,32,128]{2,1,0:T(8,128)S(1)}, f32[8,32,128]{2,1,0:T(8,128)S(1)}, u32[]{:S(2)}, u32[]{:S(2)}) collective-permute-start(f32[8,32,128]{2,1,0:T(8,128)S(1)} %get-tuple-element.24), channel_id=1, source_target_pairs={{1,2},{3,4},{5,6},{7,8},{9,10},{11,12},{13,14},{15,16},{17,18},{19... | collective-permute-start | bytes 393224 | tf_op jit(solution)/shard_map/ppermute | solution.py:409
  10.2 1.7 %collective-permute-start.2 = (f32[2,64,128]{2,1,0:T(8,128)S(1)}, f32[2,64,128]{2,1,0:T(8,128)S(1)}, u32[]{:S(2)}, u32[]{:S(2)}) collective-permute-start(f32[2,64,128]{2,1,0:T(8,128)S(1)} %get-tuple-element.22.moved_ref), channel_id=1, source_target_pairs={{0,2},{1,3},{2,4},{3,5},{4,6},{5,7},{6,8},{7,9},{8,10},{9,11},{10,... | collective-permute-start | bytes 196616 | tf_op jit(solution)/shard_map/ppermute | solution.py:392
  11.9 4.3 %collective-permute-start.3 = (f32[2,16,128]{2,1,0:T(8,128)S(1)}, f32[2,16,128]{2,1,0:T(8,128)S(1)}, u32[]{:S(2)}, u32[]{:S(2)}) collective-permute-start(f32[2,16,128]{2,1,0:T(8,128)S(1)} %get-tuple-element.25), channel_id=1, source_target_pairs={{0,3},{1,4},{2,5},{3,6},{4,7},{6,9},{7,10},{8,11},{9,12},{10,13},{... | collective-permute-start | bytes 49160 | tf_op jit(solution)/shard_map/ppermute | solution.py:392
  16.3 6.1 %collective-permute-done.3.three_ref = f32[2,16,128]{2,1,0:T(8,128)S(1)} collective-permute-done((f32[2,16,128]{2,1,0:T(8,128)S(1)}, f32[2,16,128]{2,1,0:T(8,128)S(1)}, u32[]{:S(2)}, u32[]{:S(2)}) %collective-permute-start.3) | collective-permute-done | bytes 16416 | tf_op jit(solution)/shard_map/ppermute | solution.py:392
  22.4 0.0 collective-permute-done.2.two_ref
  22.4 0.0 collective-permute-done.inner_ref
  22.4 0.0 collective-permute-done.1.outer_ref
  22.4 0.0 copy-done
  22.4 1.1 %assemble.1 = (f32[4,288,128]{2,1,0:T(8,128)S(1)}, f32[4,288,128]{2,1,0:T(8,128)S(1)}, f32[72,128]{1,0:T(8,128)S(1)}, f32[72,128]{1,0:T(8,128)S(1)}) custom-call(s32[1536]{0:T(1024)S(1)} %copy-done, f32[4,288,128]{2,1,0:T(8,128)S(1)} %get-tuple-element.20.source_in, ...), custom_call_target="tpu_custom_call", output_to_operand_aliasing={{0}: (1, {}), {1}: (2, {})} | custom-call | tf_op jit(solution)/shard_map/assemble/pallas_call | solution.py:462
  23.6 0.1 collective-permute-start.4
  23.7 2.1 %collective-permute-start.5 = (f32[72,128]{1,0:T(8,128)S(1)}, f32[72,128]{1,0:T(8,128)S(1)}, u32[]{:S(2)}, u32[]{:S(2)}) collective-permute-start(f32[72,128]{1,0:T(8,128)S(1)} %get-tuple-element.29), channel_id=1, source_target_pairs={{0,120},{8,16},{16,8},{24,32},{32,24},{40,48},{48,40},{56,64},{64,... | collective-permute-start | bytes 110600 | tf_op jit(solution)/shard_map/ppermute | solution.py:402
  25.7 0.0 copy-done.1
  25.7 5.3 %region.1.standard_in = f32[4,280,128]{2,1,0:T(8,128)S(1)} custom-call(f32[10,2]{1,0:T(8,128)S(1)} %copy-done.1, f32[4,288,128]{2,1,0:T(8,128)S(1)} %get-tuple-element.26.source_ref, f32[4,288,128]{2,1,0:T(8,128)S(1)} %get-tuple-element.27.masked_ref), custom_call_target="tpu_custom_call" | custom-call | tf_op jit(solution)/shard_map/region/pallas_call | solution.py:475
  31.0 0.0 collective-permute-done.4.inner_ref
  31.0 0.0 collective-permute-done.5.outer_ref
  31.0 3.1 %sides.1 = (f32[4,280,128]{2,1,0:T(8,128)S(1)}, f32[2,64,128]{2,1,0:T(8,128)S(1)}, f32[2,64,128]{2,1,0:T(8,128)S(1)}) custom-call(s32[1536]{0:T(1024)S(1)} %copy-done, f32[10,2]{1,0:T(8,128)S(1)} %copy-done.1, f32[4,280,128]{2,1,0:T(8,128)S(1)} %region.1.standard_in, ...), custom_call_target="tpu_custom_call", output_to_operand_aliasing={{0}: (2, {})} | custom-call | tf_op jit(solution)/shard_map/sides/pallas_call | solution.py:486
  34.1 0.1 collective-permute-start.6
  34.2 2.5 %collective-permute-start.7 = (f32[2,64,128]{2,1,0:T(8,128)S(1)}, f32[2,64,128]{2,1,0:T(8,128)S(1)}, u32[]{:S(2)}, u32[]{:S(2)}) collective-permute-start(f32[2,64,128]{2,1,0:T(8,128)S(1)} %get-tuple-element.34), channel_id=1, source_target_pairs={{0,126},{1,127},{2,0},{3,1},{4,2},{5,3},{6,4},{7,5},{8,6},{9,7},{1... | collective-permute-start | bytes 196616 | tf_op jit(solution)/shard_map/ppermute | solution.py:392
  36.7 1.6 %write.1 = (f32[12,64,128]{2,1,0:T(8,128)}, f32[2,64,128]{2,1,0:T(8,128)S(1)}) custom-call(s32[1536]{0:T(1024)S(1)} %copy-done, f32[4,280,128]{2,1,0:T(8,128)S(1)} %get-tuple-element.30.standard), custom_call_target="tpu_custom_call" | custom-call | tf_op jit(solution)/shard_map/write/pallas_call | solution.py:502
  38.3 0.0 collective-permute-done.6.one_ref
  38.3 0.0 collective-permute-done.7.two_ref
  38.3 0.7 %tail.1 = f32[12,64,128]{2,1,0:T(8,128)} custom-call(f32[12,64,128]{2,1,0:T(8,128)} %get-tuple-element.31.heights_ref, f32[2,64,128]{2,1,0:T(8,128)S(1)} %get-tuple-element.32.tail_ref, f32[2,64,128]{2,1,0:T(8,128)S(1)} %collective-permute-done.6.one_ref, f32[2,64,128]{2,1,0:T(8,128)S(1)} %collective-permute-done.7.two_ref), custom_call_target="tpu_custom_call", output_to_operand_aliasing={{}: (0, {})} | custom-call | tf_op jit(solution)/shard_map/tail/pallas_call | solution.py:510
Async XLA Ops:
  0.0 25.7 %copy-start.1 = (f32[10,2]{1,0:T(8,128)S(1)}, f32[10,2]{1,0:T(8,128)}, u32[]{:S(2)}) copy-start(f32[10,2]{1,0:T(8,128)} %constant.2.clone.scale_ref) | copy-start | bytes 244
  0.0 22.4 %copy-start = (s32[1536]{0:T(1024)S(1)}, s32[1536]{0:T(1024)}, u32[]{:S(2)}) copy-start(s32[1536]{0:T(1024)} %owner_ref.5) | copy-start | bytes 18436
  5.2 17.2 %collective-permute-start = (f32[8,32,128]{2,1,0:T(8,128)S(1)}, f32[8,32,128]{2,1,0:T(8,128)S(1)}, u32[]{:S(2)}, u32[]{:S(2)}) collective-permute-start(f32[8,32,128]{2,1,0:T(8,128)S(1)} %get-tuple-element.23), channel_id=1, source_target_pairs={{0,1},{1,0},{2,3},{3,2},{4,5},{5,4},{6,7},{7,6},{8,9},{9,8},{10,11... | collective-permute-start | bytes 393224 | tf_op jit(solution)/shard_map/ppermute | solution.py:396
  6.7 15.7 %collective-permute-start.1 = (f32[8,32,128]{2,1,0:T(8,128)S(1)}, f32[8,32,128]{2,1,0:T(8,128)S(1)}, u32[]{:S(2)}, u32[]{:S(2)}) collective-permute-start(f32[8,32,128]{2,1,0:T(8,128)S(1)} %get-tuple-element.24), channel_id=1, source_target_pairs={{1,2},{3,4},{5,6},{7,8},{9,10},{11,12},{13,14},{15,16},{17,18},{19... | collective-permute-start | bytes 393224 | tf_op jit(solution)/shard_map/ppermute | solution.py:409
  10.2 12.2 %collective-permute-start.2 = (f32[2,64,128]{2,1,0:T(8,128)S(1)}, f32[2,64,128]{2,1,0:T(8,128)S(1)}, u32[]{:S(2)}, u32[]{:S(2)}) collective-permute-start(f32[2,64,128]{2,1,0:T(8,128)S(1)} %get-tuple-element.22.moved_ref), channel_id=1, source_target_pairs={{0,2},{1,3},{2,4},{3,5},{4,6},{5,7},{6,8},{7,9},{8,10},{9,11},{10,... | collective-permute-start | bytes 196616 | tf_op jit(solution)/shard_map/ppermute | solution.py:392
  11.9 10.5 %collective-permute-start.3 = (f32[2,16,128]{2,1,0:T(8,128)S(1)}, f32[2,16,128]{2,1,0:T(8,128)S(1)}, u32[]{:S(2)}, u32[]{:S(2)}) collective-permute-start(f32[2,16,128]{2,1,0:T(8,128)S(1)} %get-tuple-element.25), channel_id=1, source_target_pairs={{0,3},{1,4},{2,5},{3,6},{4,7},{6,9},{7,10},{8,11},{9,12},{10,13},{... | collective-permute-start | bytes 49160 | tf_op jit(solution)/shard_map/ppermute | solution.py:392
  23.6 7.4 %collective-permute-start.4 = (f32[72,128]{1,0:T(8,128)S(1)}, f32[72,128]{1,0:T(8,128)S(1)}, u32[]{:S(2)}, u32[]{:S(2)}) collective-permute-start(f32[72,128]{1,0:T(8,128)S(1)} %get-tuple-element.28), channel_id=1, source_target_pairs={{0,8},{8,0},{16,24},{24,16},{32,40},{40,32},{48,56},{56,48},{64,72... | collective-permute-start | bytes 110600 | tf_op jit(solution)/shard_map/ppermute | solution.py:396
  23.7 7.3 %collective-permute-start.5 = (f32[72,128]{1,0:T(8,128)S(1)}, f32[72,128]{1,0:T(8,128)S(1)}, u32[]{:S(2)}, u32[]{:S(2)}) collective-permute-start(f32[72,128]{1,0:T(8,128)S(1)} %get-tuple-element.29), channel_id=1, source_target_pairs={{0,120},{8,16},{16,8},{24,32},{32,24},{40,48},{48,40},{56,64},{64,... | collective-permute-start | bytes 110600 | tf_op jit(solution)/shard_map/ppermute | solution.py:402
  34.1 4.2 %collective-permute-start.6 = (f32[2,64,128]{2,1,0:T(8,128)S(1)}, f32[2,64,128]{2,1,0:T(8,128)S(1)}, u32[]{:S(2)}, u32[]{:S(2)}) collective-permute-start(f32[2,64,128]{2,1,0:T(8,128)S(1)} %get-tuple-element.33), channel_id=1, source_target_pairs={{0,127},{1,0},{2,1},{3,2},{4,3},{5,4},{6,5},{7,6},{8,7},{9,8},{10,... | collective-permute-start | bytes 196616 | tf_op jit(solution)/shard_map/ppermute | solution.py:392
  34.2 4.1 %collective-permute-start.7 = (f32[2,64,128]{2,1,0:T(8,128)S(1)}, f32[2,64,128]{2,1,0:T(8,128)S(1)}, u32[]{:S(2)}, u32[]{:S(2)}) collective-permute-start(f32[2,64,128]{2,1,0:T(8,128)S(1)} %get-tuple-element.34), channel_id=1, source_target_pairs={{0,126},{1,127},{2,0},{3,1},{4,2},{5,3},{6,4},{7,5},{8,6},{9,7},{1... | collective-permute-start | bytes 196616 | tf_op jit(solution)/shard_map/ppermute | solution.py:392

commit v4 on v3

--- a/solution.py
+++ b/solution.py
@@ -57,62 +57,73 @@
     return (position < count) & (mask == 1)
 
 
-def forcing_kernel(
-    thick_in, owner_in, count_in, mask_in, tend_ref, depth_ref,
-    inner_ref, outer_ref, moved_ref, bottom_ref, source_ref, masked_ref,
-    thick_ref, owner_ref, count_ref, mask_ref, pair, levels, sea, table_sem, level_sem, sea_sem,
+def level_sum(tend_ref, slot, thick_ref):
+    totals = [jnp.zeros((16, LANES), jnp.float32) for _ in range(ROWS // 16)]
+    for level in range(LEVELS):
+        weight = thick_ref[level]
+        for tile in range(ROWS // 16):
+            part = tend_ref[slot, level, tile * 16 : tile * 16 + 16, :].astype(jnp.float32)
+            totals[tile] = totals[tile] + part * weight
+    return totals
+
+
+def moved_kernel(
+    thick_in, count_in, mask_in, tend_ref, depth_ref,
+    moved_ref, masked_ref,
+    thick_ref, count_ref, mask_ref, levels, sea, table_sem, level_sem, sea_sem,
 ):
-    myself = lax.axis_index("bx") * 8 + lax.axis_index("by")
     tables = []
     for index, (table_in, table_ref) in enumerate(
-        ((count_in, count_ref), (mask_in, mask_ref), (thick_in, thick_ref), (owner_in, owner_ref))
+        ((thick_in, thick_ref), (count_in, count_ref), (mask_in, mask_ref))
     ):
         copy = pltpu.make_async_copy(table_in, table_ref, table_sem.at[index])
         copy.start()
         tables.append(copy)
+    copies = []
+    for extra in range(MOVE):
+        copy = pltpu.make_async_copy(
+            tend_ref.at[KEPT + extra], levels.at[extra], level_sem.at[extra]
+        )
+        copy.start()
+        copies.append(copy)
     sea_copy = pltpu.make_async_copy(depth_ref, sea, sea_sem)
     sea_copy.start()
-    copies = []
-    for slot in range(SLOTS):
-        copy = pltpu.make_async_copy(tend_ref.at[slot], levels.at[slot], level_sem.at[slot])
-        copy.start()
-        copies.append(copy)
-
-    odd = lax.axis_index("by") % 2
-    ahead_ref, back_ref = pair.at[odd], pair.at[1 - odd]
-    ahead_ref[4:8, 16:32, :] = jnp.zeros((REGION, 16, LANES), jnp.float32)
-    back_ref[...] = jnp.zeros((8, 32, LANES), jnp.float32)
-    source_ref[...] = jnp.zeros(source_ref.shape, jnp.float32)
     for copy in tables:
         copy.wait()
+    for extra in range(MOVE):
+        copies[extra].wait()
+        totals = level_sum(levels, extra, thick_ref)
+        for tile, value in enumerate(totals):
+            moved_ref[extra, tile * 16 : tile * 16 + 16, :] = value
     sea_copy.wait()
     for col in range(REGION):
         lanes = slice(col * LANES, (col + 1) * LANES)
         for row in range(REGION):
             rows = slice(row * ROWS, (row + 1) * ROWS)
             wet = wetness(ROWS, count_ref[row, col], mask_ref[row, col])
-            value = jnp.where(wet, sea[rows, lanes], 0.0)
-            masked_ref[col, rows, :] = value
-            if row == 0:
-                back_ref[4 + col, 0:16, :] = value[0:16, :]
-            if row == REGION - 1:
-                ahead_ref[4 + col, 0:16, :] = value[48:64, :]
+            masked_ref[col, rows, :] = jnp.where(wet, sea[rows, lanes], 0.0)
         masked_ref[col, OWN_ROWS:PACK_ROWS, :] = jnp.zeros((PACK_ROWS - OWN_ROWS, LANES), jnp.float32)
 
-    for slot in range(SLOTS):
-        copies[slot].wait()
-        totals = [jnp.zeros((16, LANES), jnp.float32) for _ in range(ROWS // 16)]
-        for level in range(LEVELS):
-            weight = thick_ref[level]
-            for tile in range(ROWS // 16):
-                part = levels[slot, level, tile * 16 : tile * 16 + 16, :].astype(jnp.float32)
-                totals[tile] = totals[tile] + part * weight
-        if slot >= KEPT:
-            for tile, value in enumerate(totals):
-                moved_ref[slot - KEPT, tile * 16 : tile * 16 + 16, :] = value
-                half = slice(tile % 2 * 16, tile % 2 * 16 + 16)
-                ahead_ref[(slot - KEPT) * 2 + tile // 2, half, :] = value
-            bottom_ref[slot - KEPT] = totals[-1]
+
+def forcing_kernel(
+    thick_in, owner_in, tend_ref, masked_ref, moved_ref,
+    inner_ref, outer_ref, source_ref,
+    thick_ref, owner_ref, pair, table_sem,
+):
+    tables = []
+    for index, (table_in, table_ref) in enumerate(((thick_in, thick_ref), (owner_in, owner_ref))):
+        copy = pltpu.make_async_copy(table_in, table_ref, table_sem.at[index])
+        copy.start()
+        tables.append(copy)
+    myself = lax.axis_index("bx") * 8 + lax.axis_index("by")
+    upper = lax.broadcasted_iota(jnp.int32, (8, LANES), 0) < 4
+    odd = lax.axis_index("by") % 2
+    ahead_ref, back_ref = pair.at[odd], pair.at[1 - odd]
+    source_ref[...] = jnp.zeros(source_ref.shape, jnp.float32)
+    for copy in tables:
+        copy.wait()
+
+    def put(slot, totals):
         region, row, col = place(owner_ref[myself * SLOTS + slot])
 
         @pl.when(region == myself)
@@ -121,28 +132,40 @@
                 first = pl.multiple_of(row * ROWS + tile * 16, 16)
                 source_ref[col, pl.ds(first, 16), :] = value
 
-        @pl.when((region == myself) & (row == 0))
-        def _():
-            back_ref[4 + col, 16:32, :] = totals[0]
-
-        @pl.when((region == myself) & (row == REGION - 1))
-        def _():
-            ahead_ref[4 + col, 16:32, :] = totals[-1]
-
+    for slot in range(KEPT):
+        put(slot, level_sum(tend_ref, slot, thick_ref))
+    for extra in range(MOVE):
+        put(KEPT + extra, [moved_ref[extra, 16 * tile : 16 * tile + 16, :] for tile in range(4)])
+
+    for col in range(REGION):
+        back_ref[col, 0:8, :] = masked_ref[col, 0:8, :]
+        back_ref[col, 8:16, :] = source_ref[col, 0:8, :]
+        back_ref[col, 16:24, :] = jnp.where(
+            upper, masked_ref[col, 8:16, :], rolled(source_ref[col, 8:16, :], 4, 0)
+        )
+        last = OWN_ROWS - 8
+        ahead_ref[col, 0:8, :] = masked_ref[col, last:OWN_ROWS, :]
+        ahead_ref[col, 8:16, :] = source_ref[col, last:OWN_ROWS, :]
+        ahead_ref[col, 16:24, :] = jnp.where(
+            upper, rolled(source_ref[col, last - 8 : last, :], 4, 0), masked_ref[col, last - 8 : last, :]
+        )
     inner_ref[...] = pair[0]
     outer_ref[...] = pair[1]
 
 
 def gather_kernel(
-    owner_ref, source_in, masked_in, moved_ref, inner_ref, outer_ref, two_ref, three_ref,
+    owner_ref, source_in, masked_in, moved_ref, inner_ref, outer_ref, mixed_ref, two_ref, passed_two_ref,
     source_ref, masked_ref, inner_side_ref, outer_side_ref,
-    pair,
+    pair, held,
 ):
     del source_in, masked_in
     pair[0] = inner_ref[...]
     pair[1] = outer_ref[...]
     odd = lax.axis_index("by") % 2
-    one_ref, under_ref = pair.at[1 - odd], pair.at[odd]
+    over_ref, under_ref = pair.at[1 - odd], pair.at[odd]
+    held[0] = mixed_ref[...]
+    held[1] = passed_two_ref[...]
+    one_ref, three_ref = held.at[1 - odd], held.at[odd]
     row_index = lax.axis_index("by")
     myself = lax.axis_index("bx") * 8 + row_index
     end = OWN_ROWS + 8
@@ -152,18 +175,18 @@
     not_south = row_index == 7
     not_north = row_index == 0
     for col in range(REGION):
-        south_ref = under_ref.at[4 + col]
-        south = [jnp.where(not_south, 0.0, south_ref[8 * i : 8 * i + 8, :]) for i in range(2)]
-        north_ref = one_ref.at[4 + col]
-        north = [jnp.where(not_north, 0.0, north_ref[8 * i : 8 * i + 8, :]) for i in range(2)]
+        def take(ref, missing):
+            depth = [jnp.where(missing, 0.0, ref[col, rows, :]) for rows in (slice(0, 8), slice(16, 24))]
+            return depth, [ref[col, 8:16, :], rolled(ref[col, 16:24, :], 4, 0)]
+
+        south, below = take(under_ref, not_south)
+        north, above = take(over_ref, not_north)
         masked_ref[col, OWN_ROWS:end, :] = south[0]
-        masked_ref[col, end : end + 8, :] = jnp.where(upper, south[1], north[0])
-        masked_ref[col, end + 8 : end + 16, :] = north[1]
-        source_ref[col, OWN_ROWS:end, :] = south_ref[16:24, :]
-        source_ref[col, end : end + 8, :] = jnp.where(
-            upper, south_ref[24:32, :], north_ref[16:24, :]
-        )
-        source_ref[col, end + 8 : end + 16, :] = north_ref[24:32, :]
+        masked_ref[col, end : end + 8, :] = jnp.where(upper, south[1], north[1])
+        masked_ref[col, end + 8 : end + 16, :] = north[0]
+        source_ref[col, OWN_ROWS:end, :] = below[0]
+        source_ref[col, end : end + 8, :] = jnp.where(upper, below[1], above[1])
+        source_ref[col, end + 8 : end + 16, :] = above[0]
 
     def spread(sender, slot, block, bottom, inside=True, above=True, below=True):
         region, row, col = place(owner_ref[sender * SLOTS + slot])
@@ -172,15 +195,15 @@
             @pl.when(region == myself)
             def _():
                 first = pl.multiple_of(row * ROWS, ROWS)
-                source_ref[col, pl.ds(first, ROWS), :] = block[...].reshape(ROWS, LANES)
+                source_ref[col, pl.ds(first, ROWS), :] = block[...]
 
         if below:
 
             @pl.when((region == myself + 1) & (row == 0))
             def _():
-                source_ref[col, OWN_ROWS:end, :] = block[0, 0:8, :]
+                source_ref[col, OWN_ROWS:end, :] = block[0:8, :]
                 mixed = source_ref[col, end : end + 8, :]
-                source_ref[col, end : end + 8, :] = jnp.where(upper, block[0, 8:16, :], mixed)
+                source_ref[col, end : end + 8, :] = jnp.where(upper, block[8:16, :], mixed)
 
         if above:
 
@@ -192,13 +215,13 @@
 
     for extra in range(MOVE):
         slot = KEPT + extra
-        block = moved_ref.at[extra : extra + 1]
+        block = moved_ref.at[extra]
         spread(myself, slot, block, None, inside=False, above=False)
-        block = one_ref.at[2 * extra : 2 * extra + 2]
+        block = one_ref.at[extra]
         spread((myself + 127) % 128, slot, block, None, above=False)
-        block = two_ref.at[extra : extra + 1]
-        spread((myself + 126) % 128, slot, block, block.at[0, 48:64, :], below=False)
-        spread((myself + 125) % 128, slot, None, three_ref.at[extra], inside=False, below=False)
+        block = two_ref.at[extra]
+        spread((myself + 126) % 128, slot, block, block.at[48:64, :], below=False)
+        spread((myself + 125) % 128, slot, None, three_ref.at[extra, 48:64, :], inside=False, below=False)
 
     even = lax.axis_index("bx") % 2 == 0
     for row in range(FOLD // 8):
@@ -264,12 +287,11 @@
                 self.diagonal[k, col] = inv * (surface_term + around[col])
                 self.residual[k, col] = start
                 self.direction[k, col] = opening * start
-                self.total[k, col] = opening * start
 
     def below(self, ref, k):
         return self.load(ref, k + 1) if k + 1 < CHUNK else turn(self.load(ref, 0), -1)
 
-    def sweep(self, index, final=None):
+    def sweep(self, index, add, final=None):
         carry_scale, forward_scale = self.scale_ref[index, 0], self.scale_ref[index, 1]
         above = turn(self.load(self.direction, CHUNK - 1), 1)
         for k in range(CHUNK):
@@ -285,17 +307,26 @@
                 rest = self.residual[k, col] - self.diagonal[k, col] * here
                 rest = rest + self.inverse[k, col] * back[col]
                 turned = carry_scale * here + forward_scale * rest
-                summed = self.total[k, col] + turned
-                if final is not None:
-                    final(k, col, summed)
-                else:
+                if add == "first":
+                    self.total[k, col] = here + turned
+                elif final is not None:
+                    final(k, col, self.total[k, col] + (here + turned))
+                elif add:
+                    self.total[k, col] = self.total[k, col] + (here + turned)
+                if final is None:
                     self.residual[k, col] = rest
                     self.direction[k, col] = turned
-                    self.total[k, col] = summed
 
     def solve(self, final):
-        lax.fori_loop(0, ITERS - 2, lambda index, _: self.sweep(index), None)
-        self.sweep(ITERS - 2, final)
+        self.sweep(0, "first")
+
+        def two_sweeps(pair, _):
+            self.sweep(2 * pair + 1, False)
+            self.sweep(2 * pair + 2, True)
+
+        lax.fori_loop(0, ITERS // 2 - 2, two_sweeps, None, unroll=self.cols == 1)
+        self.sweep(ITERS - 3, False)
+        self.sweep(ITERS - 2, True, final)
 
 
 def join(f, *rows):
@@ -374,9 +405,10 @@
         tail_ref[extra] = out_ref[KEPT + extra]
 
 
-def tail_kernel(heights_ref, tail_ref, one_ref, two_ref, out_ref, joined, sem):
+def tail_kernel(heights_ref, tail_ref, passed_ref, back_ref, out_ref, joined, sem):
     del heights_ref
-    joined[...] = tail_ref[...] + (one_ref[...] + two_ref[...])
+    even = lax.axis_index("by") % 2 == 0
+    joined[...] = tail_ref[...] + (jnp.where(even, passed_ref[...], 0.0) + back_ref[...])
     copy = pltpu.make_async_copy(joined, out_ref.at[pl.ds(KEPT, MOVE)], sem)
     copy.start()
     copy.wait()
@@ -386,10 +418,9 @@
     return pl.BlockSpec(memory_space=space)
 
 
-def ring(value, steps, senders=range(8)):
+def ring(value, steps):
     count = lax.axis_size("bx") * lax.axis_size("by")
-    pairs = [(i, (i + steps) % count) for i in range(count) if i % 8 in senders]
-    return lax.ppermute(value, ("bx", "by"), pairs)
+    return lax.ppermute(value, ("bx", "by"), [(i, (i + steps) % count) for i in range(count)])
 
 
 def inner_swap(value, axis):
@@ -402,10 +433,22 @@
     return lax.ppermute(value, axis, pairs)
 
 
-def outer_ring_swap(value):
+def outer_row_swap(value):
+    rows, count = lax.axis_size("by"), lax.axis_size("bx") * lax.axis_size("by")
+    pairs = []
+    for i in range(count):
+        row, col = i % rows, i // rows
+        if row in (0, rows - 1):
+            pairs.append((i, (col ^ 1) * rows + row))
+        else:
+            pairs.append((i, i + 1 if row % 2 else i - 1))
+    return lax.ppermute(value, ("bx", "by"), pairs)
+
+
+def mixed_ring(value):
     count = lax.axis_size("bx") * lax.axis_size("by")
-    pairs = [(i, (i + 1) % count) for i in range(1, count, 2)]
-    pairs += [(i, i - 1) for i in range(0, count, 2) if i % 8]
+    pairs = [(i, (i + (3 if i % 2 else 1)) % count) for i in range(count)]
+    pairs = [(i, i - 5 if i % 8 == 5 else j) for i, j in pairs]
     return lax.ppermute(value, ("bx", "by"), pairs)
 
 
@@ -419,53 +462,61 @@
 
 def on_device(tendency, thickness, depth, block_owner, block_mask, ocean_counts):
     f32 = jnp.float32
-    params = pltpu.CompilerParams(vmem_limit_bytes=32 << 20)
+    params = pltpu.CompilerParams(vmem_limit_bytes=16 << 20)
     far = pl.BlockSpec(memory_space=HBM)
 
     def here(*dims):
         return pltpu.VMEM(dims, f32)
 
     field = (REGION, PACK_ROWS, LANES)
-    inner, outer, moved, bottom, source, masked = pl.pallas_call(
+    tables = [distant(x) for x in (thickness, ocean_counts, block_mask)]
+    moved, masked = pl.pallas_call(
+        moved_kernel,
+        in_specs=[far] * 5,
+        out_specs=[whole()] * 2,
+        out_shape=[here(MOVE, ROWS, LANES), here(*field)],
+        scratch_shapes=[
+            pltpu.SMEM(thickness.shape, f32),
+            pltpu.SMEM(ocean_counts.shape, jnp.int32),
+            pltpu.SMEM(block_mask.shape, jnp.int32),
+            pltpu.VMEM((MOVE, LEVELS, ROWS, LANES), jnp.bfloat16),
+            here(OWN_ROWS, REGION * LANES),
+            pltpu.SemaphoreType.DMA((3,)),
+            pltpu.SemaphoreType.DMA((MOVE,)),
+            pltpu.SemaphoreType.DMA,
+        ],
+        compiler_params=params,
+        name="moved",
+    )(*tables, distant(tendency), distant(depth))
+    two = ring(moved, 2)
+    mixed = mixed_ring(moved)
+    inner, outer, source = pl.pallas_call(
         forcing_kernel,
-        in_specs=[far] * 6,
-        out_specs=[whole()] * 6,
-        out_shape=[
-            here(8, 32, LANES),
-            here(8, 32, LANES),
-            here(MOVE, ROWS, LANES),
-            here(MOVE, 16, LANES),
-            here(*field),
-            here(*field),
-        ],
+        in_specs=[far] * 2 + [whole()] * 3,
+        out_specs=[whole()] * 3,
+        out_shape=[here(REGION, 24, LANES), here(REGION, 24, LANES), here(*field)],
         scratch_shapes=[
             pltpu.SMEM(thickness.shape, f32),
             pltpu.SMEM(block_owner.shape, jnp.int32),
-            pltpu.SMEM(ocean_counts.shape, jnp.int32),
-            pltpu.SMEM(block_mask.shape, jnp.int32),
-            here(2, 8, 32, LANES),
-            pltpu.VMEM((SLOTS, LEVELS, ROWS, LANES), jnp.bfloat16),
-            pltpu.VMEM((OWN_ROWS, REGION * LANES), f32),
-            pltpu.SemaphoreType.DMA((4,)),
-            pltpu.SemaphoreType.DMA((SLOTS,)),
-            pltpu.SemaphoreType.DMA,
+            here(2, REGION, 24, LANES),
+            pltpu.SemaphoreType.DMA((2,)),
         ],
         compiler_params=params,
         name="forcing",
-    )(*map(distant, (thickness, block_owner, ocean_counts, block_mask, tendency, depth)))
-    outer = outer_ring_swap(outer)
-    two = ring(moved, 2)
-    three = ring(bottom, 3, (0, 1, 2, 3, 4, 6, 7))
+    )(distant(thickness), distant(block_owner), near(tendency), near(masked), near(moved))
+    late_two, _ = lax.optimization_barrier((two, inner))
+    outer = outer_row_swap(outer)
     inner = inner_swap(inner, "by")
-
-    inputs = [near(x) for x in (source, masked, moved, inner, outer, two, three)]
+    passed_two = inner_swap(late_two, "by")
+
+    inputs = [near(x) for x in (source, masked, moved, inner, outer, mixed, two, passed_two)]
     source, masked, inner, outer = pl.pallas_call(
         gather_kernel,
-        in_specs=[whole(SMEM)] + [whole()] * 7,
+        in_specs=[whole(SMEM)] + [whole()] * 8,
         out_specs=[whole()] * 4,
         out_shape=[here(*field), here(*field), here(FOLD, LANES), here(FOLD, LANES)],
         input_output_aliases={1: 0, 2: 1},
-        scratch_shapes=[here(2, 8, 32, LANES)],
+        scratch_shapes=[here(2, REGION, 24, LANES), here(2, MOVE, ROWS, LANES)],
         compiler_params=params,
         name="assemble",
     )(block_owner, *inputs)
@@ -497,7 +548,9 @@
         compiler_params=params,
         name="sides",
     )(block_owner, scales, *inputs)
-    back = ring(first, -1), ring(second, -2)
+    passed = inner_swap(first, "by")
+    odd = lax.axis_index("by") % 2 == 1
+    back = ring(jnp.where(odd, second + passed, second), -2)
 
     out, tail = pl.pallas_call(
         write_kernel,
@@ -516,7 +569,7 @@
         scratch_shapes=[here(MOVE, ROWS, LANES), pltpu.SemaphoreType.DMA],
         compiler_params=params,
         name="tail",
-    )(out, near(tail), near(back[0]), near(back[1]))
+    )(out, near(tail), near(passed), near(back))
 
 
 def solution(mesh):

time: 39.1 us -> 36.4 us (0.931)
  starting transfers between devices: 15.8 us -> 14.1 us
  Pallas kernels: 16.9 us -> 15.2 us
  waiting for transfers between devices: 6.15 us -> 6.8 us
    ppermute x5 -> x4, starting transfers between devices: 12.1 us -> 9.15 us  [the longest x2 5.01 us: ring(): lax.ppermute(value, ('bx', 'by'), [(i, (i + steps) % count) for i in rang...]
    ppermute x2 -> x4, waiting for transfers between devices: 0.01 us -> 2.13 us  [inner_swap(): lax.ppermute(value, axis, [(i, i ^ 1) for i in range(lax.axis_size(axis))])]
    ppermute x5 -> x4, waiting for transfers between devices: 6.14 us -> 4.67 us  [the longest x1 2.58 us: outer_row_swap(): return lax.ppermute(value, ('bx', 'by'), pairs)]
    pallas_call x2 -> x3, Pallas kernels: 6.3 us -> 4.98 us  [the longest x1 2.18 us: on_device(): pl.pallas_call(forcing_kernel, in_specs=[far] * 2 + [whole()] * 3, out_sp...]
    ppermute x2 -> x4, starting transfers between devices: 1.59 us -> 2.67 us  [inner_swap(): lax.ppermute(value, axis, [(i, i ^ 1) for i in range(lax.axis_size(axis))])]
  transfers between devices with their start and end apart: 8 -> 9, of which waited for: 1 -> 4; matrix products, arithmetic and copies ran while one was open for 0% -> 0% of each run, Pallas kernels for 18% -> 25%
where the time goes in v4:
time: 36.4 us; the launch traced here: 36.2 us
  Pallas kernels  15.2 us (42%)
  starting transfers between devices  14.1 us (39%)
  waiting for transfers between devices  6.8 us (19%)
    pallas_call x1, Pallas kernels, on_device(): pl.pallas_call(region_kernel, in_specs=[whole(SMEM)] + [whole()] * 2, out...  5.15 us
    ppermute x2, starting transfers between devices, ring(): lax.ppermute(value, ('bx', 'by'), [(i, (i + steps) % count) for i in rang...  5.01 us
    ppermute x1, starting transfers between devices, mixed_ring(): return lax.ppermute(value, ('bx', 'by'), pairs)  4.14 us
    pallas_call x1, Pallas kernels, on_device(): pl.pallas_call(sides_kernel, in_specs=[whole(SMEM)] * 2 + [whole()] * 5,...  2.78 us
    ppermute x4, starting transfers between devices, inner_swap(): lax.ppermute(value, axis, [(i, i ^ 1) for i in range(lax.axis_size(axis))])  2.67 us
    ppermute x1, waiting for transfers between devices, outer_row_swap(): return lax.ppermute(value, ('bx', 'by'), pairs)  2.58 us
    ppermute x1, starting transfers between devices, outer_swap(): return lax.ppermute(value, axis, pairs)  2.33 us
    pallas_call x1, Pallas kernels, on_device(): pl.pallas_call(forcing_kernel, in_specs=[far] * 2 + [whole()] * 3, out_sp...  2.18 us
  transfers between devices with their start and end apart: 9, of which 4 were waited for; matrix products, arithmetic and copies ran while one was open for 0% of the time, Pallas kernels for 25%

profile of v4, /device:TPU:1, one launch (start us, length us, event | category | flops | bytes accessed | tf_op | source)
XLA Modules:
  0.0 36.2 jit_solution(17339704447347921111)
XLA Ops:
  0.0 0.0 copy-start.2
  0.0 0.0 copy-start
  0.0 0.0 copy-start.1
  0.0 1.7 %moved.1 = (f32[2,64,128]{2,1,0:T(8,128)S(1)}, f32[4,288,128]{2,1,0:T(8,128)S(1)}) custom-call(f32[40]{0:T(128)} %thick_in.3, s32[4,4]{1,0:T(4,128)} %count_in.1, s32[4,4]{1,0:T(4,128)} %mask_in.1, bf16[12,40,64,128]{3,2,1,0:T(8,128)(2,1)} %tend_ref.3, f32[256,512]{1,0:T(8,128)} %depth_ref.1), custom_call_target="tpu_custom_call" | custom-call | tf_op jit(solution)/shard_map/moved/pallas_call | solution.py:473
  1.7 2.5 %collective-permute-start.3 = (f32[2,64,128]{2,1,0:T(8,128)S(1)}, f32[2,64,128]{2,1,0:T(8,128)S(1)}, u32[]{:S(2)}, u32[]{:S(2)}) collective-permute-start(f32[2,64,128]{2,1,0:T(8,128)S(1)} %get-tuple-element.21.moved_ref), channel_id=1, source_target_pairs={{0,2},{1,3},{2,4},{3,5},{4,6},{5,7},{6,8},{7,9},{8,10},{9,11},{10,... | collective-permute-start | bytes 196616 | tf_op jit(solution)/shard_map/ppermute | solution.py:423
  4.3 4.1 %collective-permute-start.2 = (f32[2,64,128]{2,1,0:T(8,128)S(1)}, f32[2,64,128]{2,1,0:T(8,128)S(1)}, u32[]{:S(2)}, u32[]{:S(2)}) collective-permute-start(f32[2,64,128]{2,1,0:T(8,128)S(1)} %get-tuple-element.21.moved_ref), channel_id=1, source_target_pairs={{0,1},{1,4},{2,3},{3,6},{4,5},{5,0},{6,7},{7,10},{8,9},{9,12},{10,... | collective-permute-start | bytes 196616 | tf_op jit(solution)/shard_map/ppermute | solution.py:452
  8.4 0.0 copy-done
  8.4 2.2 %forcing.1 = (f32[4,24,128]{2,1,0:T(8,128)S(1)}, f32[4,24,128]{2,1,0:T(8,128)S(1)}, f32[4,288,128]{2,1,0:T(8,128)S(1)}) custom-call(f32[40]{0:T(128)} %thick_in.3, s32[1536]{0:T(1024)} %owner_ref.5, bf16[12,40,64,128]{3,2,1,0:T(8,128)(2,1)S(1)} %copy-done, f32[4,288,128]{2,1,0:T(8,128)S(1)} %get-tuple-element.20.masked_ref.masked_in, ...), custom_call_target="tpu_custom_call" | custom-call | tf_op jit(solution)/shard_map/forcing/pallas_call | solution.py:493
  10.6 2.1 %collective-permute-done.3.two_ref = f32[2,64,128]{2,1,0:T(8,128)S(1)} collective-permute-done((f32[2,64,128]{2,1,0:T(8,128)S(1)}, f32[2,64,128]{2,1,0:T(8,128)S(1)}, u32[]{:S(2)}, u32[]{:S(2)}) %collective-permute-start.3) | collective-permute-done | bytes 65568 | tf_op jit(solution)/shard_map/ppermute | solution.py:423
  12.7 1.5 %collective-permute-start.4 = (f32[2,64,128]{2,1,0:T(8,128)S(1)}, f32[2,64,128]{2,1,0:T(8,128)S(1)}, u32[]{:S(2)}, u32[]{:S(2)}) collective-permute-start(f32[2,64,128]{2,1,0:T(8,128)S(1)} %collective-permute-done.3.two_ref), channel_id=1, source_target_pairs={{0,1},{1,0},{2,3},{3,2},{4,5},{5,4},{6,7},{7,6},{8,9},{9,8},{10,11... | collective-permute-start | bytes 196616 | tf_op jit(solution)/shard_map/ppermute | solution.py:427
  14.2 0.0 collective-permute-start
  14.2 0.0 collective-permute-start.1
  14.2 1.2 %collective-permute-done.inner_ref = f32[4,24,128]{2,1,0:T(8,128)S(1)} collective-permute-done((f32[4,24,128]{2,1,0:T(8,128)S(1)}, f32[4,24,128]{2,1,0:T(8,128)S(1)}, u32[]{:S(2)}, u32[]{:S(2)}) %collective-permute-start) | collective-permute-done | bytes 49184 | tf_op jit(solution)/shard_map/ppermute | solution.py:427
  15.4 2.6 %collective-permute-done.1.outer_ref = f32[4,24,128]{2,1,0:T(8,128)S(1)} collective-permute-done((f32[4,24,128]{2,1,0:T(8,128)S(1)}, f32[4,24,128]{2,1,0:T(8,128)S(1)}, u32[]{:S(2)}, u32[]{:S(2)}) %collective-permute-start.1) | collective-permute-done | bytes 49184 | tf_op jit(solution)/shard_map/ppermute | solution.py:445
  18.0 0.0 collective-permute-done.2.mixed_ref
  18.0 0.0 collective-permute-done.4.passed_two_ref
  18.0 0.0 copy-done.1
  18.0 1.1 %assemble.1 = (f32[4,288,128]{2,1,0:T(8,128)S(1)}, f32[4,288,128]{2,1,0:T(8,128)S(1)}, f32[72,128]{1,0:T(8,128)S(1)}, f32[72,128]{1,0:T(8,128)S(1)}) custom-call(s32[1536]{0:T(1024)S(1)} %copy-done.1, f32[4,288,128]{2,1,0:T(8,128)S(1)} %get-tuple-element.22.source_in, ...), custom_call_target="tpu_custom_call", output_to_operand_aliasing={{0}: (1, {}), {1}: (2, {})} | custom-call | tf_op jit(solution)/shard_map/assemble/pallas_call | solution.py:513
  19.1 0.1 collective-permute-start.5
  19.2 2.3 %collective-permute-start.6 = (f32[72,128]{1,0:T(8,128)S(1)}, f32[72,128]{1,0:T(8,128)S(1)}, u32[]{:S(2)}, u32[]{:S(2)}) collective-permute-start(f32[72,128]{1,0:T(8,128)S(1)} %get-tuple-element.29), channel_id=1, source_target_pairs={{0,120},{8,16},{16,8},{24,32},{32,24},{40,48},{48,40},{56,64},{64,... | collective-permute-start | bytes 110600 | tf_op jit(solution)/shard_map/ppermute | solution.py:433
  21.6 0.0 copy-done.2
  21.6 5.2 %region.1.standard_in = f32[4,280,128]{2,1,0:T(8,128)S(1)} custom-call(f32[10,2]{1,0:T(8,128)S(1)} %copy-done.2, f32[4,288,128]{2,1,0:T(8,128)S(1)} %get-tuple-element.26.source_ref, f32[4,288,128]{2,1,0:T(8,128)S(1)} %get-tuple-element.27.masked_ref), custom_call_target="tpu_custom_call" | custom-call | tf_op jit(solution)/shard_map/region/pallas_call | solution.py:526
  26.7 0.0 collective-permute-done.5.inner_ref
  26.7 0.0 collective-permute-done.6.outer_ref
  26.8 2.8 %sides.1 = (f32[4,280,128]{2,1,0:T(8,128)S(1)}, f32[2,64,128]{2,1,0:T(8,128)S(1)}, f32[2,64,128]{2,1,0:T(8,128)S(1)}) custom-call(s32[1536]{0:T(1024)S(1)} %copy-done.1, f32[10,2]{1,0:T(8,128)S(1)} %copy-done.2, f32[4,280,128]{2,1,0:T(8,128)S(1)} %region.1.standard_in, ...), custom_call_target="tpu_custom_call", output_to_operand_aliasing={{0}: (2, {})} | custom-call | tf_op jit(solution)/shard_map/sides/pallas_call | solution.py:537
  29.5 1.0 %collective-permute-start.7 = (f32[2,64,128]{2,1,0:T(8,128)S(1)}, f32[2,64,128]{2,1,0:T(8,128)S(1)}, u32[]{:S(2)}, u32[]{:S(2)}) collective-permute-start(f32[2,64,128]{2,1,0:T(8,128)S(1)} %get-tuple-element.33), channel_id=1, source_target_pairs={{0,1},{1,0},{2,3},{3,2},{4,5},{5,4},{6,7},{7,6},{8,9},{9,8},{10,11... | collective-permute-start | bytes 196616 | tf_op jit(solution)/shard_map/ppermute | solution.py:427
  30.6 0.9 %collective-permute-done.7.passed_ref = f32[2,64,128]{2,1,0:T(8,128)S(1)} collective-permute-done((f32[2,64,128]{2,1,0:T(8,128)S(1)}, f32[2,64,128]{2,1,0:T(8,128)S(1)}, u32[]{:S(2)}, u32[]{:S(2)}) %collective-permute-start.7) | collective-permute-done | bytes 65568 | tf_op jit(solution)/shard_map/ppermute | solution.py:427
  31.5 2.5 %collective-permute-start.8 = (f32[2,64,128]{2,1,0:T(8,128)S(1)}, f32[2,64,128]{2,1,0:T(8,128)S(1)}, u32[]{:S(2)}, u32[]{:S(2)}) collective-permute-start(f32[2,64,128]{2,1,0:T(8,128)S(1)} %add_select_fusion), channel_id=1, source_target_pairs={{0,126},{1,127},{2,0},{3,1},{4,2},{5,3},{6,4},{7,5},{8,6},{9,7},{1... | collective-permute-start | bytes 196616 | tf_op jit(solution)/shard_map/ppermute | solution.py:423
  34.0 1.6 %write.1 = (f32[12,64,128]{2,1,0:T(8,128)}, f32[2,64,128]{2,1,0:T(8,128)S(1)}) custom-call(s32[1536]{0:T(1024)S(1)} %copy-done.1, f32[4,280,128]{2,1,0:T(8,128)S(1)} %get-tuple-element.30.standard), custom_call_target="tpu_custom_call" | custom-call | tf_op jit(solution)/shard_map/write/pallas_call | solution.py:555
  35.6 0.0 collective-permute-done.8.back_ref
  35.6 0.7 %tail.1 = f32[12,64,128]{2,1,0:T(8,128)} custom-call(f32[12,64,128]{2,1,0:T(8,128)} %get-tuple-element.31.heights_ref, f32[2,64,128]{2,1,0:T(8,128)S(1)} %get-tuple-element.32.tail_ref, f32[2,64,128]{2,1,0:T(8,128)S(1)} %collective-permute-done.7.passed_ref, f32[2,64,128]{2,1,0:T(8,128)S(1)} %collective-permute-done.8.back_ref), custom_call_target="tpu_custom_call", output_to_operand_aliasing={{}: (0, {})} | custom-call | tf_op jit(solution)/shard_map/tail/pallas_call | solution.py:563
  (1 shorter events, 0.0 us)
Async XLA Ops:
  0.0 21.6 %copy-start.2 = (f32[10,2]{1,0:T(8,128)S(1)}, f32[10,2]{1,0:T(8,128)}, u32[]{:S(2)}) copy-start(f32[10,2]{1,0:T(8,128)} %constant.20.clone.scale_ref) | copy-start | bytes 244
  0.0 8.4 %copy-start = (bf16[12,40,64,128]{3,2,1,0:T(8,128)(2,1)S(1)}, bf16[12,40,64,128]{3,2,1,0:T(8,128)(2,1)}, u32[]{:S(2)}) copy-start(bf16[12,40,64,128]{3,2,1,0:T(8,128)(2,1)} %tend_ref.3) | copy-start | bytes 23592964
  0.0 18.0 %copy-start.1 = (s32[1536]{0:T(1024)S(1)}, s32[1536]{0:T(1024)}, u32[]{:S(2)}) copy-start(s32[1536]{0:T(1024)} %owner_ref.5) | copy-start | bytes 18436
  1.7 11.0 %collective-permute-start.3 = (f32[2,64,128]{2,1,0:T(8,128)S(1)}, f32[2,64,128]{2,1,0:T(8,128)S(1)}, u32[]{:S(2)}, u32[]{:S(2)}) collective-permute-start(f32[2,64,128]{2,1,0:T(8,128)S(1)} %get-tuple-element.21.moved_ref), channel_id=1, source_target_pairs={{0,2},{1,3},{2,4},{3,5},{4,6},{5,7},{6,8},{7,9},{8,10},{9,11},{10,... | collective-permute-start | bytes 196616 | tf_op jit(solution)/shard_map/ppermute | solution.py:423
  4.3 13.8 %collective-permute-start.2 = (f32[2,64,128]{2,1,0:T(8,128)S(1)}, f32[2,64,128]{2,1,0:T(8,128)S(1)}, u32[]{:S(2)}, u32[]{:S(2)}) collective-permute-start(f32[2,64,128]{2,1,0:T(8,128)S(1)} %get-tuple-element.21.moved_ref), channel_id=1, source_target_pairs={{0,1},{1,4},{2,3},{3,6},{4,5},{5,0},{6,7},{7,10},{8,9},{9,12},{10,... | collective-permute-start | bytes 196616 | tf_op jit(solution)/shard_map/ppermute | solution.py:452
  12.7 5.4 %collective-permute-start.4 = (f32[2,64,128]{2,1,0:T(8,128)S(1)}, f32[2,64,128]{2,1,0:T(8,128)S(1)}, u32[]{:S(2)}, u32[]{:S(2)}) collective-permute-start(f32[2,64,128]{2,1,0:T(8,128)S(1)} %collective-permute-done.3.two_ref), channel_id=1, source_target_pairs={{0,1},{1,0},{2,3},{3,2},{4,5},{5,4},{6,7},{7,6},{8,9},{9,8},{10,11... | collective-permute-start | bytes 196616 | tf_op jit(solution)/shard_map/ppermute | solution.py:427
  14.2 1.2 %collective-permute-start = (f32[4,24,128]{2,1,0:T(8,128)S(1)}, f32[4,24,128]{2,1,0:T(8,128)S(1)}, u32[]{:S(2)}, u32[]{:S(2)}) collective-permute-start(f32[4,24,128]{2,1,0:T(8,128)S(1)} %get-tuple-element.23), channel_id=1, source_target_pairs={{0,1},{1,0},{2,3},{3,2},{4,5},{5,4},{6,7},{7,6},{8,9},{9,8},{10,11... | collective-permute-start | bytes 147464 | tf_op jit(solution)/shard_map/ppermute | solution.py:427
  14.2 3.8 %collective-permute-start.1 = (f32[4,24,128]{2,1,0:T(8,128)S(1)}, f32[4,24,128]{2,1,0:T(8,128)S(1)}, u32[]{:S(2)}, u32[]{:S(2)}) collective-permute-start(f32[4,24,128]{2,1,0:T(8,128)S(1)} %get-tuple-element.24), channel_id=1, source_target_pairs={{0,8},{1,2},{2,1},{3,4},{4,3},{5,6},{6,5},{7,15},{8,0},{9,10},{10,... | collective-permute-start | bytes 147464 | tf_op jit(solution)/shard_map/ppermute | solution.py:445
  19.1 7.6 %collective-permute-start.5 = (f32[72,128]{1,0:T(8,128)S(1)}, f32[72,128]{1,0:T(8,128)S(1)}, u32[]{:S(2)}, u32[]{:S(2)}) collective-permute-start(f32[72,128]{1,0:T(8,128)S(1)} %get-tuple-element.28), channel_id=1, source_target_pairs={{0,8},{8,0},{16,24},{24,16},{32,40},{40,32},{48,56},{56,48},{64,72... | collective-permute-start | bytes 110600 | tf_op jit(solution)/shard_map/ppermute | solution.py:427
  19.2 7.5 %collective-permute-start.6 = (f32[72,128]{1,0:T(8,128)S(1)}, f32[72,128]{1,0:T(8,128)S(1)}, u32[]{:S(2)}, u32[]{:S(2)}) collective-permute-start(f32[72,128]{1,0:T(8,128)S(1)} %get-tuple-element.29), channel_id=1, source_target_pairs={{0,120},{8,16},{16,8},{24,32},{32,24},{40,48},{48,40},{56,64},{64,... | collective-permute-start | bytes 110600 | tf_op jit(solution)/shard_map/ppermute | solution.py:433
  29.5 1.9 %collective-permute-start.7 = (f32[2,64,128]{2,1,0:T(8,128)S(1)}, f32[2,64,128]{2,1,0:T(8,128)S(1)}, u32[]{:S(2)}, u32[]{:S(2)}) collective-permute-start(f32[2,64,128]{2,1,0:T(8,128)S(1)} %get-tuple-element.33), channel_id=1, source_target_pairs={{0,1},{1,0},{2,3},{3,2},{4,5},{5,4},{6,7},{7,6},{8,9},{9,8},{10,11... | collective-permute-start | bytes 196616 | tf_op jit(solution)/shard_map/ppermute | solution.py:427
  31.5 4.1 %collective-permute-start.8 = (f32[2,64,128]{2,1,0:T(8,128)S(1)}, f32[2,64,128]{2,1,0:T(8,128)S(1)}, u32[]{:S(2)}, u32[]{:S(2)}) collective-permute-start(f32[2,64,128]{2,1,0:T(8,128)S(1)} %add_select_fusion), channel_id=1, source_target_pairs={{0,126},{1,127},{2,0},{3,1},{4,2},{5,3},{6,4},{7,5},{8,6},{9,7},{1... | collective-permute-start | bytes 196616 | tf_op jit(solution)/shard_map/ppermute | solution.py:423

commit v5 on v4

--- a/solution.py
+++ b/solution.py
@@ -68,17 +68,12 @@
 
 
 def moved_kernel(
-    thick_in, count_in, mask_in, tend_ref, depth_ref,
-    moved_ref, masked_ref,
-    thick_ref, count_ref, mask_ref, levels, sea, table_sem, level_sem, sea_sem,
+    thick_in, tend_ref,
+    moved_ref,
+    thick_ref, levels, table_sem, level_sem,
 ):
-    tables = []
-    for index, (table_in, table_ref) in enumerate(
-        ((thick_in, thick_ref), (count_in, count_ref), (mask_in, mask_ref))
-    ):
-        copy = pltpu.make_async_copy(table_in, table_ref, table_sem.at[index])
-        copy.start()
-        tables.append(copy)
+    table = pltpu.make_async_copy(thick_in, thick_ref, table_sem)
+    table.start()
     copies = []
     for extra in range(MOVE):
         copy = pltpu.make_async_copy(
@@ -86,15 +81,50 @@
         )
         copy.start()
         copies.append(copy)
-    sea_copy = pltpu.make_async_copy(depth_ref, sea, sea_sem)
-    sea_copy.start()
-    for copy in tables:
-        copy.wait()
+    table.wait()
     for extra in range(MOVE):
         copies[extra].wait()
         totals = level_sum(levels, extra, thick_ref)
         for tile, value in enumerate(totals):
             moved_ref[extra, tile * 16 : tile * 16 + 16, :] = value
+
+
+def forcing_kernel(
+    thick_in, owner_in, count_in, mask_in, tend_ref, depth_ref, moved_ref,
+    inner_ref, outer_ref, source_ref, masked_ref,
+    thick_ref, owner_ref, count_ref, mask_ref, sea, pair, table_sem, sea_sem,
+):
+    sea_copy = pltpu.make_async_copy(depth_ref, sea, sea_sem)
+    tables = []
+    for index, (table_in, table_ref) in enumerate(
+        ((thick_in, thick_ref), (owner_in, owner_ref), (count_in, count_ref), (mask_in, mask_ref))
+    ):
+        copy = pltpu.make_async_copy(table_in, table_ref, table_sem.at[index])
+        copy.start()
+        tables.append(copy)
+    myself = lax.axis_index("bx") * 8 + lax.axis_index("by")
+    upper = lax.broadcasted_iota(jnp.int32, (8, LANES), 0) < 4
+    odd = lax.axis_index("by") % 2
+    ahead_ref, back_ref = pair.at[odd], pair.at[1 - odd]
+    source_ref[...] = jnp.zeros(source_ref.shape, jnp.float32)
+    sea_copy.start()
+    for copy in tables:
+        copy.wait()
+
+    def put(slot, totals):
+        region, row, col = place(owner_ref[myself * SLOTS + slot])
+
+        @pl.when(region == myself)
+        def _():
+            for tile, value in enumerate(totals):
+                first = pl.multiple_of(row * ROWS + tile * 16, 16)
+                source_ref[col, pl.ds(first, 16), :] = value
+
+    for slot in range(KEPT):
+        put(slot, level_sum(tend_ref, slot, thick_ref))
+    for extra in range(MOVE):
+        put(KEPT + extra, [moved_ref[extra, 16 * tile : 16 * tile + 16, :] for tile in range(4)])
+
     sea_copy.wait()
     for col in range(REGION):
         lanes = slice(col * LANES, (col + 1) * LANES)
@@ -103,39 +133,6 @@
             wet = wetness(ROWS, count_ref[row, col], mask_ref[row, col])
             masked_ref[col, rows, :] = jnp.where(wet, sea[rows, lanes], 0.0)
         masked_ref[col, OWN_ROWS:PACK_ROWS, :] = jnp.zeros((PACK_ROWS - OWN_ROWS, LANES), jnp.float32)
-
-
-def forcing_kernel(
-    thick_in, owner_in, tend_ref, masked_ref, moved_ref,
-    inner_ref, outer_ref, source_ref,
-    thick_ref, owner_ref, pair, table_sem,
-):
-    tables = []
-    for index, (table_in, table_ref) in enumerate(((thick_in, thick_ref), (owner_in, owner_ref))):
-        copy = pltpu.make_async_copy(table_in, table_ref, table_sem.at[index])
-        copy.start()
-        tables.append(copy)
-    myself = lax.axis_index("bx") * 8 + lax.axis_index("by")
-    upper = lax.broadcasted_iota(jnp.int32, (8, LANES), 0) < 4
-    odd = lax.axis_index("by") % 2
-    ahead_ref, back_ref = pair.at[odd], pair.at[1 - odd]
-    source_ref[...] = jnp.zeros(source_ref.shape, jnp.float32)
-    for copy in tables:
-        copy.wait()
-
-    def put(slot, totals):
-        region, row, col = place(owner_ref[myself * SLOTS + slot])
-
-        @pl.when(region == myself)
-        def _():
-            for tile, value in enumerate(totals):
-                first = pl.multiple_of(row * ROWS + tile * 16, 16)
-                source_ref[col, pl.ds(first, 16), :] = value
-
-    for slot in range(KEPT):
-        put(slot, level_sum(tend_ref, slot, thick_ref))
-    for extra in range(MOVE):
-        put(KEPT + extra, [moved_ref[extra, 16 * tile : 16 * tile + 16, :] for tile in range(4)])
 
     for col in range(REGION):
         back_ref[col, 0:8, :] = masked_ref[col, 0:8, :]
@@ -469,41 +466,50 @@
         return pltpu.VMEM(dims, f32)
 
     field = (REGION, PACK_ROWS, LANES)
-    tables = [distant(x) for x in (thickness, ocean_counts, block_mask)]
-    moved, masked = pl.pallas_call(
+    moved = pl.pallas_call(
         moved_kernel,
-        in_specs=[far] * 5,
-        out_specs=[whole()] * 2,
-        out_shape=[here(MOVE, ROWS, LANES), here(*field)],
+        in_specs=[far] * 2,
+        out_specs=whole(),
+        out_shape=here(MOVE, ROWS, LANES),
         scratch_shapes=[
             pltpu.SMEM(thickness.shape, f32),
-            pltpu.SMEM(ocean_counts.shape, jnp.int32),
-            pltpu.SMEM(block_mask.shape, jnp.int32),
             pltpu.VMEM((MOVE, LEVELS, ROWS, LANES), jnp.bfloat16),
-            here(OWN_ROWS, REGION * LANES),
-            pltpu.SemaphoreType.DMA((3,)),
+            pltpu.SemaphoreType.DMA,
             pltpu.SemaphoreType.DMA((MOVE,)),
-            pltpu.SemaphoreType.DMA,
         ],
         compiler_params=params,
         name="moved",
-    )(*tables, distant(tendency), distant(depth))
+    )(distant(thickness), distant(tendency))
     two = ring(moved, 2)
     mixed = mixed_ring(moved)
-    inner, outer, source = pl.pallas_call(
+    inner, outer, source, masked = pl.pallas_call(
         forcing_kernel,
-        in_specs=[far] * 2 + [whole()] * 3,
-        out_specs=[whole()] * 3,
-        out_shape=[here(REGION, 24, LANES), here(REGION, 24, LANES), here(*field)],
+        in_specs=[far] * 4 + [whole(), far, whole()],
+        out_specs=[whole()] * 4,
+        out_shape=[
+            here(REGION, 24, LANES),
+            here(REGION, 24, LANES),
+            here(*field),
+            here(*field),
+        ],
         scratch_shapes=[
             pltpu.SMEM(thickness.shape, f32),
             pltpu.SMEM(block_owner.shape, jnp.int32),
+            pltpu.SMEM(ocean_counts.shape, jnp.int32),
+            pltpu.SMEM(block_mask.shape, jnp.int32),
+            here(OWN_ROWS, REGION * LANES),
             here(2, REGION, 24, LANES),
-            pltpu.SemaphoreType.DMA((2,)),
+            pltpu.SemaphoreType.DMA((4,)),
+            pltpu.SemaphoreType.DMA,
         ],
         compiler_params=params,
         name="forcing",
-    )(distant(thickness), distant(block_owner), near(tendency), near(masked), near(moved))
+    )(
+        *map(distant, (thickness, block_owner, ocean_counts, block_mask)),
+        near(tendency),
+        distant(depth),
+        near(moved),
+    )
     late_two, _ = lax.optimization_barrier((two, inner))
     outer = outer_row_swap(outer)
     inner = inner_swap(inner, "by")

time: 36.4 us -> 36.4 us (level)
  no operation moved by 1% of the time
where the time goes in v5:
time: 36.4 us; the launch traced here: 36.3 us
  Pallas kernels  15.2 us (42%)
  starting transfers between devices  14.3 us (39%)
  waiting for transfers between devices  6.66 us (18%)
    pallas_call x1, Pallas kernels, on_device(): pl.pallas_call(region_kernel, in_specs=[whole(SMEM)] + [whole()] * 2, out...  5.15 us
    ppermute x2, starting transfers between devices, ring(): lax.ppermute(value, ('bx', 'by'), [(i, (i + steps) % count) for i in rang...  5 us
    ppermute x1, starting transfers between devices, mixed_ring(): return lax.ppermute(value, ('bx', 'by'), pairs)  4.14 us
    pallas_call x1, Pallas kernels, on_device(): pl.pallas_call(sides_kernel, in_specs=[whole(SMEM)] * 2 + [whole()] * 5,...  2.78 us
    ppermute x4, starting transfers between devices, inner_swap(): lax.ppermute(value, axis, [(i, i ^ 1) for i in range(lax.axis_size(axis))])  2.67 us
    ppermute x1, waiting for transfers between devices, outer_row_swap(): return lax.ppermute(value, ('bx', 'by'), pairs)  2.58 us
    ppermute x1, starting transfers between devices, outer_swap(): return lax.ppermute(value, axis, pairs)  2.47 us
    pallas_call x1, Pallas kernels, on_device(): pl.pallas_call(forcing_kernel, in_specs=[far] * 4 + [whole(), far, whole(...  2.32 us
  transfers between devices with their start and end apart: 9, of which 4 were waited for; matrix products, arithmetic and copies ran while one was open for 0% of the time, Pallas kernels for 25%

profile of v5, /device:TPU:1, one launch (start us, length us, event | category | flops | bytes accessed | tf_op | source)
XLA Modules:
  0.0 36.3 jit_solution(10089574409839309654)
XLA Ops:
  0.0 0.0 copy-start.2
  0.0 0.0 copy-start
  0.0 0.0 copy-start.1
  0.0 1.6 %moved.1.moved_ref = f32[2,64,128]{2,1,0:T(8,128)S(1)} custom-call(f32[40]{0:T(128)} %thick_in.3, bf16[12,40,64,128]{3,2,1,0:T(8,128)(2,1)} %tend_ref.3), custom_call_target="tpu_custom_call" | custom-call | tf_op jit(solution)/shard_map/moved/pallas_call | solution.py:469
  1.6 2.5 %collective-permute-start.3 = (f32[2,64,128]{2,1,0:T(8,128)S(1)}, f32[2,64,128]{2,1,0:T(8,128)S(1)}, u32[]{:S(2)}, u32[]{:S(2)}) collective-permute-start(f32[2,64,128]{2,1,0:T(8,128)S(1)} %moved.1.moved_ref), channel_id=1, source_target_pairs={{0,2},{1,3},{2,4},{3,5},{4,6},{5,7},{6,8},{7,9},{8,10},{9,11},{10,... | collective-permute-start | bytes 196616 | tf_op jit(solution)/shard_map/ppermute | solution.py:420
  4.2 4.1 %collective-permute-start.2 = (f32[2,64,128]{2,1,0:T(8,128)S(1)}, f32[2,64,128]{2,1,0:T(8,128)S(1)}, u32[]{:S(2)}, u32[]{:S(2)}) collective-permute-start(f32[2,64,128]{2,1,0:T(8,128)S(1)} %moved.1.moved_ref), channel_id=1, source_target_pairs={{0,1},{1,4},{2,3},{3,6},{4,5},{5,0},{6,7},{7,10},{8,9},{9,12},{10,... | collective-permute-start | bytes 196616 | tf_op jit(solution)/shard_map/ppermute | solution.py:449
  8.3 0.0 copy-done
  8.3 2.3 %forcing.1 = (f32[4,24,128]{2,1,0:T(8,128)S(1)}, f32[4,24,128]{2,1,0:T(8,128)S(1)}, f32[4,288,128]{2,1,0:T(8,128)S(1)}, f32[4,288,128]{2,1,0:T(8,128)S(1)}) custom-call(f32[40]{0:T(128)} %thick_in.3, s32[1536]{0:T(1024)} %owner_ref.5, s32[4,4]{1,0:T(4,128)} %count_in.1, s32[4,4]{1,0:T(4,128)} %mask_in.1, bf16[12,40,64,128]{3,2,1,0:T(8,128)(2,1)S(1)} %copy-done, ...), custom_call_target="tpu_custom_call" | custom-call | tf_op jit(solution)/shard_map/forcing/pallas_call | solution.py:485
  10.6 1.9 %collective-permute-done.3.two_ref = f32[2,64,128]{2,1,0:T(8,128)S(1)} collective-permute-done((f32[2,64,128]{2,1,0:T(8,128)S(1)}, f32[2,64,128]{2,1,0:T(8,128)S(1)}, u32[]{:S(2)}, u32[]{:S(2)}) %collective-permute-start.3) | collective-permute-done | bytes 65568 | tf_op jit(solution)/shard_map/ppermute | solution.py:420
  12.6 1.5 %collective-permute-start.4 = (f32[2,64,128]{2,1,0:T(8,128)S(1)}, f32[2,64,128]{2,1,0:T(8,128)S(1)}, u32[]{:S(2)}, u32[]{:S(2)}) collective-permute-start(f32[2,64,128]{2,1,0:T(8,128)S(1)} %collective-permute-done.3.two_ref), channel_id=1, source_target_pairs={{0,1},{1,0},{2,3},{3,2},{4,5},{5,4},{6,7},{7,6},{8,9},{9,8},{10,11... | collective-permute-start | bytes 196616 | tf_op jit(solution)/shard_map/ppermute | solution.py:424
  14.1 0.0 collective-permute-start
  14.1 0.0 collective-permute-start.1
  14.1 1.2 %collective-permute-done.inner_ref = f32[4,24,128]{2,1,0:T(8,128)S(1)} collective-permute-done((f32[4,24,128]{2,1,0:T(8,128)S(1)}, f32[4,24,128]{2,1,0:T(8,128)S(1)}, u32[]{:S(2)}, u32[]{:S(2)}) %collective-permute-start) | collective-permute-done | bytes 49184 | tf_op jit(solution)/shard_map/ppermute | solution.py:424
  15.4 2.6 %collective-permute-done.1.outer_ref = f32[4,24,128]{2,1,0:T(8,128)S(1)} collective-permute-done((f32[4,24,128]{2,1,0:T(8,128)S(1)}, f32[4,24,128]{2,1,0:T(8,128)S(1)}, u32[]{:S(2)}, u32[]{:S(2)}) %collective-permute-start.1) | collective-permute-done | bytes 49184 | tf_op jit(solution)/shard_map/ppermute | solution.py:442
  17.9 0.0 collective-permute-done.2.mixed_ref
  18.0 0.0 collective-permute-done.4.passed_two_ref
  18.0 0.0 copy-done.1
  18.0 1.1 %assemble.1 = (f32[4,288,128]{2,1,0:T(8,128)S(1)}, f32[4,288,128]{2,1,0:T(8,128)S(1)}, f32[72,128]{1,0:T(8,128)S(1)}, f32[72,128]{1,0:T(8,128)S(1)}) custom-call(s32[1536]{0:T(1024)S(1)} %copy-done.1, f32[4,288,128]{2,1,0:T(8,128)S(1)} %get-tuple-element.19.source_in, ...), custom_call_target="tpu_custom_call", output_to_operand_aliasing={{0}: (1, {}), {1}: (2, {})} | custom-call | tf_op jit(solution)/shard_map/assemble/pallas_call | solution.py:519
  19.1 0.1 collective-permute-start.5
  19.2 2.5 %collective-permute-start.6 = (f32[72,128]{1,0:T(8,128)S(1)}, f32[72,128]{1,0:T(8,128)S(1)}, u32[]{:S(2)}, u32[]{:S(2)}) collective-permute-start(f32[72,128]{1,0:T(8,128)S(1)} %get-tuple-element.27), channel_id=1, source_target_pairs={{0,120},{8,16},{16,8},{24,32},{32,24},{40,48},{48,40},{56,64},{64,... | collective-permute-start | bytes 110600 | tf_op jit(solution)/shard_map/ppermute | solution.py:430
  21.6 0.0 copy-done.2
  21.6 5.2 %region.1.standard_in = f32[4,280,128]{2,1,0:T(8,128)S(1)} custom-call(f32[10,2]{1,0:T(8,128)S(1)} %copy-done.2, f32[4,288,128]{2,1,0:T(8,128)S(1)} %get-tuple-element.24.source_ref, f32[4,288,128]{2,1,0:T(8,128)S(1)} %get-tuple-element.25.masked_ref), custom_call_target="tpu_custom_call" | custom-call | tf_op jit(solution)/shard_map/region/pallas_call | solution.py:532
  26.8 0.0 collective-permute-done.5.inner_ref
  26.8 0.0 collective-permute-done.6.outer_ref
  26.8 2.8 %sides.1 = (f32[4,280,128]{2,1,0:T(8,128)S(1)}, f32[2,64,128]{2,1,0:T(8,128)S(1)}, f32[2,64,128]{2,1,0:T(8,128)S(1)}) custom-call(s32[1536]{0:T(1024)S(1)} %copy-done.1, f32[10,2]{1,0:T(8,128)S(1)} %copy-done.2, f32[4,280,128]{2,1,0:T(8,128)S(1)} %region.1.standard_in, ...), custom_call_target="tpu_custom_call", output_to_operand_aliasing={{0}: (2, {})} | custom-call | tf_op jit(solution)/shard_map/sides/pallas_call | solution.py:543
  29.6 1.0 %collective-permute-start.7 = (f32[2,64,128]{2,1,0:T(8,128)S(1)}, f32[2,64,128]{2,1,0:T(8,128)S(1)}, u32[]{:S(2)}, u32[]{:S(2)}) collective-permute-start(f32[2,64,128]{2,1,0:T(8,128)S(1)} %get-tuple-element.31), channel_id=1, source_target_pairs={{0,1},{1,0},{2,3},{3,2},{4,5},{5,4},{6,7},{7,6},{8,9},{9,8},{10,11... | collective-permute-start | bytes 196616 | tf_op jit(solution)/shard_map/ppermute | solution.py:424
  30.6 0.9 %collective-permute-done.7.passed_ref = f32[2,64,128]{2,1,0:T(8,128)S(1)} collective-permute-done((f32[2,64,128]{2,1,0:T(8,128)S(1)}, f32[2,64,128]{2,1,0:T(8,128)S(1)}, u32[]{:S(2)}, u32[]{:S(2)}) %collective-permute-start.7) | collective-permute-done | bytes 65568 | tf_op jit(solution)/shard_map/ppermute | solution.py:424
  31.6 2.5 %collective-permute-start.8 = (f32[2,64,128]{2,1,0:T(8,128)S(1)}, f32[2,64,128]{2,1,0:T(8,128)S(1)}, u32[]{:S(2)}, u32[]{:S(2)}) collective-permute-start(f32[2,64,128]{2,1,0:T(8,128)S(1)} %add_select_fusion), channel_id=1, source_target_pairs={{0,126},{1,127},{2,0},{3,1},{4,2},{5,3},{6,4},{7,5},{8,6},{9,7},{1... | collective-permute-start | bytes 196616 | tf_op jit(solution)/shard_map/ppermute | solution.py:420
  34.0 1.6 %write.1 = (f32[12,64,128]{2,1,0:T(8,128)}, f32[2,64,128]{2,1,0:T(8,128)S(1)}) custom-call(s32[1536]{0:T(1024)S(1)} %copy-done.1, f32[4,280,128]{2,1,0:T(8,128)S(1)} %get-tuple-element.28.standard), custom_call_target="tpu_custom_call" | custom-call | tf_op jit(solution)/shard_map/write/pallas_call | solution.py:561
  35.6 0.0 collective-permute-done.8.back_ref
  35.6 0.7 %tail.1 = f32[12,64,128]{2,1,0:T(8,128)} custom-call(f32[12,64,128]{2,1,0:T(8,128)} %get-tuple-element.29.heights_ref, f32[2,64,128]{2,1,0:T(8,128)S(1)} %get-tuple-element.30.tail_ref, f32[2,64,128]{2,1,0:T(8,128)S(1)} %collective-permute-done.7.passed_ref, f32[2,64,128]{2,1,0:T(8,128)S(1)} %collective-permute-done.8.back_ref), custom_call_target="tpu_custom_call", output_to_operand_aliasing={{}: (0, {})} | custom-call | tf_op jit(solution)/shard_map/tail/pallas_call | solution.py:569
  (1 shorter events, 0.0 us)
Async XLA Ops:
  0.0 21.6 %copy-start.2 = (f32[10,2]{1,0:T(8,128)S(1)}, f32[10,2]{1,0:T(8,128)}, u32[]{:S(2)}) copy-start(f32[10,2]{1,0:T(8,128)} %constant.20.clone.scale_ref) | copy-start | bytes 244
  0.0 8.3 %copy-start = (bf16[12,40,64,128]{3,2,1,0:T(8,128)(2,1)S(1)}, bf16[12,40,64,128]{3,2,1,0:T(8,128)(2,1)}, u32[]{:S(2)}) copy-start(bf16[12,40,64,128]{3,2,1,0:T(8,128)(2,1)} %tend_ref.3) | copy-start | bytes 23592964
  0.0 18.0 %copy-start.1 = (s32[1536]{0:T(1024)S(1)}, s32[1536]{0:T(1024)}, u32[]{:S(2)}) copy-start(s32[1536]{0:T(1024)} %owner_ref.5) | copy-start | bytes 18436
  1.6 11.0 %collective-permute-start.3 = (f32[2,64,128]{2,1,0:T(8,128)S(1)}, f32[2,64,128]{2,1,0:T(8,128)S(1)}, u32[]{:S(2)}, u32[]{:S(2)}) collective-permute-start(f32[2,64,128]{2,1,0:T(8,128)S(1)} %moved.1.moved_ref), channel_id=1, source_target_pairs={{0,2},{1,3},{2,4},{3,5},{4,6},{5,7},{6,8},{7,9},{8,10},{9,11},{10,... | collective-permute-start | bytes 196616 | tf_op jit(solution)/shard_map/ppermute | solution.py:420
  4.2 13.8 %collective-permute-start.2 = (f32[2,64,128]{2,1,0:T(8,128)S(1)}, f32[2,64,128]{2,1,0:T(8,128)S(1)}, u32[]{:S(2)}, u32[]{:S(2)}) collective-permute-start(f32[2,64,128]{2,1,0:T(8,128)S(1)} %moved.1.moved_ref), channel_id=1, source_target_pairs={{0,1},{1,4},{2,3},{3,6},{4,5},{5,0},{6,7},{7,10},{8,9},{9,12},{10,... | collective-permute-start | bytes 196616 | tf_op jit(solution)/shard_map/ppermute | solution.py:449
  12.6 5.4 %collective-permute-start.4 = (f32[2,64,128]{2,1,0:T(8,128)S(1)}, f32[2,64,128]{2,1,0:T(8,128)S(1)}, u32[]{:S(2)}, u32[]{:S(2)}) collective-permute-start(f32[2,64,128]{2,1,0:T(8,128)S(1)} %collective-permute-done.3.two_ref), channel_id=1, source_target_pairs={{0,1},{1,0},{2,3},{3,2},{4,5},{5,4},{6,7},{7,6},{8,9},{9,8},{10,11... | collective-permute-start | bytes 196616 | tf_op jit(solution)/shard_map/ppermute | solution.py:424
  14.1 1.2 %collective-permute-start = (f32[4,24,128]{2,1,0:T(8,128)S(1)}, f32[4,24,128]{2,1,0:T(8,128)S(1)}, u32[]{:S(2)}, u32[]{:S(2)}) collective-permute-start(f32[4,24,128]{2,1,0:T(8,128)S(1)} %get-tuple-element.21), channel_id=1, source_target_pairs={{0,1},{1,0},{2,3},{3,2},{4,5},{5,4},{6,7},{7,6},{8,9},{9,8},{10,11... | collective-permute-start | bytes 147464 | tf_op jit(solution)/shard_map/ppermute | solution.py:424
  14.1 3.8 %collective-permute-start.1 = (f32[4,24,128]{2,1,0:T(8,128)S(1)}, f32[4,24,128]{2,1,0:T(8,128)S(1)}, u32[]{:S(2)}, u32[]{:S(2)}) collective-permute-start(f32[4,24,128]{2,1,0:T(8,128)S(1)} %get-tuple-element.22), channel_id=1, source_target_pairs={{0,8},{1,2},{2,1},{3,4},{4,3},{5,6},{6,5},{7,15},{8,0},{9,10},{10,... | collective-permute-start | bytes 147464 | tf_op jit(solution)/shard_map/ppermute | solution.py:442
  19.1 7.7 %collective-permute-start.5 = (f32[72,128]{1,0:T(8,128)S(1)}, f32[72,128]{1,0:T(8,128)S(1)}, u32[]{:S(2)}, u32[]{:S(2)}) collective-permute-start(f32[72,128]{1,0:T(8,128)S(1)} %get-tuple-element.26), channel_id=1, source_target_pairs={{0,8},{8,0},{16,24},{24,16},{32,40},{40,32},{48,56},{56,48},{64,72... | collective-permute-start | bytes 110600 | tf_op jit(solution)/shard_map/ppermute | solution.py:424
  19.2 7.6 %collective-permute-start.6 = (f32[72,128]{1,0:T(8,128)S(1)}, f32[72,128]{1,0:T(8,128)S(1)}, u32[]{:S(2)}, u32[]{:S(2)}) collective-permute-start(f32[72,128]{1,0:T(8,128)S(1)} %get-tuple-element.27), channel_id=1, source_target_pairs={{0,120},{8,16},{16,8},{24,32},{32,24},{40,48},{48,40},{56,64},{64,... | collective-permute-start | bytes 110600 | tf_op jit(solution)/shard_map/ppermute | solution.py:430
  29.6 1.9 %collective-permute-start.7 = (f32[2,64,128]{2,1,0:T(8,128)S(1)}, f32[2,64,128]{2,1,0:T(8,128)S(1)}, u32[]{:S(2)}, u32[]{:S(2)}) collective-permute-start(f32[2,64,128]{2,1,0:T(8,128)S(1)} %get-tuple-element.31), channel_id=1, source_target_pairs={{0,1},{1,0},{2,3},{3,2},{4,5},{5,4},{6,7},{7,6},{8,9},{9,8},{10,11... | collective-permute-start | bytes 196616 | tf_op jit(solution)/shard_map/ppermute | solution.py:424
  31.6 4.1 %collective-permute-start.8 = (f32[2,64,128]{2,1,0:T(8,128)S(1)}, f32[2,64,128]{2,1,0:T(8,128)S(1)}, u32[]{:S(2)}, u32[]{:S(2)}) collective-permute-start(f32[2,64,128]{2,1,0:T(8,128)S(1)} %add_select_fusion), channel_id=1, source_target_pairs={{0,126},{1,127},{2,0},{3,1},{4,2},{5,3},{6,4},{7,5},{8,6},{9,7},{1... | collective-permute-start | bytes 196616 | tf_op jit(solution)/shard_map/ppermute | solution.py:420

commit v6 on v5

--- a/solution.py
+++ b/solution.py
@@ -75,15 +75,19 @@
     table = pltpu.make_async_copy(thick_in, thick_ref, table_sem)
     table.start()
     copies = []
+    part = LEVELS // 4
     for extra in range(MOVE):
-        copy = pltpu.make_async_copy(
-            tend_ref.at[KEPT + extra], levels.at[extra], level_sem.at[extra]
-        )
-        copy.start()
-        copies.append(copy)
+        for quarter in range(4):
+            some = pl.ds(quarter * part, part)
+            copy = pltpu.make_async_copy(
+                tend_ref.at[KEPT + extra, some], levels.at[extra, some], level_sem.at[extra, quarter]
+            )
+            copy.start()
+            copies.append(copy)
     table.wait()
     for extra in range(MOVE):
-        copies[extra].wait()
+        for copy in copies[4 * extra : 4 * extra + 4]:
+            copy.wait()
         totals = level_sum(levels, extra, thick_ref)
         for tile, value in enumerate(totals):
             moved_ref[extra, tile * 16 : tile * 16 + 16, :] = value
@@ -475,7 +479,7 @@
             pltpu.SMEM(thickness.shape, f32),
             pltpu.VMEM((MOVE, LEVELS, ROWS, LANES), jnp.bfloat16),
             pltpu.SemaphoreType.DMA,
-            pltpu.SemaphoreType.DMA((MOVE,)),
+            pltpu.SemaphoreType.DMA((MOVE, 4)),
         ],
         compiler_params=params,
         name="moved",

time: 36.4 us -> 36.5 us (level)
  no operation moved by 1% of the time
where the time goes in v6:
time: 36.5 us; the launch traced here: 36.4 us
  Pallas kernels  15.4 us (42%)
  starting transfers between devices  14.3 us (39%)
  waiting for transfers between devices  6.66 us (18%)
    pallas_call x1, Pallas kernels, on_device(): pl.pallas_call(region_kernel, in_specs=[whole(SMEM)] + [whole()] * 2, out...  5.15 us
    ppermute x2, starting transfers between devices, ring(): lax.ppermute(value, ('bx', 'by'), [(i, (i + steps) % count) for i in rang...  5.01 us
    ppermute x1, starting transfers between devices, mixed_ring(): return lax.ppermute(value, ('bx', 'by'), pairs)  4.14 us
    pallas_call x1, Pallas kernels, on_device(): pl.pallas_call(sides_kernel, in_specs=[whole(SMEM)] * 2 + [whole()] * 5,...  2.78 us
    ppermute x4, starting transfers between devices, inner_swap(): lax.ppermute(value, axis, [(i, i ^ 1) for i in range(lax.axis_size(axis))])  2.67 us
    ppermute x1, waiting for transfers between devices, outer_row_swap(): return lax.ppermute(value, ('bx', 'by'), pairs)  2.58 us
    ppermute x1, starting transfers between devices, outer_swap(): return lax.ppermute(value, axis, pairs)  2.47 us
    pallas_call x1, Pallas kernels, on_device(): pl.pallas_call(forcing_kernel, in_specs=[far] * 4 + [whole(), far, whole(...  2.32 us
  transfers between devices with their start and end apart: 9, of which 4 were waited for; matrix products, arithmetic and copies ran while one was open for 0% of the time, Pallas kernels for 25%

profile of v6, /device:TPU:1, one launch (start us, length us, event | category | flops | bytes accessed | tf_op | source)
XLA Modules:
  0.0 36.4 jit_solution(17030609185865973148)
XLA Ops:
  0.0 0.0 copy-start.2
  0.0 0.0 copy-start
  0.0 0.0 copy-start.1
  0.0 1.8 %moved.1.moved_ref = f32[2,64,128]{2,1,0:T(8,128)S(1)} custom-call(f32[40]{0:T(128)} %thick_in.3, bf16[12,40,64,128]{3,2,1,0:T(8,128)(2,1)} %tend_ref.3), custom_call_target="tpu_custom_call" | custom-call | tf_op jit(solution)/shard_map/moved/pallas_call | solution.py:473
  1.8 2.5 %collective-permute-start.3 = (f32[2,64,128]{2,1,0:T(8,128)S(1)}, f32[2,64,128]{2,1,0:T(8,128)S(1)}, u32[]{:S(2)}, u32[]{:S(2)}) collective-permute-start(f32[2,64,128]{2,1,0:T(8,128)S(1)} %moved.1.moved_ref), channel_id=1, source_target_pairs={{0,2},{1,3},{2,4},{3,5},{4,6},{5,7},{6,8},{7,9},{8,10},{9,11},{10,... | collective-permute-start | bytes 196616 | tf_op jit(solution)/shard_map/ppermute | solution.py:424
  4.3 4.1 %collective-permute-start.2 = (f32[2,64,128]{2,1,0:T(8,128)S(1)}, f32[2,64,128]{2,1,0:T(8,128)S(1)}, u32[]{:S(2)}, u32[]{:S(2)}) collective-permute-start(f32[2,64,128]{2,1,0:T(8,128)S(1)} %moved.1.moved_ref), channel_id=1, source_target_pairs={{0,1},{1,4},{2,3},{3,6},{4,5},{5,0},{6,7},{7,10},{8,9},{9,12},{10,... | collective-permute-start | bytes 196616 | tf_op jit(solution)/shard_map/ppermute | solution.py:453
  8.5 0.0 copy-done
  8.5 2.3 %forcing.1 = (f32[4,24,128]{2,1,0:T(8,128)S(1)}, f32[4,24,128]{2,1,0:T(8,128)S(1)}, f32[4,288,128]{2,1,0:T(8,128)S(1)}, f32[4,288,128]{2,1,0:T(8,128)S(1)}) custom-call(f32[40]{0:T(128)} %thick_in.3, s32[1536]{0:T(1024)} %owner_ref.5, s32[4,4]{1,0:T(4,128)} %count_in.1, s32[4,4]{1,0:T(4,128)} %mask_in.1, bf16[12,40,64,128]{3,2,1,0:T(8,128)(2,1)S(1)} %copy-done, ...), custom_call_target="tpu_custom_call" | custom-call | tf_op jit(solution)/shard_map/forcing/pallas_call | solution.py:489
  10.8 1.9 %collective-permute-done.3.two_ref = f32[2,64,128]{2,1,0:T(8,128)S(1)} collective-permute-done((f32[2,64,128]{2,1,0:T(8,128)S(1)}, f32[2,64,128]{2,1,0:T(8,128)S(1)}, u32[]{:S(2)}, u32[]{:S(2)}) %collective-permute-start.3) | collective-permute-done | bytes 65568 | tf_op jit(solution)/shard_map/ppermute | solution.py:424
  12.7 1.5 %collective-permute-start.4 = (f32[2,64,128]{2,1,0:T(8,128)S(1)}, f32[2,64,128]{2,1,0:T(8,128)S(1)}, u32[]{:S(2)}, u32[]{:S(2)}) collective-permute-start(f32[2,64,128]{2,1,0:T(8,128)S(1)} %collective-permute-done.3.two_ref), channel_id=1, source_target_pairs={{0,1},{1,0},{2,3},{3,2},{4,5},{5,4},{6,7},{7,6},{8,9},{9,8},{10,11... | collective-permute-start | bytes 196616 | tf_op jit(solution)/shard_map/ppermute | solution.py:428
  14.3 0.0 collective-permute-start
  14.3 0.0 collective-permute-start.1
  14.3 1.2 %collective-permute-done.inner_ref = f32[4,24,128]{2,1,0:T(8,128)S(1)} collective-permute-done((f32[4,24,128]{2,1,0:T(8,128)S(1)}, f32[4,24,128]{2,1,0:T(8,128)S(1)}, u32[]{:S(2)}, u32[]{:S(2)}) %collective-permute-start) | collective-permute-done | bytes 49184 | tf_op jit(solution)/shard_map/ppermute | solution.py:428
  15.5 2.6 %collective-permute-done.1.outer_ref = f32[4,24,128]{2,1,0:T(8,128)S(1)} collective-permute-done((f32[4,24,128]{2,1,0:T(8,128)S(1)}, f32[4,24,128]{2,1,0:T(8,128)S(1)}, u32[]{:S(2)}, u32[]{:S(2)}) %collective-permute-start.1) | collective-permute-done | bytes 49184 | tf_op jit(solution)/shard_map/ppermute | solution.py:446
  18.1 0.0 collective-permute-done.2.mixed_ref
  18.1 0.0 collective-permute-done.4.passed_two_ref
  18.1 0.0 copy-done.1
  18.1 1.1 %assemble.1 = (f32[4,288,128]{2,1,0:T(8,128)S(1)}, f32[4,288,128]{2,1,0:T(8,128)S(1)}, f32[72,128]{1,0:T(8,128)S(1)}, f32[72,128]{1,0:T(8,128)S(1)}) custom-call(s32[1536]{0:T(1024)S(1)} %copy-done.1, f32[4,288,128]{2,1,0:T(8,128)S(1)} %get-tuple-element.19.source_in, ...), custom_call_target="tpu_custom_call", output_to_operand_aliasing={{0}: (1, {}), {1}: (2, {})} | custom-call | tf_op jit(solution)/shard_map/assemble/pallas_call | solution.py:523
  19.2 0.1 collective-permute-start.5
  19.3 2.5 %collective-permute-start.6 = (f32[72,128]{1,0:T(8,128)S(1)}, f32[72,128]{1,0:T(8,128)S(1)}, u32[]{:S(2)}, u32[]{:S(2)}) collective-permute-start(f32[72,128]{1,0:T(8,128)S(1)} %get-tuple-element.27), channel_id=1, source_target_pairs={{0,120},{8,16},{16,8},{24,32},{32,24},{40,48},{48,40},{56,64},{64,... | collective-permute-start | bytes 110600 | tf_op jit(solution)/shard_map/ppermute | solution.py:434
  21.8 0.0 copy-done.2
  21.8 5.2 %region.1.standard_in = f32[4,280,128]{2,1,0:T(8,128)S(1)} custom-call(f32[10,2]{1,0:T(8,128)S(1)} %copy-done.2, f32[4,288,128]{2,1,0:T(8,128)S(1)} %get-tuple-element.24.source_ref, f32[4,288,128]{2,1,0:T(8,128)S(1)} %get-tuple-element.25.masked_ref), custom_call_target="tpu_custom_call" | custom-call | tf_op jit(solution)/shard_map/region/pallas_call | solution.py:536
  26.9 0.0 collective-permute-done.5.inner_ref
  26.9 0.0 collective-permute-done.6.outer_ref
  27.0 2.8 %sides.1 = (f32[4,280,128]{2,1,0:T(8,128)S(1)}, f32[2,64,128]{2,1,0:T(8,128)S(1)}, f32[2,64,128]{2,1,0:T(8,128)S(1)}) custom-call(s32[1536]{0:T(1024)S(1)} %copy-done.1, f32[10,2]{1,0:T(8,128)S(1)} %copy-done.2, f32[4,280,128]{2,1,0:T(8,128)S(1)} %region.1.standard_in, ...), custom_call_target="tpu_custom_call", output_to_operand_aliasing={{0}: (2, {})} | custom-call | tf_op jit(solution)/shard_map/sides/pallas_call | solution.py:547
  29.7 1.0 %collective-permute-start.7 = (f32[2,64,128]{2,1,0:T(8,128)S(1)}, f32[2,64,128]{2,1,0:T(8,128)S(1)}, u32[]{:S(2)}, u32[]{:S(2)}) collective-permute-start(f32[2,64,128]{2,1,0:T(8,128)S(1)} %get-tuple-element.31), channel_id=1, source_target_pairs={{0,1},{1,0},{2,3},{3,2},{4,5},{5,4},{6,7},{7,6},{8,9},{9,8},{10,11... | collective-permute-start | bytes 196616 | tf_op jit(solution)/shard_map/ppermute | solution.py:428
  30.8 0.9 %collective-permute-done.7.passed_ref = f32[2,64,128]{2,1,0:T(8,128)S(1)} collective-permute-done((f32[2,64,128]{2,1,0:T(8,128)S(1)}, f32[2,64,128]{2,1,0:T(8,128)S(1)}, u32[]{:S(2)}, u32[]{:S(2)}) %collective-permute-start.7) | collective-permute-done | bytes 65568 | tf_op jit(solution)/shard_map/ppermute | solution.py:428
  31.7 2.5 %collective-permute-start.8 = (f32[2,64,128]{2,1,0:T(8,128)S(1)}, f32[2,64,128]{2,1,0:T(8,128)S(1)}, u32[]{:S(2)}, u32[]{:S(2)}) collective-permute-start(f32[2,64,128]{2,1,0:T(8,128)S(1)} %add_select_fusion), channel_id=1, source_target_pairs={{0,126},{1,127},{2,0},{3,1},{4,2},{5,3},{6,4},{7,5},{8,6},{9,7},{1... | collective-permute-start | bytes 196616 | tf_op jit(solution)/shard_map/ppermute | solution.py:424
  34.2 1.6 %write.1 = (f32[12,64,128]{2,1,0:T(8,128)}, f32[2,64,128]{2,1,0:T(8,128)S(1)}) custom-call(s32[1536]{0:T(1024)S(1)} %copy-done.1, f32[4,280,128]{2,1,0:T(8,128)S(1)} %get-tuple-element.28.standard), custom_call_target="tpu_custom_call" | custom-call | tf_op jit(solution)/shard_map/write/pallas_call | solution.py:565
  35.8 0.0 collective-permute-done.8.back_ref
  35.8 0.7 %tail.1 = f32[12,64,128]{2,1,0:T(8,128)} custom-call(f32[12,64,128]{2,1,0:T(8,128)} %get-tuple-element.29.heights_ref, f32[2,64,128]{2,1,0:T(8,128)S(1)} %get-tuple-element.30.tail_ref, f32[2,64,128]{2,1,0:T(8,128)S(1)} %collective-permute-done.7.passed_ref, f32[2,64,128]{2,1,0:T(8,128)S(1)} %collective-permute-done.8.back_ref), custom_call_target="tpu_custom_call", output_to_operand_aliasing={{}: (0, {})} | custom-call | tf_op jit(solution)/shard_map/tail/pallas_call | solution.py:573
  (1 shorter events, 0.0 us)
Async XLA Ops:
  0.0 21.8 %copy-start.2 = (f32[10,2]{1,0:T(8,128)S(1)}, f32[10,2]{1,0:T(8,128)}, u32[]{:S(2)}) copy-start(f32[10,2]{1,0:T(8,128)} %constant.20.clone.scale_ref) | copy-start | bytes 244
  0.0 8.5 %copy-start = (bf16[12,40,64,128]{3,2,1,0:T(8,128)(2,1)S(1)}, bf16[12,40,64,128]{3,2,1,0:T(8,128)(2,1)}, u32[]{:S(2)}) copy-start(bf16[12,40,64,128]{3,2,1,0:T(8,128)(2,1)} %tend_ref.3) | copy-start | bytes 23592964
  0.0 18.1 %copy-start.1 = (s32[1536]{0:T(1024)S(1)}, s32[1536]{0:T(1024)}, u32[]{:S(2)}) copy-start(s32[1536]{0:T(1024)} %owner_ref.5) | copy-start | bytes 18436
  1.8 11.0 %collective-permute-start.3 = (f32[2,64,128]{2,1,0:T(8,128)S(1)}, f32[2,64,128]{2,1,0:T(8,128)S(1)}, u32[]{:S(2)}, u32[]{:S(2)}) collective-permute-start(f32[2,64,128]{2,1,0:T(8,128)S(1)} %moved.1.moved_ref), channel_id=1, source_target_pairs={{0,2},{1,3},{2,4},{3,5},{4,6},{5,7},{6,8},{7,9},{8,10},{9,11},{10,... | collective-permute-start | bytes 196616 | tf_op jit(solution)/shard_map/ppermute | solution.py:424
  4.3 13.8 %collective-permute-start.2 = (f32[2,64,128]{2,1,0:T(8,128)S(1)}, f32[2,64,128]{2,1,0:T(8,128)S(1)}, u32[]{:S(2)}, u32[]{:S(2)}) collective-permute-start(f32[2,64,128]{2,1,0:T(8,128)S(1)} %moved.1.moved_ref), channel_id=1, source_target_pairs={{0,1},{1,4},{2,3},{3,6},{4,5},{5,0},{6,7},{7,10},{8,9},{9,12},{10,... | collective-permute-start | bytes 196616 | tf_op jit(solution)/shard_map/ppermute | solution.py:453
  12.7 5.4 %collective-permute-start.4 = (f32[2,64,128]{2,1,0:T(8,128)S(1)}, f32[2,64,128]{2,1,0:T(8,128)S(1)}, u32[]{:S(2)}, u32[]{:S(2)}) collective-permute-start(f32[2,64,128]{2,1,0:T(8,128)S(1)} %collective-permute-done.3.two_ref), channel_id=1, source_target_pairs={{0,1},{1,0},{2,3},{3,2},{4,5},{5,4},{6,7},{7,6},{8,9},{9,8},{10,11... | collective-permute-start | bytes 196616 | tf_op jit(solution)/shard_map/ppermute | solution.py:428
  14.3 1.2 %collective-permute-start = (f32[4,24,128]{2,1,0:T(8,128)S(1)}, f32[4,24,128]{2,1,0:T(8,128)S(1)}, u32[]{:S(2)}, u32[]{:S(2)}) collective-permute-start(f32[4,24,128]{2,1,0:T(8,128)S(1)} %get-tuple-element.21), channel_id=1, source_target_pairs={{0,1},{1,0},{2,3},{3,2},{4,5},{5,4},{6,7},{7,6},{8,9},{9,8},{10,11... | collective-permute-start | bytes 147464 | tf_op jit(solution)/shard_map/ppermute | solution.py:428
  14.3 3.8 %collective-permute-start.1 = (f32[4,24,128]{2,1,0:T(8,128)S(1)}, f32[4,24,128]{2,1,0:T(8,128)S(1)}, u32[]{:S(2)}, u32[]{:S(2)}) collective-permute-start(f32[4,24,128]{2,1,0:T(8,128)S(1)} %get-tuple-element.22), channel_id=1, source_target_pairs={{0,8},{1,2},{2,1},{3,4},{4,3},{5,6},{6,5},{7,15},{8,0},{9,10},{10,... | collective-permute-start | bytes 147464 | tf_op jit(solution)/shard_map/ppermute | solution.py:446
  19.2 7.7 %collective-permute-start.5 = (f32[72,128]{1,0:T(8,128)S(1)}, f32[72,128]{1,0:T(8,128)S(1)}, u32[]{:S(2)}, u32[]{:S(2)}) collective-permute-start(f32[72,128]{1,0:T(8,128)S(1)} %get-tuple-element.26), channel_id=1, source_target_pairs={{0,8},{8,0},{16,24},{24,16},{32,40},{40,32},{48,56},{56,48},{64,72... | collective-permute-start | bytes 110600 | tf_op jit(solution)/shard_map/ppermute | solution.py:428
  19.3 7.6 %collective-permute-start.6 = (f32[72,128]{1,0:T(8,128)S(1)}, f32[72,128]{1,0:T(8,128)S(1)}, u32[]{:S(2)}, u32[]{:S(2)}) collective-permute-start(f32[72,128]{1,0:T(8,128)S(1)} %get-tuple-element.27), channel_id=1, source_target_pairs={{0,120},{8,16},{16,8},{24,32},{32,24},{40,48},{48,40},{56,64},{64,... | collective-permute-start | bytes 110600 | tf_op jit(solution)/shard_map/ppermute | solution.py:434
  29.7 1.9 %collective-permute-start.7 = (f32[2,64,128]{2,1,0:T(8,128)S(1)}, f32[2,64,128]{2,1,0:T(8,128)S(1)}, u32[]{:S(2)}, u32[]{:S(2)}) collective-permute-start(f32[2,64,128]{2,1,0:T(8,128)S(1)} %get-tuple-element.31), channel_id=1, source_target_pairs={{0,1},{1,0},{2,3},{3,2},{4,5},{5,4},{6,7},{7,6},{8,9},{9,8},{10,11... | collective-permute-start | bytes 196616 | tf_op jit(solution)/shard_map/ppermute | solution.py:428
  31.7 4.1 %collective-permute-start.8 = (f32[2,64,128]{2,1,0:T(8,128)S(1)}, f32[2,64,128]{2,1,0:T(8,128)S(1)}, u32[]{:S(2)}, u32[]{:S(2)}) collective-permute-start(f32[2,64,128]{2,1,0:T(8,128)S(1)} %add_select_fusion), channel_id=1, source_target_pairs={{0,126},{1,127},{2,0},{3,1},{4,2},{5,3},{6,4},{7,5},{8,6},{9,7},{1... | collective-permute-start | bytes 196616 | tf_op jit(solution)/shard_map/ppermute | solution.py:424
